TPU v7x, 32 devices: a whole 2x2x4 slice. The times are simulated.
32 devices in a mesh: dp: 8 (over y, x, core), tensor: 4 (over z).
Axes of the slice: x: 2, y: 2, z: 4, core: 2. Of those that a mesh axis runs over, the one named last changes fastest.
Arguments:
- tokens: bfloat16 [16384, 2048], P(('dp', 'tensor')), may hold values from -6 to 6
- segments: int32 [8, 2048], P('dp'), may hold values from 0 to 7, never falling along the last dimension, each value on 1 to 1024 neighbouring positions
- ln_gain: float32 [2048], replicated, may hold values from 0.5 to 1.5
- ln_shift: float32 [2048], replicated, may hold values from -1.5 to 1.5
- qkv_weight: bfloat16 [2048, 3, 2048], P('dp', None, 'tensor'), may hold values from -0.125 to 0.125
- qkv_bias: float32 [3, 2048], P(None, 'tensor'), may hold values from -3 to 3
- out_weight: bfloat16 [2048, 2048], P('tensor', 'dp'), may hold values from -1 to 1
- out_bias: float32 [2048], replicated, may hold values from -3 to 3
- fc1_weight: bfloat16 [2048, 8192], P('dp', 'tensor'), may hold values from -0.125 to 0.125
- fc1_bias: float32 [8192], P('tensor'), may hold values from -3 to 3
- fc2_weight: bfloat16 [8192, 2048], P('tensor', 'dp'), may hold values from -0.0625 to 0.0625
- fc2_bias: float32 [2048], replicated, may hold values from -3 to 3
- cotangent: bfloat16 [16384, 2048], P(('dp', 'tensor')), may hold values from -6 to 6
Outputs:
- mixed: bfloat16 [16384, 2048], P(('dp', 'tensor'))
- input_grad: bfloat16 [16384, 2048], P(('dp', 'tensor'))
- qkv_weight_grad: float32 [2048, 3, 2048], P('dp', None, 'tensor')
- qkv_bias_grad: float32 [3, 2048], P(None, 'tensor')
- out_weight_grad: float32 [2048, 2048], P('tensor', 'dp')
- out_bias_grad: float32 [2048], replicated
- fc1_weight_grad: float32 [2048, 8192], P('dp', 'tensor')
- fc1_bias_grad: float32 [8192], P('tensor')
- fc2_weight_grad: float32 [8192, 2048], P('tensor', 'dp')
- fc2_bias_grad: float32 [2048], replicated
- gain_grad: float32 [2048], replicated
- shift_grad: float32 [2048], replicated
Inputs may be any that keep to these rules, and one draw needn't show every extreme that they name: `segments`: each row holds one data group's 2048 tokens; along a row the sequence numbers never fall, each sequence covers 1 to 1024 consecutive tokens, and some sequence covers exactly 1024.
All inputs are finite; a program needn't handle non-finite values.
Results may differ from a plain program's by a relative error of at most 0.013.
Values may be sent and summed in bfloat16 or wider, within the bound.
A program may use at most 320 MiB of HBM per device.

v0:
```python
import jax
import jax.numpy as jnp
from jax import lax
from jax.sharding import PartitionSpec as P

D = 2048
H = 32
HD = 64
ROT = 32


EPS = 1e-05
ROPE_BASE = 10000.0
NEGATIVE = -1e30


def contract_rows(left_op, right_op):
    return lax.dot_general(
        left_op, right_op, (((0,), (0,)), ((), ())), preferred_element_type=jnp.float32
    )


def contract_cols(left_op, right_op):
    return lax.dot_general(
        left_op, right_op, (((1,), (1,)), ((), ())), preferred_element_type=jnp.float32
    )


def gelu_tanh(values_in):
    return jax.nn.gelu(values_in, approximate=True)


def seq_positions(segment_row):
    row_count = segment_row.shape[0]
    row_index = jnp.arange(row_count, dtype=jnp.int32)
    seq_begins = jnp.concatenate([jnp.ones((1,), dtype=bool), segment_row[1:] != segment_row[:-1]])
    starts = lax.cummax(jnp.where(seq_begins, row_index, jnp.zeros_like(row_index)), axis=0)
    return row_index - starts


def rotary_tables(positions):
    half_rot = ROT // 2
    frequency = ROPE_BASE ** (-(jnp.arange(half_rot, dtype=jnp.float32) * 2.0) / ROT)
    angles = positions.astype(jnp.float32)[:, None] * frequency[None, :]
    return (jnp.cos(angles)[:, None, :], jnp.sin(angles)[:, None, :])


def rotate(heads_in, cosine_table, sine_table):
    half_rot = ROT // 2
    first_half = heads_in[..., :half_rot]
    second_half = heads_in[..., half_rot:ROT]
    return jnp.concatenate(
        [
            first_half * cosine_table - second_half * sine_table,
            second_half * cosine_table + first_half * sine_table,
            heads_in[..., ROT:],
        ],
        axis=-1,
    )


def allowed_block(segment_row, first_row, block_rows):
    key_count = segment_row.shape[0]
    query_index = first_row + jnp.arange(block_rows, dtype=jnp.int32)
    key_index = jnp.arange(key_count, dtype=jnp.int32)
    query_seg = lax.dynamic_slice_in_dim(segment_row, first_row, block_rows, 0)
    return (query_seg[:, None] == segment_row[None, :]) & (
        key_index[None, :] <= query_index[:, None]
    )


def attend(queries, key_rows, value_rows, segment_row, block_rows):
    group_rows = queries.shape[0]
    factor = HD ** (-0.5)

    def one_block(block_index):
        first_row = block_index * block_rows
        query_block = lax.dynamic_slice_in_dim(queries, first_row, block_rows, 0)
        raw_scores = (
            jnp.einsum("qhd,khd->hqk", query_block, key_rows, preferred_element_type=jnp.float32)
            * factor
        )
        allowed = allowed_block(segment_row, first_row, block_rows)
        scores = jnp.where(allowed[None], raw_scores, NEGATIVE)
        row_max = jnp.max(scores, axis=-1, keepdims=True)
        exponent = jnp.exp(scores - row_max)
        row_total = jnp.sum(exponent, axis=-1, keepdims=True)
        attn_probs = (exponent / row_total).astype(jnp.bfloat16)
        block_out = jnp.einsum(
            "hqk,khd->qhd", attn_probs, value_rows, preferred_element_type=jnp.float32
        )
        return (block_out, (row_max + jnp.log(row_total))[..., 0])

    block_out, log_norm = lax.map(one_block, jnp.arange(group_rows // block_rows, dtype=jnp.int32))
    return (block_out.reshape(group_rows, -1), log_norm)


def attend_back(queries, key_rows, value_rows, grad_mix, log_norm, segment_row, block_rows):
    group_rows = queries.shape[0]
    factor = HD ** (-0.5)

    def one_block(running, block_item):
        grad_keys, grad_values = running
        block_index, block_norm = block_item
        first_row = block_index * block_rows
        query_block = lax.dynamic_slice_in_dim(queries, first_row, block_rows, 0)
        grad_block = lax.dynamic_slice_in_dim(grad_mix, first_row, block_rows, 0)
        raw_scores = (
            jnp.einsum("qhd,khd->hqk", query_block, key_rows, preferred_element_type=jnp.float32)
            * factor
        )
        allowed = allowed_block(segment_row, first_row, block_rows)
        attn_probs = jnp.where(allowed[None], jnp.exp(raw_scores - block_norm[..., None]), 0.0)
        grad_values = grad_values + jnp.einsum(
            "hqk,qhd->khd",
            attn_probs.astype(jnp.bfloat16),
            grad_block,
            preferred_element_type=jnp.float32,
        )
        grad_probs = jnp.einsum(
            "qhd,khd->hqk", grad_block, value_rows, preferred_element_type=jnp.float32
        )
        inner = jnp.sum(attn_probs * grad_probs, axis=-1, keepdims=True)
        grad_scores = (attn_probs * (grad_probs - inner)).astype(jnp.bfloat16)
        grad_queries = (
            jnp.einsum("hqk,khd->qhd", grad_scores, key_rows, preferred_element_type=jnp.float32)
            * factor
        )
        grad_keys = (
            grad_keys
            + jnp.einsum(
                "hqk,qhd->khd", grad_scores, query_block, preferred_element_type=jnp.float32
            )
            * factor
        )
        return ((grad_keys, grad_values), grad_queries)

    zero_rows = jnp.zeros(queries.shape, jnp.float32)
    block_ids = jnp.arange(group_rows // block_rows, dtype=jnp.int32)
    (grad_keys, grad_values), grad_queries = lax.scan(
        one_block, (zero_rows, zero_rows), (block_ids, log_norm)
    )
    return (grad_queries.reshape(queries.shape), grad_keys, grad_values)


def local(
    tokens,
    segments,
    ln_gain,
    ln_shift,
    qkv_weight,
    qkv_bias,
    out_weight,
    out_bias,
    fc1_weight,
    fc1_bias,
    fc2_weight,
    fc2_bias,
    cotangent,
):
    heads_here = H // lax.axis_size("tensor")
    segment_row = segments[0]
    group_rows = segment_row.shape[0]
    block_rows = min(512, group_rows)
    x_local = tokens.astype(jnp.float32)
    row_mean = jnp.mean(x_local, axis=-1, keepdims=True)
    centred = x_local - row_mean
    inv_std = lax.rsqrt(jnp.mean(centred * centred, axis=-1, keepdims=True) + EPS)
    normalized = centred * inv_std
    normed = lax.all_gather(
        (normalized * ln_gain + ln_shift).astype(jnp.bfloat16), "tensor", axis=0, tiled=True
    )
    w_qkv, w_out, w_up, w_down = (
        lax.all_gather(qkv_weight, "dp", axis=0, tiled=True),
        lax.all_gather(out_weight, "dp", axis=1, tiled=True),
        lax.all_gather(fc1_weight, "dp", axis=0, tiled=True),
        lax.all_gather(fc2_weight, "dp", axis=1, tiled=True),
    )
    local_width = w_qkv.shape[2]
    flat_qkv = w_qkv.reshape(D, 3 * local_width)
    qkv_raw = jnp.dot(normed, flat_qkv, preferred_element_type=jnp.float32).reshape(
        group_rows, 3, local_width
    )
    qkv_raw = qkv_raw + qkv_bias[None]
    positions = seq_positions(segment_row)
    cosine_table, sine_table = rotary_tables(positions)
    queries = rotate(
        qkv_raw[:, 0].reshape(group_rows, heads_here, HD), cosine_table, sine_table
    ).astype(jnp.bfloat16)
    key_rows = rotate(
        qkv_raw[:, 1].reshape(group_rows, heads_here, HD), cosine_table, sine_table
    ).astype(jnp.bfloat16)
    value_rows = qkv_raw[:, 2].reshape(group_rows, heads_here, HD).astype(jnp.bfloat16)
    attended_f32, log_norm = attend(queries, key_rows, value_rows, segment_row, block_rows)
    attended = attended_f32.astype(jnp.bfloat16)
    hidden = jnp.dot(normed, w_up, preferred_element_type=jnp.float32) + fc1_bias
    activated = gelu_tanh(hidden).astype(jnp.bfloat16)
    block_sum = lax.psum_scatter(
        (
            jnp.dot(attended, w_out, preferred_element_type=jnp.float32)
            + jnp.dot(activated, w_down, preferred_element_type=jnp.float32)
        ).astype(jnp.bfloat16),
        "tensor",
        scatter_dimension=0,
        tiled=True,
    ).astype(jnp.float32)
    mixed = (x_local + block_sum + out_bias + fc2_bias).astype(jnp.bfloat16)
    w_qkv, w_out, w_up, w_down = (
        lax.all_gather(qkv_weight, "dp", axis=0, tiled=True),
        lax.all_gather(out_weight, "dp", axis=1, tiled=True),
        lax.all_gather(fc1_weight, "dp", axis=0, tiled=True),
        lax.all_gather(fc2_weight, "dp", axis=1, tiled=True),
    )
    flat_qkv = w_qkv.reshape(D, 3 * local_width)
    grad_full = lax.all_gather(cotangent, "tensor", axis=0, tiled=True)
    grad_act = contract_cols(grad_full, w_down)
    gelu_value, gelu_pull = jax.vjp(gelu_tanh, hidden)
    grad_hidden = gelu_pull(grad_act)[0].astype(jnp.bfloat16)
    grad_up = contract_rows(normed, grad_hidden)
    grad_up_bias = jnp.sum(grad_hidden.astype(jnp.float32), axis=0)
    grad_mix = (
        contract_cols(grad_full, w_out).astype(jnp.bfloat16).reshape(group_rows, heads_here, HD)
    )
    grad_queries, grad_keys, grad_values = attend_back(
        queries, key_rows, value_rows, grad_mix, log_norm, segment_row, block_rows
    )
    grad_qkv = jnp.stack(
        [
            rotate(grad_queries, cosine_table, -sine_table).reshape(group_rows, local_width),
            rotate(grad_keys, cosine_table, -sine_table).reshape(group_rows, local_width),
            grad_values.reshape(group_rows, local_width),
        ],
        axis=1,
    ).astype(jnp.bfloat16)
    grad_qkv_bias = jnp.sum(grad_qkv.astype(jnp.float32), axis=0)
    flat_grad = grad_qkv.reshape(group_rows, 3 * local_width)
    grad_qkv_w = contract_rows(normed, flat_grad).reshape(D, 3, local_width)
    grad_down = contract_rows(activated, grad_full)
    grad_out = contract_rows(attended, grad_full)
    summed_qkv, summed_out, summed_up, summed_down = (
        lax.psum_scatter(
            grad_qkv_w.astype(jnp.bfloat16), "dp", scatter_dimension=0, tiled=True
        ).astype(jnp.float32),
        lax.psum_scatter(
            grad_out.astype(jnp.bfloat16), "dp", scatter_dimension=1, tiled=True
        ).astype(jnp.float32),
        lax.psum_scatter(
            grad_up.astype(jnp.bfloat16), "dp", scatter_dimension=0, tiled=True
        ).astype(jnp.float32),
        lax.psum_scatter(
            grad_down.astype(jnp.bfloat16), "dp", scatter_dimension=1, tiled=True
        ).astype(jnp.float32),
    )
    grad_normed = lax.psum_scatter(
        (contract_cols(flat_grad, flat_qkv) + contract_cols(grad_hidden, w_up)).astype(
            jnp.bfloat16
        ),
        "tensor",
        scatter_dimension=0,
        tiled=True,
    ).astype(jnp.float32)
    grad_scaled = grad_normed * ln_gain
    input_grad = inv_std * (
        grad_scaled
        - jnp.mean(grad_scaled, axis=-1, keepdims=True)
        - normalized * jnp.mean(grad_scaled * normalized, axis=-1, keepdims=True)
    )
    input_grad = (input_grad + cotangent.astype(jnp.float32)).astype(jnp.bfloat16)
    gain_sum, shift_sum, output_sum = lax.psum(
        (
            jnp.sum(grad_normed * normalized, axis=0),
            jnp.sum(grad_normed, axis=0),
            jnp.sum(cotangent.astype(jnp.float32), axis=0),
        ),
        ("dp", "tensor"),
    )
    qkv_bias_sum, up_bias_sum = lax.psum((grad_qkv_bias, grad_up_bias), "dp")
    return (
        mixed,
        input_grad,
        summed_qkv,
        qkv_bias_sum,
        summed_out,
        output_sum,
        summed_up,
        up_bias_sum,
        summed_down,
        output_sum,
        gain_sum,
        shift_sum,
    )


def solution(mesh):
    in_specs = (
        P(("dp", "tensor"), None),
        P("dp", None),
        P(),
        P(),
        P("dp", None, "tensor"),
        P(None, "tensor"),
        P("tensor", "dp"),
        P(),
        P("dp", "tensor"),
        P("tensor"),
        P("tensor", "dp"),
        P(),
        P(("dp", "tensor"), None),
    )
    out_specs = (
        P(("dp", "tensor"), None),
        P(("dp", "tensor"), None),
        P("dp", None, "tensor"),
        P(None, "tensor"),
        P("tensor", "dp"),
        P(),
        P("dp", "tensor"),
        P("tensor"),
        P("tensor", "dp"),
        P(),
        P(),
        P(),
    )
    return jax.shard_map(local, mesh=mesh, in_specs=in_specs, out_specs=out_specs, check_vma=False)
```

profile of v0, /device:TPU:0, one launch (start us, length us, event | category | flops | bytes accessed | tf_op | source)
XLA Modules:
  0.0 1624.3 jit_solution(4911673076161956696)
XLA Ops:
  19.7 38.5 %all-gather.9.cloned.1.call-done = bf16[2048,3,512]{2,0,1:T(8,128)(2,1)} async-done(((bf16[256,3,512]{2,0,1:T(8,128)(2,1)}), bf16[2048,3,512]{2,0,1:T(8,128)(2,1)}) %all-gather.9.cloned.1.call-update) | async-done | bytes 6291472 | tf_op jit(solution)/shard_map/all_gather | solution.py:174
  67.0 143.0 %all-gather.7.cloned.1.call-done = bf16[2048,2048]{1,0:T(8,128)(2,1)} async-done(((bf16[512,2048]{1,0:T(8,128)(2,1)}), bf16[2048,2048]{1,0:T(8,128)(2,1)}) %all-gather.7.cloned.1.call-update) | async-done | bytes 8388624 | tf_op jit(solution)/shard_map/all_gather | solution.py:170
  210.0 17.8 %broadcast_add_fusion = f32[2048,3,512]{0,2,1:T(8,128)S(1)} fusion(f32[3,512]{1,0:T(4,128)S(1)} %copy-done.20, bf16[2048,3,512]{0,2,1:T(8,128)(2,1)} %copy.29, bf16[2048,2048]{1,0:T(8,128)(2,1)} %all-gather.7.cloned.1.call-done), kind=kOutput, calls=%fused_computation.66 | convolution fusion | flops 12888047616 | bytes 27269120 | tf_op jit(solution)/shard_map/dot_general | solution.py:181
  233.0 196.4 %while.27 = (s32[]{:T(128)}, bf16[4,512,8,64]{1,3,2,0:T(8,128)(2,1)}, f32[4,8,512]{2,1,0:T(8,128)S(1)}, s32[4]{0:T(128)S(1)}, s32[2048]{0:T(1024)S(1)}, /*index=...) while((s32[]{:T(128)}, ...), condition=%wide.region_7.8_spmd, body=%wide.region_4.7_spmd.sunk | while | flops 2251289088 | bytes 110774976 | solution.py:94
  439.4 528.9 %while.28 = (s32[]{:T(128)}, f32[2048,8,64]{0,2,1:T(8,128)}, f32[2048,8,64]{0,2,1:T(8,128)}, f32[4,512,8,64]{1,0,3,2:T(4,128)}, s32[4]{0:T(128)S(1)}, /*index=5*...) while((s32[]{:T(128)}, f32[2048,8,64]{0,2,1:T(8,128)}, ...), condition=%wide.region_11.12_spmd.clone, body=%wide.region_9.11_spmd.clone.sunk | while | flops 5452853760 | bytes 284264672 | solution.py:140
  442.1 18.6 %fusion.132 = f32[8,512,2048]{2,1,0:T(8,128)} fusion(bf16[2048,8,64]{0,2,1:T(8,128)(2,1)} %get-tuple-element.467, bf16[2048,8,64]{0,2,1:T(8,128)(2,1)} %get-tuple-element.466, s32[]{:T(128)S(6)} %select_n.49), kind=kOutput, calls=%fused_computation.29.clone.1 | convolution fusion | flops 1073741824 | bytes 36175876 | tf_op jit(solution)/shard_map/while/body/eval_jaxpr/qhd,khd->hqk/dot_general | solution.py:120
  460.7 25.0 %multiply_reduce_fusion.2 = (f32[8,512]{1,0:T(8,128)S(1)}, f32[8,512,2048]{2,1,0:T(8,128)}) fusion(f32[8,512,2048]{2,1,0:T(8,128)} %fusion.132, f32[8,512]{1,0:T(8,128)S(1)} %dynamic-slice_bitcast_fusion.2, bf16[2048,8,64]{0,2,1:T(8,128)(2,1)S(1)} %get-tuple-element.464, bf16[2048,8,64]{0,2,1:T(8,128)(2,1)} %get-tuple-element.461, ...), kind=kOutput, calls=%fused_computation.18.clone.1 | convolution fusion | flops 1115680768 | bytes 70811648 | tf_op jit(solution)/shard_map/while/body/eval_jaxpr/qhd,khd->hqk/dot_general | solution.py:109
  485.6 28.1 %multiply_convert_fusion.5 = bf16[8,512,2048]{2,1,0:T(8,128)(2,1)} fusion(f32[8,512,2048]{2,1,0:T(8,128)} %get-tuple-element.383, f32[8,512,2048]{2,1,0:T(8,128)} %fusion.132, f32[8,512]{1,0:T(8,128)S(1)} %get-tuple-element.384), kind=kLoop, calls=%fused_computation.17.clone.1 | loop fusion | flops 25165824 | bytes 83902464 | tf_op jit(solution)/shard_map/while/body/eval_jaxpr/convert_element_type | solution.py:124
  523.5 21.0 %dynamic_update_slice.19 = f32[4,512,8,64]{1,0,3,2:T(4,128)} dynamic-update-slice(f32[4,512,8,64]{1,0,3,2:T(4,128)} %get-tuple-element.443, f32[1,512,8,64]{1,0,3,2:T(1,128)S(1)} %copy.52, s32[]{:T(128)} %get-tuple-element.440, s32[]{:T(128)} %constant.48.clone.1..sunk.1, s32[]{:T(128)} %constant.48.clone.1..sunk.1, s32[]{:T(128)} %constant.48.clone.1..sunk.1) | dynamic-update-slice | bytes 2097156 | tf_op jit(solution)/shard_map/while/body/jit(dynamic_update_index_in_dim)/dynamic_update_slice | solution.py:94
  573.9 17.4 %fusion.132 = f32[8,512,2048]{2,1,0:T(8,128)} fusion(bf16[2048,8,64]{0,2,1:T(8,128)(2,1)} %get-tuple-element.467, bf16[2048,8,64]{0,2,1:T(8,128)(2,1)} %get-tuple-element.466, s32[]{:T(128)S(6)} %select_n.49), kind=kOutput, calls=%fused_computation.29.clone.1 | convolution fusion | flops 1073741824 | bytes 36175876 | tf_op jit(solution)/shard_map/while/body/eval_jaxpr/qhd,khd->hqk/dot_general | solution.py:120
  591.3 24.9 %multiply_reduce_fusion.2 = (f32[8,512]{1,0:T(8,128)S(1)}, f32[8,512,2048]{2,1,0:T(8,128)}) fusion(f32[8,512,2048]{2,1,0:T(8,128)} %fusion.132, f32[8,512]{1,0:T(8,128)S(1)} %dynamic-slice_bitcast_fusion.2, bf16[2048,8,64]{0,2,1:T(8,128)(2,1)S(1)} %get-tuple-element.464, bf16[2048,8,64]{0,2,1:T(8,128)(2,1)} %get-tuple-element.461, ...), kind=kOutput, calls=%fused_computation.18.clone.1 | convolution fusion | flops 1115680768 | bytes 70811648 | tf_op jit(solution)/shard_map/while/body/eval_jaxpr/qhd,khd->hqk/dot_general | solution.py:109
  616.1 27.4 %multiply_convert_fusion.5 = bf16[8,512,2048]{2,1,0:T(8,128)(2,1)} fusion(f32[8,512,2048]{2,1,0:T(8,128)} %get-tuple-element.383, f32[8,512,2048]{2,1,0:T(8,128)} %fusion.132, f32[8,512]{1,0:T(8,128)S(1)} %get-tuple-element.384), kind=kLoop, calls=%fused_computation.17.clone.1 | loop fusion | flops 25165824 | bytes 83902464 | tf_op jit(solution)/shard_map/while/body/eval_jaxpr/convert_element_type | solution.py:124
  653.3 21.0 %dynamic_update_slice.19 = f32[4,512,8,64]{1,0,3,2:T(4,128)} dynamic-update-slice(f32[4,512,8,64]{1,0,3,2:T(4,128)} %get-tuple-element.443, f32[1,512,8,64]{1,0,3,2:T(1,128)S(1)} %copy.52, s32[]{:T(128)} %get-tuple-element.440, s32[]{:T(128)} %constant.48.clone.1..sunk.1, s32[]{:T(128)} %constant.48.clone.1..sunk.1, s32[]{:T(128)} %constant.48.clone.1..sunk.1) | dynamic-update-slice | bytes 2097156 | tf_op jit(solution)/shard_map/while/body/jit(dynamic_update_index_in_dim)/dynamic_update_slice | solution.py:94
  706.1 17.4 %fusion.132 = f32[8,512,2048]{2,1,0:T(8,128)} fusion(bf16[2048,8,64]{0,2,1:T(8,128)(2,1)} %get-tuple-element.467, bf16[2048,8,64]{0,2,1:T(8,128)(2,1)} %get-tuple-element.466, s32[]{:T(128)S(6)} %select_n.49), kind=kOutput, calls=%fused_computation.29.clone.1 | convolution fusion | flops 1073741824 | bytes 36175876 | tf_op jit(solution)/shard_map/while/body/eval_jaxpr/qhd,khd->hqk/dot_general | solution.py:120
  723.4 24.9 %multiply_reduce_fusion.2 = (f32[8,512]{1,0:T(8,128)S(1)}, f32[8,512,2048]{2,1,0:T(8,128)}) fusion(f32[8,512,2048]{2,1,0:T(8,128)} %fusion.132, f32[8,512]{1,0:T(8,128)S(1)} %dynamic-slice_bitcast_fusion.2, bf16[2048,8,64]{0,2,1:T(8,128)(2,1)S(1)} %get-tuple-element.464, bf16[2048,8,64]{0,2,1:T(8,128)(2,1)} %get-tuple-element.461, ...), kind=kOutput, calls=%fused_computation.18.clone.1 | convolution fusion | flops 1115680768 | bytes 70811648 | tf_op jit(solution)/shard_map/while/body/eval_jaxpr/qhd,khd->hqk/dot_general | solution.py:109
  748.3 27.4 %multiply_convert_fusion.5 = bf16[8,512,2048]{2,1,0:T(8,128)(2,1)} fusion(f32[8,512,2048]{2,1,0:T(8,128)} %get-tuple-element.383, f32[8,512,2048]{2,1,0:T(8,128)} %fusion.132, f32[8,512]{1,0:T(8,128)S(1)} %get-tuple-element.384), kind=kLoop, calls=%fused_computation.17.clone.1 | loop fusion | flops 25165824 | bytes 83902464 | tf_op jit(solution)/shard_map/while/body/eval_jaxpr/convert_element_type | solution.py:124
  785.5 21.0 %dynamic_update_slice.19 = f32[4,512,8,64]{1,0,3,2:T(4,128)} dynamic-update-slice(f32[4,512,8,64]{1,0,3,2:T(4,128)} %get-tuple-element.443, f32[1,512,8,64]{1,0,3,2:T(1,128)S(1)} %copy.52, s32[]{:T(128)} %get-tuple-element.440, s32[]{:T(128)} %constant.48.clone.1..sunk.1, s32[]{:T(128)} %constant.48.clone.1..sunk.1, s32[]{:T(128)} %constant.48.clone.1..sunk.1) | dynamic-update-slice | bytes 2097156 | tf_op jit(solution)/shard_map/while/body/jit(dynamic_update_index_in_dim)/dynamic_update_slice | solution.py:94
  855.6 24.9 %multiply_reduce_fusion.2 = (f32[8,512]{1,0:T(8,128)S(1)}, f32[8,512,2048]{2,1,0:T(8,128)}) fusion(f32[8,512,2048]{2,1,0:T(8,128)} %fusion.132, f32[8,512]{1,0:T(8,128)S(1)} %dynamic-slice_bitcast_fusion.2, bf16[2048,8,64]{0,2,1:T(8,128)(2,1)S(1)} %get-tuple-element.464, bf16[2048,8,64]{0,2,1:T(8,128)(2,1)} %get-tuple-element.461, ...), kind=kOutput, calls=%fused_computation.18.clone.1 | convolution fusion | flops 1115680768 | bytes 70811648 | tf_op jit(solution)/shard_map/while/body/eval_jaxpr/qhd,khd->hqk/dot_general | solution.py:109
  880.5 27.4 %multiply_convert_fusion.5 = bf16[8,512,2048]{2,1,0:T(8,128)(2,1)} fusion(f32[8,512,2048]{2,1,0:T(8,128)} %get-tuple-element.383, f32[8,512,2048]{2,1,0:T(8,128)} %fusion.132, f32[8,512]{1,0:T(8,128)S(1)} %get-tuple-element.384), kind=kLoop, calls=%fused_computation.17.clone.1 | loop fusion | flops 25165824 | bytes 83902464 | tf_op jit(solution)/shard_map/while/body/eval_jaxpr/convert_element_type | solution.py:124
  917.7 21.0 %dynamic_update_slice.19 = f32[4,512,8,64]{1,0,3,2:T(4,128)} dynamic-update-slice(f32[4,512,8,64]{1,0,3,2:T(4,128)} %get-tuple-element.443, f32[1,512,8,64]{1,0,3,2:T(1,128)S(1)} %copy.52, s32[]{:T(128)} %get-tuple-element.440, s32[]{:T(128)} %constant.48.clone.1..sunk.1, s32[]{:T(128)} %constant.48.clone.1..sunk.1, s32[]{:T(128)} %constant.48.clone.1..sunk.1) | dynamic-update-slice | bytes 2097156 | tf_op jit(solution)/shard_map/while/body/jit(dynamic_update_index_in_dim)/dynamic_update_slice | solution.py:94
  1019.1 19.3 %fusion.51 = bf16[2048,3,512]{2,0,1:T(8,128)(2,1)} fusion(bf16[2048,3,512]{0,2,1:T(8,128)(2,1)} %copy.35, bf16[2048,2048]{1,0:T(8,128)(2,1)} %all-gather.7.cloned.1.call-done), kind=kOutput, calls=%fused_computation.79 | convolution fusion | flops 12888047616 | bytes 20971520 | tf_op jit(solution)/shard_map/dot_general | solution.py:18
  1038.6 24.4 %fusion.72 = f32[2048,2048]{1,0:T(8,128)} fusion(bf16[2048,2048]{1,0:T(8,128)(2,1)} %all-gather.7.cloned.1.call-done, bf16[2048,2048]{1,0:T(8,128)(2,1)} %all-gather.13.cloned.1.call-done), kind=kOutput, calls=%fused_computation.124 | convolution fusion | flops 17179869184 | bytes 33554432 | tf_op jit(solution)/shard_map/dot_general | solution.py:196
  1063.0 36.4 %convert_reduce_fusion = (f32[2048]{0:T(1024)}, bf16[2048,2048]{1,0:T(8,128)(2,1)}) fusion(f32[2048,2048]{1,0:T(8,128)} %fusion.72, f32[2048]{0:T(1024)S(1)} %copy-done.21, bf16[2048,2048]{1,0:T(8,128)(2,1)} %all-gather.17.cloned.1.call-done, bf16[2048,2048]{1,0:T(8,128)(2,1)} %all-gather.15.cloned.1.call-done), kind=kOutput, calls=%fused_computation.50 | convolution fusion | flops 17276336128 | bytes 41959424 | tf_op jit(solution)/shard_map/dot_general | solution.py:24
  1099.4 24.1 %convolution_convert_fusion.1 = bf16[2048,2048]{1,0:T(8,128)(2,1)} fusion(bf16[2048,2048]{1,0:T(8,128)(2,1)} %all-gather.7.cloned.1.call-done, bf16[2048,2048]{1,0:T(8,128)(2,1)} %get-tuple-element.220), kind=kOutput, calls=%fused_computation.60 | convolution fusion | flops 17184063488 | bytes 25165824 | tf_op jit(solution)/shard_map/dot_general | solution.py:18
  1123.5 27.1 %convolution_convert_fusion = bf16[2048,2048]{1,0:T(8,128)(2,1)} fusion(bf16[2048,2048]{1,0:T(8,128)(2,1)} %all-gather.17.cloned.1.call-done, f32[2048,2048]{1,0:T(8,128)} %fusion.72, f32[2048]{0:T(1024)S(1)} %copy-done.21), kind=kOutput, calls=%fused_computation.59 | convolution fusion | flops 17226006528 | bytes 33562624 | tf_op jit(solution)/shard_map/dot_general | solution.py:18
  1150.7 20.6 %fusion.73 = f32[2048,2048,1]{1,0,2:T(8,128)} fusion(bf16[2048,3,512]{2,0,1:T(8,128)(2,1)} %get-tuple-element.222, bf16[2048,3,512]{2,0,1:T(8,128)(2,1)} %all-gather.9.cloned.1.call-done), kind=kOutput, calls=%fused_computation.125 | convolution fusion | flops 12884901888 | bytes 29360128 | tf_op jit(solution)/shard_map/dot_general | solution.py:24
  1171.3 25.6 %fusion.33 = bf16[2048,2048]{1,0:T(8,128)(2,1)} fusion(f32[2048,2048,1]{1,0,2:T(8,128)} %fusion.73, bf16[2048,2048]{1,0:T(8,128)(2,1)} %get-tuple-element.220, bf16[2048,2048]{1,0:T(8,128)(2,1)} %all-gather.13.cloned.1.call-done), kind=kOutput, calls=%fused_computation.49 | convolution fusion | flops 17188257792 | bytes 41943040 | tf_op jit(solution)/shard_map/dot_general | solution.py:24
  1208.6 31.4 %add_convert_fusion = bf16[2048,2048]{1,0:T(8,128)(2,1)} fusion(f32[2048,2048]{1,0:T(8,128)} %fusion.71, bf16[2048,2048]{1,0:T(8,128)(2,1)} %all-gather.15.cloned.1.call-done, f32[2048,2048]{1,0:T(8,128)} %fusion.72, f32[2048]{0:T(1024)S(1)} %copy-done.21), kind=kOutput, calls=%fused_computation.51 | convolution fusion | flops 17230200832 | bytes 50339840 | tf_op jit(solution)/shard_map/dot_general | solution.py:201
  1240.7 24.5 %all-reduce.1 = (f32[3,512]{1,0:T(4,128)}, f32[2048]{0:T(1024)}) all-reduce(f32[3,512]{1,0:T(4,128)S(1)} %copy-done.15, f32[2048]{0:T(1024)S(1)} %copy-done.16), channel_id=1, replica_groups=mesh['dp'=8,'tensor'=4] {'dp'}, use_global_device_ids=true, to_apply=%region_17.18 | all-reduce | flops 3584 | bytes 28672 | tf_op jit(solution)/shard_map/psum | solution.py:277
  1277.0 144.1 %reduce-scatter.9.cloned.1.call-done = bf16[512,2048]{1,0:T(8,128)(2,1)} async-done(((bf16[2048,2048]{1,0:T(8,128)(2,1)}), bf16[512,2048]{1,0:T(8,128)(2,1)}) %reduce-scatter.9.cloned.1.call-update) | async-done | bytes 2097168 | tf_op jit(solution)/shard_map/reduce_scatter | solution.py:254
  1424.6 143.9 %reduce-scatter.7.cloned.1.call-done = bf16[512,2048]{1,0:T(8,128)(2,1)} async-done(((bf16[2048,2048]{1,0:T(8,128)(2,1)}), bf16[512,2048]{1,0:T(8,128)(2,1)}) %reduce-scatter.7.cloned.1.call-update) | async-done | bytes 2097168 | tf_op jit(solution)/shard_map/reduce_scatter | solution.py:198
  1575.1 41.5 %all-reduce = (f32[2048]{0:T(1024)S(1)}, f32[2048]{0:T(1024)}, f32[2048]{0:T(1024)}) all-reduce(f32[2048]{0:T(1024)S(1)} %get-tuple-element.237, f32[2048]{0:T(1024)S(1)} %get-tuple-element.168, f32[2048]{0:T(1024)S(1)} %get-tuple-element.171), channel_id=1, replica_groups=mesh['dp'=8,'tensor'=4] {'dp','tensor'}, use_global_device_ids=true, to_apply=%region_20.21 | all-reduce | flops 6144 | bytes 49152 | tf_op jit(solution)/shard_map/psum | solution.py:269
  (198 shorter events, 493.8 us)
Async XLA Ops:
  7.2 5.1 copy-start
  7.2 51.0 %all-gather.9.cloned.1.call-start = ((), (), s32[]{:S(2)}) async-start(), calls=%async_computation.7 | async-start | bytes 7077888 | tf_op jit(solution)/shard_map/all_gather | solution.py:174
  7.9 202.1 %all-gather.7.cloned.1.call-start = ((), (), s32[]{:S(2)}) async-start(), calls=%async_computation.6 | async-start | bytes 10485760 | tf_op jit(solution)/shard_map/all_gather | solution.py:170
  9.9 7.7 copy-start.11
  9.9 7.8 copy-start.6
  12.2 6.2 copy-start.13
  15.1 414.3 %all-gather.11.cloned.1.call-start = ((), (), s32[]{:S(2)}) async-start(), calls=%async_computation.8 | async-start | bytes 2359296 | tf_op jit(solution)/shard_map/all_gather | solution.py:175
  15.9 413.6 %all-gather.17.cloned.1.call-start = ((), (), s32[]{:S(2)}) async-start(), calls=%async_computation.12 | async-start | bytes 10485760 | tf_op jit(solution)/shard_map/all_gather | solution.py:215
  16.5 1022.1 %all-gather.13.cloned.1.call-start = ((), (), s32[]{:S(2)}) async-start(), calls=%async_computation.9 | async-start | bytes 9437184 | tf_op jit(solution)/shard_map/all_gather | solution.py:176
  17.0 1045.9 %all-gather.15.cloned.1.call-start = ((), (), s32[]{:S(2)}) async-start(), calls=%async_computation.10 | async-start | bytes 9437184 | tf_op jit(solution)/shard_map/all_gather | solution.py:177
  17.6 1247.6 %reduce-scatter.13.cloned.1.call-start = ((), (), s32[]{:S(2)}) async-start(), calls=%async_computation.15 | async-start | bytes 2359296 | tf_op jit(solution)/shard_map/reduce_scatter | solution.py:244
  19.7 211.1 %copy-start.7 = (f32[2048,16]{0,1:T(8,128)}, f32[2048,16]{0,1:T(8,128)S(1)}, u32[]{:S(2)}) copy-start(f32[2048,16]{0,1:T(8,128)S(1)} %get-tuple-element.246) | copy-start | bytes 393220
  19.7 190.3 %copy-start.20 = (f32[3,512]{1,0:T(4,128)S(1)}, f32[3,512]{1,0:T(4,128)}, u32[]{:S(2)}) copy-start(f32[3,512]{1,0:T(4,128)} %param.22) | copy-start | bytes 18436
  968.3 9.6 copy-start.8
  968.3 9.6 copy-start.9
  991.5 5.3 copy-start.2
  991.5 5.3 copy-start.3
  1001.1 9.0 copy-start.4
  1019.1 247.9 %reduce-scatter.11.cloned.1.call-start = ((), (), s32[]{:S(2)}) async-start(), calls=%async_computation.14 | async-start | bytes 7077888 | tf_op jit(solution)/shard_map/reduce_scatter | solution.py:241
  1038.5 24.5 %copy-start.21 = (f32[2048]{0:T(1024)S(1)}, f32[2048]{0:T(1024)}, u32[]{:S(2)}) copy-start(f32[2048]{0:T(1024)} %param.26) | copy-start | bytes 24580
  1038.5 231.0 %reduce-scatter.15.cloned.1.call-start = ((), (), s32[]{:S(2)}) async-start(), calls=%async_computation.16 | async-start | bytes 9437184 | tf_op jit(solution)/shard_map/reduce_scatter | solution.py:247
  1123.5 150.8 %reduce-scatter.17.cloned.1.call-start = ((), (), s32[]{:S(2)}) async-start(), calls=%async_computation.17 | async-start | bytes 9437184 | tf_op jit(solution)/shard_map/reduce_scatter | solution.py:250
  1150.6 270.4 %reduce-scatter.9.cloned.1.call-start = ((), (), s32[]{:S(2)}) async-start(), calls=%async_computation.13 | async-start | bytes 10485760 | tf_op jit(solution)/shard_map/reduce_scatter | solution.py:254
  1196.9 1.6 copy-start.5
  1196.9 371.6 %reduce-scatter.7.cloned.1.call-start = ((), (), s32[]{:S(2)}) async-start(), calls=%async_computation.11 | async-start | bytes 10485760 | tf_op jit(solution)/shard_map/reduce_scatter | solution.py:198
  1240.0 0.7 copy-start.16
  1240.0 181.1 %copy-start.1 = (bf16[512,2048]{1,0:T(8,128)(2,1)S(1)}, bf16[512,2048]{1,0:T(8,128)(2,1)}, u32[]{:S(2)}) copy-start(bf16[512,2048]{1,0:T(8,128)(2,1)} %param.17) | copy-start | bytes 6291460
  1240.0 181.0 %copy-start.10 = (f32[2048]{0:T(1024)S(1)}, f32[2048]{0:T(1024)}, u32[]{:S(2)}) copy-start(f32[2048]{0:T(1024)} %param.19) | copy-start | bytes 24580
  1240.1 181.0 %copy-start.12 = (f32[512]{0:T(512)S(1)}, f32[512]{0:T(512)}, u32[]{:S(2)}) copy-start(f32[512]{0:T(512)} %copy-done.11) | copy-start | bytes 6148
  1240.1 181.0 %copy-start.14 = (f32[512]{0:T(512)S(1)}, f32[512]{0:T(512)}, u32[]{:S(2)}) copy-start(f32[512]{0:T(512)} %copy-done.13) | copy-start | bytes 6148
  1267.0 301.5 %copy-start.18 = (f32[2048]{0:T(1024)S(1)}, f32[2048]{0:T(1024)}, u32[]{:S(2)}) copy-start(f32[2048]{0:T(1024)} %param.28) | copy-start | bytes 24580
  1267.0 301.5 %copy-start.19 = (f32[2048]{0:T(1024)S(1)}, f32[2048]{0:T(1024)}, u32[]{:S(2)}) copy-start(f32[2048]{0:T(1024)} %param.24) | copy-start | bytes 24580
  (2 other events, 1.3 us)
Sparse Core Ops, SparseCore 0:
  9.9 48.2 all-gather.8
  60.3 149.6 all-gather.6
  211.9 26.4 all-gather.10
  239.8 149.6 all-gather.16
  391.2 52.6 all-gather.12
  445.6 55.9 all-gather.14
  1019.2 39.2 reduce-scatter.12
  1062.3 61.7 reduce-scatter.10
  1127.5 71.2 reduce-scatter.14
  1202.5 71.6 reduce-scatter.16
  1276.6 144.4 reduce-scatter.8
  1423.3 145.1 reduce-scatter.6
where the time goes:
time: 1640 us; the launch traced here: 1620 us
  matrix products  701 us (43%)
  waiting for transfers between devices  475 us (29%)
  other arithmetic  221 us (13%)
  local copies, waits for them, and re-layouts  141 us (9%)
  blocking collectives  66 us (4%)
    dot_general x8, matrix products, one_block(): jnp.einsum('qhd,khd->hqk', query_block, key_rows, preferred_element_type=...  161 us
    reduce_scatter x1, waiting for transfers between devices, local(): lax.psum_scatter((contract_cols(flat_grad, flat_qkv) + contract_cols(grad...  144 us
    reduce_scatter x1, waiting for transfers between devices, local(): lax.psum_scatter((jnp.dot(attended, w_out, preferred_element_type=jnp.flo...  144 us
    all_gather x1, waiting for transfers between devices, local(): lax.all_gather((normalized * ln_gain + ln_shift).astype(jnp.bfloat16), 't...  143 us
    convert_element_type x4, other arithmetic, one_block(): grad_scores = (attn_probs * (grad_probs - inner)).astype(jnp.bfloat16)  110 us
    dot_general x4, matrix products, contract_cols(): lax.dot_general(left_op, right_op, (((1,), (1,)), ((), ())), preferred_el...  92.6 us
    dynamic_update_slice x8, local copies, waits for them, and re-layouts, attend(): lax.map(one_block, jnp.arange(group_rows // block_rows, dtype=jnp.int32))  88.3 us
    dot_general x4, matrix products, contract_rows(): lax.dot_general(left_op, right_op, (((0,), (0,)), ((), ())), preferred_el...  79.5 us
  transfers between devices with their start and end apart: 12, of which 5 were waited for; matrix products, arithmetic and copies ran while one was open for 65% of the time, Pallas kernels for 0%

commit v1 on v0

v1 whole, which is shorter than its diff:
```python
import functools

import jax
import jax.numpy as jnp
from jax import lax
from jax.experimental import pallas as pl
from jax.experimental.pallas import tpu as pltpu
from jax.sharding import PartitionSpec as P

HD = 64
ROT = 32
EPS = 1e-05
ROPE_BASE = 10000.0
NEGATIVE = -1e30
BLOCK = 256
ROWS = 256
SHRINK = 20

F32 = jnp.float32
BF16 = jnp.bfloat16


def dot_nn(a, b):
    return lax.dot_general(a, b, (((1,), (0,)), ((), ())), preferred_element_type=F32)


def dot_nt(a, b):
    return lax.dot_general(a, b, (((1,), (1,)), ((), ())), preferred_element_type=F32)


def dot_tn(a, b):
    return lax.dot_general(a, b, (((0,), (0,)), ((), ())), preferred_element_type=F32)


def cost(flops, moved, trans=0):
    return pl.CostEstimate(flops=int(flops / SHRINK), bytes_accessed=int(moved / SHRINK), transcendentals=0)


def whole(a):
    return pl.BlockSpec(a.shape, lambda *_: (0,) * a.ndim)


def seq_starts(segment_row):
    count = segment_row.shape[0]
    index = jnp.arange(count, dtype=jnp.int32)
    begins = jnp.concatenate([jnp.ones((1,), dtype=bool), segment_row[1:] != segment_row[:-1]])
    return lax.cummax(jnp.where(begins, index, jnp.zeros_like(index)), axis=0)


def rotary_tables(positions):
    half = ROT // 2
    lane = jnp.arange(128, dtype=jnp.int32) % HD
    frequency = ROPE_BASE ** (-((lane % half).astype(F32) * 2.0) / ROT)
    angles = positions.astype(F32)[:, None] * frequency[None, :]
    cosine = jnp.where(lane < ROT, jnp.cos(angles), 1.0)
    sine = jnp.sin(angles)
    sine_up = jnp.where(lane < half, -sine, 0.0)
    sine_down = jnp.where((lane >= half) & (lane < ROT), sine, 0.0)
    return cosine, sine_up, sine_down


def rotate(x, cosine, sine_up, sine_down):
    return (
        x * cosine
        + pltpu.roll(x, 128 - ROT // 2, axis=1) * sine_up
        + pltpu.roll(x, ROT // 2, axis=1) * sine_down
    )


def unrotate(x, cosine, sine_up, sine_down):
    return (
        x * cosine
        - pltpu.roll(x, 128 - ROT // 2, axis=1) * sine_up
        - pltpu.roll(x, ROT // 2, axis=1) * sine_down
    )


def norm_kernel(x_ref, gain_ref, shift_ref, o_ref):
    x = x_ref[...].astype(F32)
    centred = x - jnp.mean(x, axis=1, keepdims=True)
    inv_std = lax.rsqrt(jnp.mean(centred * centred, axis=1, keepdims=True) + EPS)
    o_ref[...] = (centred * inv_std * gain_ref[...] + shift_ref[...]).astype(BF16)


def norm(x, gain, shift):
    rows, width = x.shape
    step = rows // 2
    row = pl.BlockSpec((1, width), lambda i: (0, 0))
    tile = pl.BlockSpec((step, width), lambda i: (i, 0))
    return pl.pallas_call(
        norm_kernel,
        grid=(rows // step,),
        in_specs=[tile, row, row],
        out_specs=tile,
        out_shape=jax.ShapeDtypeStruct(x.shape, BF16),
        cost_estimate=cost(rows * width * 8, rows * width * 4),
        name="norm",
    )(x, gain, shift)


def norm_back_kernel(x_ref, cot_ref, *refs):
    gain_ref, o_ref, sums_ref = refs[-3:]

    @pl.when(pl.program_id(0) == 0)
    def _():
        sums_ref[...] = jnp.zeros_like(sums_ref)

    x = x_ref[...].astype(F32)
    centred = x - jnp.mean(x, axis=1, keepdims=True)
    inv_std = lax.rsqrt(jnp.mean(centred * centred, axis=1, keepdims=True) + EPS)
    normalized = centred * inv_std
    grad = jnp.concatenate([r[...] for r in refs[:-3]], axis=1).astype(F32)
    sums_ref[0:1, :] += jnp.sum(grad * normalized, axis=0, keepdims=True)
    sums_ref[1:2, :] += jnp.sum(grad, axis=0, keepdims=True)
    cot = cot_ref[...].astype(F32)
    sums_ref[2:3, :] += jnp.sum(cot, axis=0, keepdims=True)
    scaled = grad * gain_ref[...]
    first = jnp.mean(scaled, axis=1, keepdims=True)
    second = jnp.mean(scaled * normalized, axis=1, keepdims=True)
    o_ref[...] = (inv_std * (scaled - first - normalized * second) + cot).astype(BF16)


def norm_back(x, cot, grads, gain):
    rows, width = x.shape
    step = min(128, rows)
    tile = pl.BlockSpec((step, width), lambda i: (i, 0))
    return pl.pallas_call(
        norm_back_kernel,
        grid=(rows // step,),
        in_specs=[tile, tile]
        + [pl.BlockSpec((step, g.shape[1]), lambda i: (i, 0)) for g in grads]
        + [pl.BlockSpec((1, width), lambda i: (0, 0))],
        out_specs=[tile, pl.BlockSpec((8, width), lambda i: (0, 0))],
        out_shape=[jax.ShapeDtypeStruct(x.shape, BF16), jax.ShapeDtypeStruct((8, width), F32)],
        cost_estimate=cost(rows * width * 20, rows * width * 12),
        name="norm_back",
    )(x, cot, *grads, gain)


def pick(where_ref, i, tiles):
    turn = lax.div(i, tiles)
    busy = turn < where_ref[4]
    slot = jnp.where(busy, where_ref[2 * turn], where_ref[5])
    return jnp.where(busy, lax.rem(i, tiles), tiles - 1), slot, busy


def pick_shard(where_ref, i, tiles, refs, o_ref):
    turn = lax.div(i, tiles)
    if len(refs) == 1:
        o_ref[...] = refs[0][...]
        return

    @pl.when(where_ref[2 * turn + 1] == 0)
    def _():
        o_ref[...] = refs[0][...]

    @pl.when(where_ref[2 * turn + 1] == 1)
    def _():
        o_ref[...] = refs[1][...]


def project_tile(j, tall, x_ref, wq_ref, wu_ref, bq_ref, bu_ref, tables, qkv_ref, act_ref, slope_ref, over):
    if qkv_ref is not None:
        width = wq_ref.shape[1]

        @pl.when(j < 2)
        def _():
            scale = jnp.where(j == 0, HD**-0.5, 1.0).astype(F32)

            def turned(m, t):
                raw = (dot_nn(x_ref[m, :], wq_ref[...]) + bq_ref[...]) * scale
                turn = [r[t, :] for r in tables]
                for p in range(width // 128):
                    lanes = slice(p * 128, (p + 1) * 128)
                    qkv_ref[m, lanes] = rotate(raw[:, lanes], *turn).astype(BF16)

            over(turned)

        @pl.when(j == 2)
        def _():
            def plain(m, t):
                qkv_ref[m, :] = (dot_nn(x_ref[m, :], wq_ref[...]) + bq_ref[...]).astype(BF16)

            over(plain)

    if act_ref is not None:

        @pl.when(j > 2)
        def _():
            def gelu(m, t):
                act_ref[m, :], slope_ref[m, :] = gelu_and_slope(dot_nn(x_ref[m, :], wu_ref[...]) + bu_ref[...])

            over(gelu)


def gelu_and_slope(v):
    root = 0.7978845608028654
    cubic = 0.044715
    square = v * v
    t = jnp.tanh(v * (root + (root * cubic) * square))
    half = 0.5 + 0.5 * t
    slope = half + (v * (0.5 - 0.5 * (t * t))) * (root + (3.0 * root * cubic) * square)
    return (v * half).astype(BF16), slope.astype(BF16)


def forward_kernel(came, tiles, where_ref, *refs):
    x_refs, refs = refs[:came], refs[came:]
    wq_ref, wu_ref, bq_ref, bu_ref = refs[:4]
    tables = refs[4:7]
    normed_ref, qkv_ref, act_ref, slope_ref = refs[-4:]
    i = pl.program_id(0)
    j, _, busy = pick(where_ref, i, tiles)
    rows = normed_ref.shape[0]
    step = min(ROWS, rows)

    @pl.when(busy & (j == 0))
    def _():
        pick_shard(where_ref, i, tiles, x_refs, normed_ref)

    def over(act):
        for m in range(0, rows, step):
            act(slice(m, m + step), slice(m, m + step))

    @pl.when(busy)
    def _():
        project_tile(j, None, normed_ref, wq_ref, wu_ref, bq_ref, bu_ref, tables, qkv_ref, act_ref, slope_ref, over)


def queries_kernel(came, tiles, where_ref, *refs):
    x_refs, refs = refs[:came], refs[came:]
    wq_ref, bq_ref = refs[:2]
    tables = refs[2:5]
    normed_ref, qkv_ref = refs[-2:]
    i = pl.program_id(0)
    j, _, busy = pick(where_ref, i, tiles)
    rows = normed_ref.shape[0]
    step = min(ROWS, rows)

    @pl.when(busy & (j == 0))
    def _():
        pick_shard(where_ref, i, tiles, x_refs, normed_ref)

    def over(act):
        for m in range(0, rows, step):
            act(slice(m, m + step), slice(m, m + step))

    @pl.when(busy)
    def _():
        project_tile(j, None, normed_ref, wq_ref, None, bq_ref, None, tables, qkv_ref, None, None, over)


def queries_chunk(where, xs, wq, bq, tables, bufs, parts):
    rows, depth = xs[0].shape
    width = wq.shape[1] // 3
    tiles = 3

    def at(k):
        def index(i, w):
            j, slot, _ = pick(w, i, tiles)
            return ((slot, j), (0, j), (0, 0), (slot, 0), (jnp.minimum(slot, parts - 1), 0))[k]

        return index

    args = [where, *xs, wq, bq, *tables]
    return pl.pallas_call(
        functools.partial(queries_kernel, len(xs), tiles),
        grid_spec=pltpu.PrefetchScalarGridSpec(
            num_scalar_prefetch=1,
            grid=(len(xs) * tiles,),
            in_specs=[pl.BlockSpec((rows, depth), at(2))] * len(xs)
            + [pl.BlockSpec((depth, width), at(1)), pl.BlockSpec((1, width), at(1))]
            + [pl.BlockSpec((rows, 128), at(4))] * 3
            + [pl.BlockSpec(memory_space=pl.ANY)] * 2,
            out_specs=[pl.BlockSpec((rows, depth), at(3)), pl.BlockSpec((rows, width), at(0))],
        ),
        out_shape=[jax.ShapeDtypeStruct(b.shape, BF16) for b in bufs],
        input_output_aliases={len(args): 0, len(args) + 1: 1},
        cost_estimate=cost(6 * rows * depth * width, 6 * depth * width),
        name="queries_chunk",
    )(*args, *bufs)


def forward_chunk(where, xs, wq, wu, bq, bu, tables, bufs, parts):
    rows, depth = xs[0].shape
    width = wq.shape[1] // 3
    ff = wu.shape[1]
    tiles = 3 + ff // width

    def at(k):
        def index(i, w):
            j, slot, _ = pick(w, i, tiles)
            return (
                (slot, jnp.minimum(j, 2)),
                (slot, jnp.maximum(j - 3, 0)),
                (slot, 0),
                (0, jnp.minimum(j, 2)),
                (0, jnp.maximum(j - 3, 0)),
                (0, 0),
                (jnp.minimum(slot, parts - 1), 0),
            )[k]

        return index

    in_specs = (
        [pl.BlockSpec((rows, depth), at(5))] * len(xs)
        + [
            pl.BlockSpec((depth, width), at(3)),
            pl.BlockSpec((depth, width), at(4)),
            pl.BlockSpec((1, width), at(3)),
            pl.BlockSpec((1, width), at(4)),
        ]
        + [pl.BlockSpec((rows, 128), at(6))] * 3
    )
    total = (parts + 1) * rows
    shapes = [(total, depth), (total, 3 * width), (total, ff), (total, ff)]
    args = [where, *xs, wq, wu, bq, bu, *tables]
    aliases = {}
    if bufs is not None:
        aliases = {len(args) + k: k for k in range(4)}
        args += list(bufs)
        in_specs += [pl.BlockSpec(memory_space=pl.ANY)] * 4
    return pl.pallas_call(
        functools.partial(forward_kernel, len(xs), tiles),
        grid_spec=pltpu.PrefetchScalarGridSpec(
            num_scalar_prefetch=1,
            grid=(len(xs) * tiles,),
            in_specs=in_specs,
            out_specs=[
                pl.BlockSpec((rows, depth), at(2)),
                pl.BlockSpec((rows, width), at(0)),
                pl.BlockSpec((rows, width), at(1)),
                pl.BlockSpec((rows, width), at(1)),
            ],
        ),
        out_shape=[jax.ShapeDtypeStruct(s, BF16) for s in shapes],
        input_output_aliases=aliases,
        cost_estimate=cost(2 * rows * depth * (3 * width + ff), 2 * depth * (3 * width + ff)),
        name="forward_chunk",
    )(*args)


def collect(where_ref, came, shards, x_refs, held_ref, full_ref, in_sems, out_sems, first, last):
    rows = x_refs[0].shape[0]

    def spot(c):
        return pl.ds(pl.multiple_of(where_ref[1 + shards + 2 * c] * rows, rows), rows)

    def loads(c):
        return pltpu.make_async_copy(x_refs[c], held_ref.at[spot(c)], in_sems.at[c])

    def stores(c):
        return pltpu.make_async_copy(held_ref.at[spot(c)], full_ref.at[spot(c)], out_sems.at[c])

    def each(act):
        for c in range(came):
            pl.when(where_ref[2 + shards + 2 * c] > 0)(functools.partial(act, c))

    @pl.when(first)
    def _():
        each(lambda c: loads(c).start())
        each(lambda c: loads(c).wait())
        if full_ref is not None:
            each(lambda c: stores(c).start())

    def finish():
        pl.when(last)(lambda: each(lambda c: stores(c).wait()))

    return finish


def early_over(where_ref, rows):
    step = min(ROWS, rows)

    def over(act):
        def body(t, carry):
            for m in range(0, rows, step):
                at = pl.ds(pl.multiple_of(where_ref[1 + t] * rows + m, step), step)
                act(at, at)
            return carry

        lax.fori_loop(0, where_ref[0], body, 0)

    return over


def queries_early_kernel(came, shards, where_ref, *refs):
    x_refs, refs = refs[:came], refs[came:]
    wq_ref, bq_ref = refs[:2]
    tables = refs[2:5]
    normed_ref, qkv_ref, held_ref, in_sems, out_sems = refs[5:]
    j = pl.program_id(0)
    finish = collect(
        where_ref, came, shards, x_refs, held_ref, normed_ref, in_sems, out_sems,
        j == 0, j == pl.num_programs(0) - 1,
    )
    over = early_over(where_ref, x_refs[0].shape[0])
    project_tile(j, None, held_ref, wq_ref, None, bq_ref, None, tables, qkv_ref, None, None, over)
    finish()


def units_early_kernel(came, shards, where_ref, *refs):
    x_refs, refs = refs[:came], refs[came:]
    wu_ref, bu_ref, act_ref, slope_ref, held_ref, in_sems = refs
    j = pl.program_id(0)
    collect(where_ref, came, shards, x_refs, held_ref, None, in_sems, None, j == 0, None)
    over = early_over(where_ref, x_refs[0].shape[0])
    project_tile(j + 3, None, held_ref, None, wu_ref, None, bu_ref, None, None, act_ref, slope_ref, over)


def queries_early(where, xs, wq, bq, tables, parts):
    rows, depth = xs[0].shape
    width = wq.shape[1] // 3
    count = parts * rows
    in_place = pl.BlockSpec(memory_space=pl.ANY)
    return pl.pallas_call(
        functools.partial(queries_early_kernel, len(xs), parts),
        grid_spec=pltpu.PrefetchScalarGridSpec(
            num_scalar_prefetch=1,
            grid=(3,),
            in_specs=[in_place] * len(xs)
            + [pl.BlockSpec((depth, width), lambda j, w: (0, j)), pl.BlockSpec((1, width), lambda j, w: (0, j))]
            + [whole(t) for t in tables],
            out_specs=[in_place, pl.BlockSpec((count, width), lambda j, w: (0, j))],
            scratch_shapes=[
                pltpu.VMEM((count, depth), BF16),
                pltpu.SemaphoreType.DMA((len(xs),)),
                pltpu.SemaphoreType.DMA((len(xs),)),
            ],
        ),
        out_shape=[
            jax.ShapeDtypeStruct((count + rows, depth), BF16),
            jax.ShapeDtypeStruct((count + rows, 3 * width), BF16),
        ],
        cost_estimate=cost(6 * count * depth * width, 6 * depth * width),
        name="queries_early",
    )(where, *xs, wq, bq, *tables)


def units_early(where, xs, wu, bu, width, parts):
    rows, depth = xs[0].shape
    ff = wu.shape[1]
    count = parts * rows
    return pl.pallas_call(
        functools.partial(units_early_kernel, len(xs), parts),
        grid_spec=pltpu.PrefetchScalarGridSpec(
            num_scalar_prefetch=1,
            grid=(ff // width,),
            in_specs=[pl.BlockSpec(memory_space=pl.ANY)] * len(xs)
            + [pl.BlockSpec((depth, width), lambda j, w: (0, j)), pl.BlockSpec((1, width), lambda j, w: (0, j))],
            out_specs=[pl.BlockSpec((count, width), lambda j, w: (0, j))] * 2,
            scratch_shapes=[pltpu.VMEM((count, depth), BF16), pltpu.SemaphoreType.DMA((len(xs),))],
        ),
        out_shape=[jax.ShapeDtypeStruct((count + rows, ff), BF16)] * 2,
        cost_estimate=cost(2 * count * depth * ff, 2 * depth * ff),
        name="units_early",
    )(where, *xs, wu, bu)


def backward_early_kernel(came, shards, where_ref, *refs):
    c_refs, refs = refs[:came], refs[came:]
    wo_ref, wd_ref, slope_ref, cot_ref, ga_ref, gh_ref, held_ref, in_sems, out_sems = refs
    j = pl.program_id(0)
    finish = collect(
        where_ref, came, shards, c_refs, held_ref, cot_ref, in_sems, out_sems,
        j == 0, j == pl.num_programs(0) - 1,
    )
    rows = c_refs[0].shape[0]
    step = min(ROWS, rows)

    def over(act):
        def body(t, carry):
            for m in range(0, rows, step):
                act(pl.ds(pl.multiple_of(where_ref[1 + t] * rows + m, step), step))
            return carry

        lax.fori_loop(0, where_ref[0], body, 0)

    @pl.when(j == 0)
    def _():
        weight = side_by_side(wo_ref)

        def act(m):
            ga_ref[m, :] = dot_nt(held_ref[m, :], weight).astype(BF16)

        over(act)

    @pl.when(j > 0)
    def _():
        weight = side_by_side(wd_ref)

        def act(m):
            gh_ref[m, :] = (dot_nt(held_ref[m, :], weight) * slope_ref[m, :].astype(F32)).astype(BF16)

        over(act)

    finish()


def backward_early(where, cots, wo, wd, slope, parts):
    rows, depth = cots[0].shape
    pieces, width, piece = wo.shape
    ff = wd.shape[1]
    count = parts * rows
    total = count + rows
    in_place = pl.BlockSpec(memory_space=pl.ANY)

    def tile(j):
        return jnp.maximum(j - 1, 0)

    return pl.pallas_call(
        functools.partial(backward_early_kernel, len(cots), parts),
        grid_spec=pltpu.PrefetchScalarGridSpec(
            num_scalar_prefetch=1,
            grid=(1 + ff // width,),
            in_specs=[in_place] * len(cots)
            + [
                whole(wo),
                pl.BlockSpec((pieces, width, piece), lambda j, w: (0, tile(j), 0)),
                pl.BlockSpec((count, width), lambda j, w: (0, tile(j))),
            ],
            out_specs=[
                in_place,
                pl.BlockSpec((count, width), lambda j, w: (0, 0)),
                pl.BlockSpec((count, width), lambda j, w: (0, tile(j))),
            ],
            scratch_shapes=[
                pltpu.VMEM((count, depth), BF16),
                pltpu.SemaphoreType.DMA((len(cots),)),
                pltpu.SemaphoreType.DMA((len(cots),)),
            ],
        ),
        out_shape=[jax.ShapeDtypeStruct(s, BF16) for s in ((total, depth), (total, width), (total, ff))],
        cost_estimate=cost(2 * count * depth * (width + ff), 2 * depth * (width + ff)),
        name="backward_early",
    )(where, *cots, wo, wd, slope)


def low_lanes(rows):
    return lax.broadcasted_iota(jnp.int32, (rows, 128), 1) < HD


def attend_kernel(
    first_ref, q_ref, k_ref, v_ref, segc_ref, segr_ref, *refs
):
    o_ref, lse_ref, max_ref, acc_ref, bias_ref = refs[-5:]
    i = pl.program_id(0)
    block, width = q_ref.shape
    pairs = width // 128
    low = low_lanes(block)
    owns = (low, jnp.logical_not(low))
    max_ref[...] = jnp.full_like(max_ref, NEGATIVE)
    lse_ref[...] = jnp.zeros_like(lse_ref)
    acc_ref[...] = jnp.zeros_like(acc_ref)
    q0 = pl.multiple_of(i * block, block)
    query_seg = segr_ref[:, pl.ds(q0, block)]
    query_row = q0 + lax.broadcasted_iota(jnp.int32, (1, block), 1)

    def set_bias(k0):
        key_seg = segc_ref[pl.ds(k0, block), :]
        key_row = k0 + lax.broadcasted_iota(jnp.int32, (block, 1), 0)
        bias_ref[...] = jnp.where((key_seg == query_seg) & (key_row <= query_row), 0.0, NEGATIVE)

    def scores(k0, p, h):
        lanes = slice(p * 128, (p + 1) * 128)
        q = q_ref[:, lanes]
        mine = jnp.where(owns[h], q, jnp.zeros_like(q))
        return dot_nt(k_ref[pl.ds(k0, block), lanes], mine) + bias_ref[...]

    def find_max(j, carry):
        k0 = pl.multiple_of(j * block, block)
        set_bias(k0)
        for p in range(pairs):
            for h in range(2):
                s = scores(k0, p, h)
                max_ref[2 * p + h] = jnp.maximum(max_ref[2 * p + h], jnp.max(s, axis=0, keepdims=True))
        return carry

    lax.fori_loop(first_ref[i], i + 1, find_max, 0)

    def add_up(j, carry):
        k0 = pl.multiple_of(j * block, block)
        set_bias(k0)
        for p in range(pairs):
            v = v_ref[pl.ds(k0, block), p * 128 : (p + 1) * 128]
            for h in range(2):
                e = jnp.exp(scores(k0, p, h) - max_ref[2 * p + h])
                lse_ref[p, h : h + 1, :] += jnp.sum(e, axis=0, keepdims=True)
                acc_ref[2 * p + h] += dot_tn(e.astype(BF16), jnp.where(owns[h], v, jnp.ones_like(v)))
        return carry

    lax.fori_loop(first_ref[i], i + 1, add_up, 0)
    for p in range(pairs):
        even, odd = acc_ref[2 * p], acc_ref[2 * p + 1]
        o_ref[:, p * 128 : (p + 1) * 128] = jnp.where(
            low, even / pltpu.roll(even, HD, axis=1), odd / pltpu.roll(odd, HD, axis=1)
        ).astype(BF16)
        for h in range(2):
            lse_ref[p, h : h + 1, :] = max_ref[2 * p + h] + jnp.log(lse_ref[p, h : h + 1, :])


def attend(qkv, segc, segr, first, part, parts, bufs):
    count = segr.shape[1]
    whole_width = qkv.shape[1] // 3
    width = whole_width // parts
    pairs = width // 128
    in_place = [] if bufs is None else [pl.BlockSpec(memory_space=pl.ANY)] * 2
    return pl.pallas_call(
        attend_kernel,
        grid_spec=pltpu.PrefetchScalarGridSpec(
            num_scalar_prefetch=1,
            grid=(count // BLOCK,),
            in_specs=[
                pl.BlockSpec((BLOCK, width), lambda i, f: (i, part)),
                pl.BlockSpec((count, width), lambda i, f: (0, parts + part)),
                pl.BlockSpec((count, width), lambda i, f: (0, 2 * parts + part)),
                whole(segc),
                whole(segr),
            ]
            + in_place,
            out_specs=[
                pl.BlockSpec((BLOCK, width), lambda i, f: (i, part)),
                pl.BlockSpec((pairs, 8, BLOCK), lambda i, f: (part, 0, i)),
            ],
            scratch_shapes=[
                pltpu.VMEM((2 * pairs, 1, BLOCK), F32),
                pltpu.VMEM((2 * pairs, BLOCK, 128), F32),
                pltpu.VMEM((BLOCK, BLOCK), F32),
            ],
        ),
        out_shape=[
            jax.ShapeDtypeStruct((count, whole_width), BF16),
            jax.ShapeDtypeStruct((parts * pairs, 8, count), F32),
        ],
        input_output_aliases={} if bufs is None else {6: 0, 7: 1},
        cost_estimate=cost(30e9 * width / 512, count * width * 8),
        name="attend",
    )(first, qkv, qkv, qkv, segc, segr, *([] if bufs is None else bufs))


def attend_back_kernel(
    first_ref, q_ref, k_ref, v_ref, go_ref, o_ref, lse_ref, segc_ref, segr_ref,
    cos_ref, up_ref, down_ref, *refs,
):
    gq_ref, gk_ref, gv_ref, dq_ref, dk_ref, dv_ref, bias_ref = refs[-7:]
    i = pl.program_id(0)
    steps = pl.num_programs(0)
    block, width = q_ref.shape
    pairs = width // 128
    low = low_lanes(block)
    owns = (low, jnp.logical_not(low))

    @pl.when(i == 0)
    def _():
        dk_ref[...] = jnp.zeros_like(dk_ref)
        dv_ref[...] = jnp.zeros_like(dv_ref)

    dq_ref[...] = jnp.zeros_like(dq_ref)
    q0 = pl.multiple_of(i * block, block)
    query_seg = segr_ref[:, pl.ds(q0, block)]
    query_row = q0 + lax.broadcasted_iota(jnp.int32, (1, block), 1)
    half = jnp.where(
        lax.broadcasted_iota(jnp.int32, (8, 128), 1) // HD == lax.broadcasted_iota(jnp.int32, (8, 128), 0),
        1.0,
        0.0,
    ).astype(F32)
    inner = []
    for p in range(pairs):
        lanes = slice(p * 128, (p + 1) * 128)
        product = go_ref[:, lanes].astype(F32) * o_ref[:, lanes].astype(F32)
        inner.append(
            lax.dot_general(
                half, product, (((1,), (1,)), ((), ())),
                precision=lax.Precision.HIGHEST, preferred_element_type=F32,
            )
        )

    def body(j, carry):
        k0 = pl.multiple_of(j * block, block)
        key_seg = segc_ref[pl.ds(k0, block), :]
        key_row = k0 + lax.broadcasted_iota(jnp.int32, (block, 1), 0)
        bias_ref[...] = jnp.where((key_seg == query_seg) & (key_row <= query_row), 0.0, NEGATIVE)
        for p in range(pairs):
            lanes = slice(p * 128, (p + 1) * 128)
            k = k_ref[pl.ds(k0, block), lanes]
            v = v_ref[pl.ds(k0, block), lanes]
            q = q_ref[:, lanes]
            go = go_ref[:, lanes]
            sums = None
            for h in range(2):
                q_own, go_own, k_own = [jnp.where(owns[h], a, jnp.zeros_like(a)) for a in (q, go, k)]
                prob = jnp.exp(dot_nt(k, q_own) + bias_ref[...] - lse_ref[p, h : h + 1, :])
                grad_score = (prob * (dot_nt(v, go_own) - inner[p][h : h + 1, :])).astype(BF16)
                new = (
                    dot_nn(prob.astype(BF16), go_own),
                    dot_nn(grad_score, q_own),
                    dot_tn(grad_score, k_own),
                )
                sums = new if sums is None else tuple(a + b for a, b in zip(sums, new))
            dv_ref[pl.ds(k0, block), lanes] += sums[0]
            dk_ref[pl.ds(k0, block), lanes] += sums[1]
            dq_ref[:, lanes] += sums[2]
        return carry

    lax.fori_loop(first_ref[i], i + 1, body, 0)
    turn = [r[pl.ds(q0, block), :] for r in (cos_ref, up_ref, down_ref)]
    for p in range(pairs):
        lanes = slice(p * 128, (p + 1) * 128)
        gq_ref[:, lanes] = unrotate(dq_ref[:, lanes] * HD**-0.5, *turn).astype(BF16)

    @pl.when(i == steps - 1)
    def _():
        def finish(j, carry):
            k0 = pl.multiple_of(j * block, block)
            rows = pl.ds(k0, block)
            turn = [r[rows, :] for r in (cos_ref, up_ref, down_ref)]
            for p in range(pairs):
                lanes = slice(p * 128, (p + 1) * 128)
                gk_ref[rows, lanes] = unrotate(dk_ref[rows, lanes], *turn).astype(BF16)
                gv_ref[rows, lanes] = dv_ref[rows, lanes].astype(BF16)
            return carry

        lax.fori_loop(0, steps, finish, 0)


def attend_back(qkv, grad_out, out, lse, segc, segr, first, tables, part, parts, bufs):
    count = segr.shape[1]
    whole_width = qkv.shape[1] // 3
    width = whole_width // parts
    pairs = width // 128
    row_tile = pl.BlockSpec((BLOCK, width), lambda i, f: (i, part))
    column = pl.BlockSpec((count, width), lambda i, f: (0, part))
    in_place = [] if bufs is None else [pl.BlockSpec(memory_space=pl.ANY)] * 3
    args = [first, qkv, qkv, qkv, grad_out, out, lse, segc, segr, *tables]
    return pl.pallas_call(
        attend_back_kernel,
        grid_spec=pltpu.PrefetchScalarGridSpec(
            num_scalar_prefetch=1,
            grid=(count // BLOCK,),
            in_specs=[
                row_tile,
                pl.BlockSpec((count, width), lambda i, f: (0, parts + part)),
                pl.BlockSpec((count, width), lambda i, f: (0, 2 * parts + part)),
                row_tile,
                row_tile,
                pl.BlockSpec((pairs, 8, BLOCK), lambda i, f: (part, 0, i)),
                whole(segc),
                whole(segr),
                *[whole(t) for t in tables],
            ]
            + in_place,
            out_specs=[row_tile, column, column],
            scratch_shapes=[
                pltpu.VMEM((BLOCK, width), F32),
                pltpu.VMEM((count, width), F32),
                pltpu.VMEM((count, width), F32),
                pltpu.VMEM((BLOCK, BLOCK), F32),
            ],
        ),
        out_shape=[jax.ShapeDtypeStruct((count, whole_width), BF16)] * 3,
        input_output_aliases={} if bufs is None else {len(args) + k: k for k in range(3)},
        cost_estimate=cost(44e9 * width / 512, count * width * 20),
        name="attend_back",
    )(*args, *([] if bufs is None else bufs))


def side_by_side(ref):
    return jnp.concatenate([ref[b] for b in range(ref.shape[0])], axis=1)


def mix_kernel(att_ref, act_ref, wo_ref, wd_ref, o_ref):
    wo, wd = side_by_side(wo_ref), side_by_side(wd_ref)
    step = min(512, att_ref.shape[0])
    for m in range(0, att_ref.shape[0], step):
        rs = slice(m, m + step)
        o_ref[rs, :] = (dot_nn(att_ref[rs, :], wo) + dot_nn(act_ref[rs, :], wd)).astype(BF16)


def mix(att, act, wo, wd):
    pieces, width, piece = wo.shape
    ff = wd.shape[1]
    count = att.shape[0]
    group = max(1, 512 // piece)
    return pl.pallas_call(
        mix_kernel,
        grid=(pieces // group,),
        in_specs=[
            pl.BlockSpec((count, width), lambda j: (0, 0)),
            pl.BlockSpec((count, ff), lambda j: (0, 0)),
            pl.BlockSpec((group, width, piece), lambda j: (j, 0, 0)),
            pl.BlockSpec((group, ff, piece), lambda j: (j, 0, 0)),
        ],
        out_specs=pl.BlockSpec((count, group * piece), lambda j: (0, j)),
        out_shape=jax.ShapeDtypeStruct((count, pieces * piece), BF16),
        cost_estimate=cost(2 * count * (width + ff) * pieces * piece, 4 * count * ff),
        name="mix",
    )(att, act, wo, wd)


def mixed_kernel(x_ref, sum_ref, bias_ref, o_ref):
    o_ref[...] = (x_ref[...].astype(F32) + sum_ref[...].astype(F32) + bias_ref[...]).astype(BF16)


def mixed_out(x, total, bias):
    rows, width = x.shape
    step = min(256, rows)
    tile = pl.BlockSpec((step, width), lambda i: (i, 0))
    return pl.pallas_call(
        mixed_kernel,
        grid=(rows // step,),
        in_specs=[tile, tile, pl.BlockSpec((1, width), lambda i: (0, 0))],
        out_specs=tile,
        out_shape=jax.ShapeDtypeStruct(x.shape, BF16),
        cost_estimate=cost(rows * width * 4, rows * width * 6),
        name="mixed_out",
    )(x, total, bias)


def backward_kernel(came, tiles, where_ref, *refs):
    c_refs, refs = refs[:came], refs[came:]
    wo_ref, wd_ref, slope_ref = refs[:3]
    cot_ref, ga_ref, gh_ref = refs[-3:]
    i = pl.program_id(0)
    j, _, busy = pick(where_ref, i, tiles)
    rows = cot_ref.shape[0]
    step = min(ROWS, rows)

    @pl.when(busy & (j == 0))
    def _():
        pick_shard(where_ref, i, tiles, c_refs, cot_ref)
        weight = side_by_side(wo_ref)
        for m in range(0, rows, step):
            ga_ref[m : m + step, :] = dot_nt(cot_ref[m : m + step, :], weight).astype(BF16)

    @pl.when(busy & (j > 0))
    def _():
        weight = side_by_side(wd_ref)
        for m in range(0, rows, step):
            gh_ref[m : m + step, :] = (
                dot_nt(cot_ref[m : m + step, :], weight) * slope_ref[m : m + step, :].astype(F32)
            ).astype(BF16)


def backward_chunk(where, cots, wo, wd, slope, bufs, parts):
    rows, depth = cots[0].shape
    pieces, width, piece = wo.shape
    ff = wd.shape[1]
    tiles = 1 + ff // width

    def at(k):
        def index(i, w):
            j, slot, _ = pick(w, i, tiles)
            return ((0, 0), (0, jnp.maximum(j - 1, 0), 0), (slot, jnp.maximum(j - 1, 0)), (slot, 0))[k]

        return index

    in_specs = [pl.BlockSpec((rows, depth), at(0))] * len(cots) + [
        whole(wo),
        pl.BlockSpec((pieces, width, piece), at(1)),
        pl.BlockSpec((rows, width), at(2)),
    ]
    total = (parts + 1) * rows
    shapes = [(total, depth), (total, width), (total, ff)]
    args = [where, *cots, wo, wd, slope]
    aliases = {}
    if bufs is not None:
        aliases = {len(args) + k: k for k in range(3)}
        args += list(bufs)
        in_specs += [pl.BlockSpec(memory_space=pl.ANY)] * 3
    return pl.pallas_call(
        functools.partial(backward_kernel, len(cots), tiles),
        grid_spec=pltpu.PrefetchScalarGridSpec(
            num_scalar_prefetch=1,
            grid=(len(cots) * tiles,),
            in_specs=in_specs,
            out_specs=[
                pl.BlockSpec((rows, depth), at(3)),
                pl.BlockSpec((rows, width), at(3)),
                pl.BlockSpec((rows, width), at(2)),
            ],
        ),
        out_shape=[jax.ShapeDtypeStruct(s, BF16) for s in shapes],
        input_output_aliases=aliases,
        cost_estimate=cost(2 * rows * depth * (width + ff), 2 * depth * (width + ff)),
        name="backward_chunk",
    )(*args)


def grad_kernel(gq_ref, gk_ref, gv_ref, gh_ref, wq_ref, wu_ref, o_ref):
    step = min(512, gq_ref.shape[0])
    width = gq_ref.shape[1]
    for m in range(0, gq_ref.shape[0], step):
        rs = slice(m, m + step)
        left = jnp.concatenate([r[rs, :] for r in (gq_ref, gk_ref, gv_ref)], axis=1)
        o_ref[rs, :] = (dot_nt(left, wq_ref[...]) + dot_nt(gh_ref[rs, :], wu_ref[...])).astype(BF16)


def grad_normed(gqkv, gh, wq, wu, start, stop):
    count, width = gqkv[0].shape
    ff = gh.shape[1]
    tile = min(256, stop - start)
    first = start // tile
    return pl.pallas_call(
        grad_kernel,
        grid=((stop - start) // tile,),
        in_specs=[once((count, width))] * 3
        + [
            once((count, ff)),
            pl.BlockSpec((tile, wq.shape[1]), lambda j: (first + j, 0)),
            pl.BlockSpec((tile, wu.shape[1]), lambda j: (first + j, 0)),
        ],
        out_specs=pl.BlockSpec((count, tile), lambda j: (0, j)),
        out_shape=jax.ShapeDtypeStruct((count, stop - start), BF16),
        cost_estimate=cost(2 * count * (stop - start) * (3 * width + ff), 4 * count * ff),
        name="grad_normed",
    )(*gqkv, gh, wq, wu)


def put_columns(att_ref, act_ref, cot, o_ref, start, stop, add):
    width = att_ref.shape[1]
    at = start
    while at < stop:
        if at < width:
            end = min(stop, width)
            left = att_ref[:, at:end]
        else:
            end = min(stop, at + 512)
            left = act_ref[:, at - width : end - width]
        rows = slice(at - start, end - start)
        total = dot_tn(left, cot)
        if add is not None:
            total = total + add[0, rows, :].astype(F32)
        o_ref[0, rows, :] = total.astype(BF16)
        at = end


def columns_send_kernel(where_ref, att_ref, act_ref, c_ref, o_ref):
    put_columns(att_ref, act_ref, c_ref[...], o_ref, 0, o_ref.shape[1], None)


def columns_keep_kernel(where_ref, att_ref, act_ref, c_ref, came_ref, a_ref, b_ref):
    half = a_ref.shape[1]
    first = pl.program_id(0) < pl.num_programs(0) // 2

    @pl.when(first)
    def _():
        put_columns(att_ref, act_ref, c_ref[...], a_ref, 0, half, came_ref)

    @pl.when(jnp.logical_not(first))
    def _():
        put_columns(att_ref, act_ref, c_ref[...], b_ref, half, 2 * half, came_ref)


def rows_send_kernel(arrays, where_ref, x_ref, *refs):
    g_refs, o_ref, sum_ref = refs[:arrays], refs[-2], refs[-1]
    x = x_ref[...]
    first = pl.program_id(0) == 0
    start = 0
    for g_ref in g_refs:
        width = g_ref.shape[1]
        step = min(512, width)
        for m in range(0, width, step):
            o_ref[0, :, start + m : start + m + step] = dot_tn(x, g_ref[:, m : m + step]).astype(BF16)

        @pl.when(first)
        def _():
            ones = jnp.ones((8, g_ref.shape[0]), BF16)
            for m in range(0, width, step):
                sum_ref[:, start + m : start + m + step] = dot_nn(ones, g_ref[:, m : m + step])

        start += width


def rows_keep_kernel(arrays, where_ref, x_ref, *refs):
    g_refs, came_ref, a_ref, b_ref = refs[:arrays], *refs[arrays:]
    first = pl.program_id(0) < pl.num_programs(0) // 2
    x = x_ref[...]
    half = a_ref.shape[2]

    def put(o_ref, low):
        start = 0
        for g_ref in g_refs:
            width = g_ref.shape[1]
            at = max(start, low)
            while at < min(start + width, low + half):
                end = min(start + width, low + half, at + 512)
                o_ref[0, :, at - low : end - low] = (
                    dot_tn(x, g_ref[:, at - start : end - start])
                    + came_ref[0, :, at - low : end - low].astype(F32)
                ).astype(BF16)
                at = end
            start += width

    pl.when(first)(lambda: put(a_ref, 0))
    pl.when(jnp.logical_not(first))(lambda: put(b_ref, half))


def once(shape):
    return pl.BlockSpec(shape, lambda *_: (0,) * len(shape), pipeline_mode=pl.Buffered(1))


def column_grads(where, att, act, cot, places, came=None):
    count, width = att.shape
    ff = act.shape[1]
    piece = cot.shape[1] // (2 * places)
    flops = 2 * count * (width + ff) * piece * places
    base = [once((count, width)), once((count, ff)), pl.BlockSpec((count, piece), lambda t, w: (0, w[t]))]
    if came is None:
        return pl.pallas_call(
            columns_send_kernel,
            grid_spec=pltpu.PrefetchScalarGridSpec(
                num_scalar_prefetch=1,
                grid=(places,),
                in_specs=base,
                out_specs=pl.BlockSpec((1, width + ff, piece), lambda t, w: (t, 0, 0)),
            ),
            out_shape=jax.ShapeDtypeStruct((places, width + ff, piece), BF16),
            cost_estimate=cost(flops, 2 * count * (width + ff)),
            name="columns_send",
        )(where, att, act, cot)
    half = (width + ff) // 2
    turns = 2 * places
    return pl.pallas_call(
        columns_keep_kernel,
        grid_spec=pltpu.PrefetchScalarGridSpec(
            num_scalar_prefetch=1,
            grid=(turns,),
            in_specs=base
            + [pl.BlockSpec((1, half, piece), lambda t, w: (w[turns + t], t // places, 0))],
            out_specs=[
                pl.BlockSpec((1, half, piece), lambda t, w: (jnp.minimum(t, places - 1), 0, 0)),
                pl.BlockSpec((1, half, piece), lambda t, w: (jnp.maximum(t - places, 0), 0, 0)),
            ],
        ),
        out_shape=[jax.ShapeDtypeStruct((places, half, piece), BF16)] * 2,
        cost_estimate=cost(flops, 2 * count * (width + ff)),
        name="columns_keep",
    )(where, att, act, cot, came)


def row_grads(where, x, gs, count, places, came=None):
    width = sum(g.shape[1] for g in gs)
    piece = x.shape[1] // (2 * places)
    flops = 2 * count * width * piece * places
    base = [pl.BlockSpec((count, piece), lambda t, w: (0, w[t]))] + [once((count, g.shape[1])) for g in gs]
    if came is None:
        return pl.pallas_call(
            functools.partial(rows_send_kernel, len(gs)),
            grid_spec=pltpu.PrefetchScalarGridSpec(
                num_scalar_prefetch=1,
                grid=(places,),
                in_specs=base,
                out_specs=[
                    pl.BlockSpec((1, piece, width), lambda t, w: (t, 0, 0)),
                    pl.BlockSpec((8, width), lambda t, w: (0, 0)),
                ],
            ),
            out_shape=[
                jax.ShapeDtypeStruct((places, piece, width), BF16),
                jax.ShapeDtypeStruct((8, width), F32),
            ],
            cost_estimate=cost(flops, 2 * count * width),
            name="rows_send",
        )(where, x, *gs)
    half = width // 2
    turns = 2 * places
    return pl.pallas_call(
        functools.partial(rows_keep_kernel, len(gs)),
        grid_spec=pltpu.PrefetchScalarGridSpec(
            num_scalar_prefetch=1,
            grid=(turns,),
            in_specs=base
            + [pl.BlockSpec((1, piece, half), lambda t, w: (w[turns + t], 0, t // places))],
            out_specs=[
                pl.BlockSpec((1, piece, half), lambda t, w: (jnp.minimum(t, places - 1), 0, 0)),
                pl.BlockSpec((1, piece, half), lambda t, w: (jnp.maximum(t - places, 0), 0, 0)),
            ],
        ),
        out_shape=[jax.ShapeDtypeStruct((places, piece, half), BF16)] * 2,
        cost_estimate=cost(flops, 2 * count * width),
        name="rows_keep",
    )(where, x, *gs, came)


def after(value, *marks):
    return lax.optimization_barrier((value, *marks))[0]


def swap(x, bit):
    size = lax.axis_size("dp")
    return lax.ppermute(x, "dp", [(i, i ^ (1 << bit)) for i in range(size)])


def halve(xs, orders, k, sent=None):
    kept = []
    for x, y, bits in zip(xs, sent or xs, orders):
        rest = x.shape[0] // 2
        came = swap(y[rest:], bits[k])
        total = x[:rest].astype(F32) + came.astype(F32)
        kept.append(total if k == len(bits) - 1 else total.astype(BF16))
    return kept


def small_sum_kernel(phases, x_ref, o_ref, sent_ref, came_ref, send_sems, came_sems):
    barrier = pltpu.get_barrier_semaphore()

    def partner(axis, bit):
        return {axis: lax.axis_index(axis) ^ (1 << bit)}

    for axis, bit, _ in phases:
        pl.semaphore_signal(
            barrier, inc=1, device_id=partner(axis, bit), device_id_type=pl.DeviceIdType.MESH
        )
    pl.semaphore_wait(barrier, len(phases))
    sent_ref[0] = x_ref[...]
    for k, (axis, bit, rows) in enumerate(phases):
        span = pl.ds(0, rows)
        copy = pltpu.make_async_remote_copy(
            src_ref=sent_ref.at[k, span],
            dst_ref=came_ref.at[k, span],
            send_sem=send_sems.at[k],
            recv_sem=came_sems.at[k],
            device_id=partner(axis, bit),
            device_id_type=pl.DeviceIdType.MESH,
        )
        copy.start()
        copy.wait()
        total = sent_ref[k, 0:rows] + came_ref[k, 0:rows]
        if k == len(phases) - 1:
            o_ref[...] = sent_ref[k]
            o_ref[0:rows] = total
        else:
            sent_ref[k + 1] = sent_ref[k]
            sent_ref[k + 1, 0:rows] = total


def small_sums(x, common):
    rows = x.shape[0]
    phases = []
    for axis, height in (("dp", rows), ("tensor", common)):
        for bit in range(lax.axis_size(axis).bit_length() - 1):
            phases.append((axis, bit, height))
    return pl.pallas_call(
        functools.partial(small_sum_kernel, phases),
        in_specs=[pl.BlockSpec(memory_space=pltpu.VMEM)],
        out_specs=pl.BlockSpec(memory_space=pltpu.VMEM),
        out_shape=jax.ShapeDtypeStruct(x.shape, F32),
        scratch_shapes=[
            pltpu.VMEM((len(phases), *x.shape), F32),
            pltpu.VMEM((len(phases), *x.shape), F32),
            pltpu.SemaphoreType.DMA((len(phases),)),
            pltpu.SemaphoreType.DMA((len(phases),)),
        ],
        compiler_params=pltpu.CompilerParams(collective_id=0, has_side_effects=True),
        name="small_sums",
    )(x)


def local(
    tokens, segments, ln_gain, ln_shift, qkv_weight, qkv_bias, out_weight, out_bias,
    fc1_weight, fc1_bias, fc2_weight, fc2_bias, cotangent,
):
    n = lax.axis_size("tensor")
    pieces = lax.axis_size("dp")
    me = lax.axis_index("tensor")
    rows, depth = tokens.shape
    count = segments.shape[1]
    width = qkv_weight.shape[2]

    def shift(x, pairs):
        return lax.ppermute(x, "tensor", pairs)

    def turns(step):
        left, right = me - step, me + step
        has_left, has_right = left >= 0, right < n
        one = jnp.where(has_left, left, right)
        last = jnp.where(has_right, right, jnp.where(has_left, left, n))
        busy = has_left.astype(jnp.int32) + has_right.astype(jnp.int32)
        values = [one, jnp.where(has_left, 0, 1), right, 1, busy, last]
        return jnp.stack([jnp.asarray(v, jnp.int32) for v in values])

    def present_shards(steps):
        offsets = [0] + [d * s for s in range(1, steps + 1) for d in (-1, 1)]
        shards = jnp.stack([me + d for d in offsets])
        present = (shards >= 0) & (shards < n)
        order = jnp.sort(jnp.where(present, shards, n))
        order = jnp.concatenate([order, jnp.full((n,), n, order.dtype)])[:n]
        return jnp.concatenate(
            [
                jnp.sum(present.astype(jnp.int32))[None],
                order,
                jnp.stack([jnp.clip(shards, 0, n - 1), present.astype(jnp.int32)], axis=1).reshape(-1),
            ]
        ).astype(jnp.int32)

    early = present_shards(n - 2)
    late = turns(n - 1)

    own_normed = norm(tokens, ln_gain[None], ln_shift[None])

    w_qkv = lax.all_gather(qkv_weight.reshape(-1, 3 * width), "dp", axis=0, tiled=True)
    w_up = lax.all_gather(fc1_weight, "dp", axis=0, tiled=True)
    w_out = lax.all_gather(out_weight, "dp", axis=0)
    w_down = lax.all_gather(fc2_weight, "dp", axis=0)

    segment_row = segments[0]
    starts = seq_starts(segment_row)
    tables = rotary_tables(jnp.arange(count, dtype=jnp.int32) - starts)
    first = starts[::BLOCK] // BLOCK
    segc, segr = segment_row[:, None], segment_row[None, :]

    bias_qkv, bias_up = qkv_bias.reshape(1, -1), fc1_bias[None]
    def line_step(pair, s):
        right, left = pair
        return [
            shift(right, [(i, i + 1) for i in range(s - 1, n - 1)]),
            shift(left, [(i, i - 1) for i in range(1, n - s + 1)]),
        ]

    def line_sum(x):
        return lax.psum_scatter(x, "tensor", scatter_dimension=0, tiled=True)

    def flat(pairs):
        return [x for pair in pairs for x in pair]

    project = (w_qkv, w_up, bias_qkv, bias_up, tables)
    normed_in = [line_step([own_normed] * 2, 1)]
    normed, qkv = queries_early(
        after(present_shards(1), first, segc), [own_normed] + normed_in[0], w_qkv, bias_qkv, tables, n
    )
    for s in range(2, n):
        normed_in.append(line_step(after(tuple(normed_in[-1]), qkv) if s == 3 else normed_in[-1], s))
    act, slope = units_early(
        after(early, qkv), [own_normed] + flat(normed_in[:-1]), w_up, bias_up, width, n
    )
    normed, qkv = after((normed, qkv), act)
    for s in range(2, n - 1):
        normed, qkv = queries_chunk(turns(s), normed_in[s - 1], w_qkv, bias_qkv, tables, (normed, qkv), n)
    cot_in = [line_step([after(cotangent, *normed_in[-1], qkv)] * 2, 1)]
    normed, qkv, act, slope = forward_chunk(late, normed_in[-1], *project, (normed, qkv, act, slope), n)

    att, lse = attend(qkv, segc, segr, first, 0, 1, None)
    cot_in.append(line_step(after(tuple(cot_in[-1]), att), 2))
    part = mix(att, act, w_out, w_down)
    for s in range(3, n):
        cot_in.append(line_step(after(tuple(cot_in[-1]), part), s))
    bufs = backward_early(after(early, part), [cotangent] + flat(cot_in[:-1]), w_out, w_down, slope, n)
    block_sum = line_sum(after(part, bufs[2], *cot_in[-1]))
    cot, grad_att, grad_hid = backward_chunk(late, cot_in[-1], w_out, w_down, slope, bufs, n)
    bits = [b for b in range(1, pieces.bit_length() - 1)]
    places = pieces // 2
    mine = lax.axis_index("dp")

    def place_of(r, order):
        return sum(((r >> (len(order) - 1 - k)) & 1) << bit for k, bit in enumerate(order))

    kept = [place_of(r, bits) for r in range(places)] + [place_of(r, bits[::-1]) for r in range(places)]
    send_where = mine ^ jnp.array([2 * q + 1 for q in range(places)], jnp.int32)
    keep_where = jnp.concatenate([mine ^ jnp.array(kept, jnp.int32), jnp.array(kept, jnp.int32) // 2])

    orders = (bits, bits[::-1])

    def finish(pair, axis, *marks):
        for k in range(1, len(bits)):
            pair = halve([after(half, *marks) for half in pair], orders, k, pair)
        return jnp.concatenate([half[0].astype(F32) for half in pair], axis=axis)

    col_send = column_grads(send_where, att, act, cot, places)
    up_send, up_sum = row_grads(send_where, normed, [after(grad_hid, col_send)], count, places)
    grad_qkv = attend_back(
        qkv, after(grad_att, up_sum), att, lse, segc, segr, first, tables, 0, 1, None
    )
    col_came, up_came = swap(col_send, 0), swap(up_send, 0)
    part = grad_normed(grad_qkv, after(grad_hid, col_came, up_came), w_qkv, w_up, 0, depth)
    grad_sum = line_sum(after(part, block_sum))
    col_pair = column_grads(keep_where, att, act, after(cot, part), places, col_came)
    qkv_send, qkv_sum = row_grads(send_where, normed, after(tuple(grad_qkv), col_pair[0]), count, places)
    up_pair = row_grads(
        keep_where, normed, [after(grad_hid, qkv_sum)], count, places, up_came
    )
    col_pair = halve([after(c, up_pair[0]) for c in col_pair], orders, 0, col_pair)
    qkv_pair = row_grads(
        keep_where, after(normed, *col_pair), grad_qkv, count, places, swap(qkv_send, 0)
    )
    up_pair = halve([after(u, qkv_pair[0]) for u in up_pair], orders, 0, up_pair)
    qkv_kept = qkv_pair[0]
    qkv_pair = halve(qkv_pair, orders, 0)
    mixed = mixed_out(tokens, after(block_sum, *qkv_pair), (out_bias + fc2_bias)[None])
    input_grad, sums = norm_back(tokens, after(cotangent, mixed), [grad_sum], ln_gain[None])
    common = 3 * depth // 128
    pack = jnp.concatenate([a.reshape(-1, 128) for a in (sums[:3], up_sum[0], qkv_sum[0])])
    pack = jnp.pad(pack, ((0, -pack.shape[0] % 8), (0, 0)))
    pack = small_sums(pack, common)
    col_out, up_out, qkv_out = finish(col_pair, 0, qkv_kept), finish(up_pair, 1, *qkv_pair), finish(qkv_pair, 1)
    total = pack[:common].reshape(3, depth)
    ff_rows = up_sum.shape[1] // 128
    up_bias_grad = pack[common : common + ff_rows].reshape(-1)
    qkv_bias_grad = pack[common + ff_rows : common + ff_rows + 3 * width // 128].reshape(3, width)
    return (
        mixed,
        input_grad,
        qkv_out.reshape(-1, 3, width),
        qkv_bias_grad,
        col_out[:width],
        total[2],
        up_out,
        up_bias_grad,
        col_out[width:],
        total[2],
        total[0],
        total[1],
    )


def solution(mesh):
    in_specs = (
        P(("dp", "tensor"), None),
        P("dp", None),
        P(),
        P(),
        P("dp", None, "tensor"),
        P(None, "tensor"),
        P("tensor", "dp"),
        P(),
        P("dp", "tensor"),
        P("tensor"),
        P("tensor", "dp"),
        P(),
        P(("dp", "tensor"), None),
    )
    out_specs = (
        P(("dp", "tensor"), None),
        P(("dp", "tensor"), None),
        P("dp", None, "tensor"),
        P(None, "tensor"),
        P("tensor", "dp"),
        P(),
        P("dp", "tensor"),
        P("tensor"),
        P("tensor", "dp"),
        P(),
        P(),
        P(),
    )
    return jax.shard_map(local, mesh=mesh, in_specs=in_specs, out_specs=out_specs, check_vma=False)
```

time: 1640 us -> 689 us (0.42)
  matrix products: 701 us -> 0 us
  Pallas kernels: 0 us -> 422 us
  waiting for transfers between devices: 475 us -> 134 us
  other arithmetic: 221 us -> 27.4 us
  local copies, waits for them, and re-layouts: 141 us -> 28 us
  blocking collectives: 66 us -> 0 us
  starting transfers between devices: 0.48 us -> 55.8 us
    dot_general x40 -> x0, matrix products: 701 us -> none  [the longest x8 161 us: one_block(): jnp.einsum('qhd,khd->hqk', query_block, key_rows, preferred_element_type=...]
    pallas_call x0 -> x20, Pallas kernels: none -> 422 us  [the longest x1 60.5 us: attend_back(): pl.pallas_call(attend_back_kernel, grid_spec=pltpu.PrefetchScalarGridSpec...]
    reduce_scatter x6 -> x2, waiting for transfers between devices: 290 us -> 0.02 us  [line_sum(): return lax.psum_scatter(x, 'tensor', scatter_dimension=0, tiled=True)]
    all_gather x6 -> x4, waiting for transfers between devices: 181 us -> 0.04 us  [the longest x1 0.02 us: local(): w_out = lax.all_gather(out_weight, 'dp', axis=0)]
    ppermute x0 -> x27, waiting for transfers between devices: none -> 132 us  [the longest x12 103 us: shift(): return lax.ppermute(x, 'tensor', pairs)]
    convert_element_type x10 -> x9, other arithmetic: 123 us -> 7.55 us  [the longest x6 7.46 us: halve(): kept.append(total if k == len(bits) - 1 else total.astype(BF16))]
    dynamic_update_slice x8 -> x0, local copies, waits for them, and re-layouts: 88.3 us -> none  [attend(): lax.map(one_block, jnp.arange(group_rows // block_rows, dtype=jnp.int32))]
    reduce_sum x9 -> x2, other arithmetic: 79.1 us -> 1.37 us  [present_shards(): jnp.sum(present.astype(jnp.int32))[None]]
  transfers between devices with their start and end apart: 12 -> 33, of which waited for: 5 -> 12; matrix products, arithmetic and copies ran while one was open for 65% -> 7% of each run, Pallas kernels for 0% -> 59%
where the time goes in v1:
time: 689 us; the launch traced here: 682 us
  Pallas kernels  422 us (61%)
  waiting for transfers between devices  134 us (19%)
  starting transfers between devices  55.8 us (8%)
  local copies, waits for them, and re-layouts  28 us (4%)
  other arithmetic  27.4 us (4%)
  between operations  15.2 us (2%)
    ppermute x12, waiting for transfers between devices, shift(): return lax.ppermute(x, 'tensor', pairs)  103 us
    pallas_call x1, Pallas kernels, attend_back(): pl.pallas_call(attend_back_kernel, grid_spec=pltpu.PrefetchScalarGridSpec...  60.5 us
    pallas_call x1, Pallas kernels, attend(): pl.pallas_call(attend_kernel, grid_spec=pltpu.PrefetchScalarGridSpec(num_...  42 us
    pallas_call x1, Pallas kernels, grad_normed(): pl.pallas_call(grad_kernel, grid=((stop - start) // tile,), in_specs=[onc...  39.2 us
    pallas_call x2, Pallas kernels, row_grads(): pl.pallas_call(functools.partial(rows_keep_kernel, len(gs)), grid_spec=pl...  32.7 us
    pallas_call x2, Pallas kernels, row_grads(): pl.pallas_call(functools.partial(rows_send_kernel, len(gs)), grid_spec=pl...  31 us
    ppermute x12, starting transfers between devices, shift(): return lax.ppermute(x, 'tensor', pairs)  30.5 us
    pallas_call x1, Pallas kernels, backward_early(): pl.pallas_call(functools.partial(backward_early_kernel, len(cots), parts)...  28.9 us
  transfers between devices with their start and end apart: 33, of which 12 were waited for; matrix products, arithmetic and copies ran while one was open for 7% of the time, Pallas kernels for 59%

profile of v1, /device:TPU:0, one launch (start us, length us, event | category | flops | bytes accessed | tf_op | source)
XLA Modules:
  0.0 682.3 jit_solution(3957219748247253107)
XLA Ops:
  11.9 3.7 norm.1.refs_0_
  15.7 5.0 collective-permute-start
  22.3 43.5 %collective-permute-done.refs_1_ = bf16[512,2048]{1,0:T(8,128)(2,1)S(1)} collective-permute-done((bf16[512,2048]{1,0:T(8,128)(2,1)}, bf16[512,2048]{1,0:T(8,128)(2,1)S(1)}, u32[]{:S(2)}, u32[]{:S(2)}) %collective-permute-start) | collective-permute-done | bytes 2097184 | tf_op jit(solution)/shard_map/ppermute | solution.py:1170
  76.1 5.8 fusion
  81.9 15.8 %queries_early.1 = (bf16[2560,2048]{1,0:T(8,128)(2,1)}, bf16[2560,1536]{1,0:T(8,128)(2,1)}) custom-call(s32[11]{0:T(128)} %pad_add_fusion.4.where_ref, bf16[512,2048]{1,0:T(8,128)(2,1)} %norm.1.refs_0_, bf16[512,2048]{1,0:T(8,128)(2,1)} %copy-done, bf16[512,2048]{1,0:T(8,128)(2,1)} %collective-permute-done.2.refs_2_, ...), custom_call_target="tpu_custom_call" | custom-call | flops 644245120 | bytes 314572 | tf_op jit(solution)/shard_map/queries_early/pallas_call | solution.py:415
  97.8 22.0 %collective-permute-done.3.refs_4_.refs_1_ = bf16[512,2048]{1,0:T(8,128)(2,1)} collective-permute-done((bf16[512,2048]{1,0:T(8,128)(2,1)}, bf16[512,2048]{1,0:T(8,128)(2,1)}, u32[]{:S(2)}, u32[]{:S(2)}) %collective-permute-start.3) | collective-permute-done | bytes 2097184 | tf_op jit(solution)/shard_map/ppermute | solution.py:1170
  126.9 28.7 %units_early.1 = (bf16[2560,2048]{1,0:T(8,128)(2,1)}, bf16[2560,2048]{1,0:T(8,128)(2,1)}) custom-call(s32[15]{0:T(128)} %pad_add_fusion.5.where_ref, bf16[512,2048]{1,0:T(8,128)(2,1)} %norm.1.refs_0_, bf16[512,2048]{1,0:T(8,128)(2,1)} %copy-done, bf16[512,2048]{1,0:T(8,128)(2,1)} %collective-permute-done.2.refs_2_, ...), custom_call_target="tpu_custom_call" | custom-call | flops 858993472 | bytes 419430 | tf_op jit(solution)/shard_map/units_early/pallas_call | solution.py:443
  155.6 10.8 %queries_chunk.1 = (bf16[2560,2048]{1,0:T(8,128)(2,1)}, bf16[2560,1536]{1,0:T(8,128)(2,1)}) custom-call(s32[6]{0:T(128)} %stack.102.where_ref, bf16[512,2048]{1,0:T(8,128)(2,1)} %collective-permute-done.1.refs_3_.refs_0_, bf16[512,2048]{1,0:T(8,128)(2,1)} %collective-permute-done.3.refs_4_.refs_1_, ...), custom_call_target="tpu_custom_call", output_to_operand_aliasing={{0}: (8, {}), {1}: (9, {})} | custom-call | flops 161061280 | bytes 314572 | tf_op jit(solution)/shard_map/queries_chunk/pallas_call | solution.py:265
  169.7 11.7 %collective-permute-start.6 = (bf16[512,2048]{1,0:T(8,128)(2,1)S(1)}, bf16[512,2048]{1,0:T(8,128)(2,1)}, u32[]{:S(2)}, u32[]{:S(2)}) collective-permute-start(bf16[512,2048]{1,0:T(8,128)(2,1)S(1)} %copy-done.1), channel_id=1, source_target_pairs={{0,1},{1,2},{2,3},{4,5},{5,6},{6,7},{8,9},{9,10},{10,11},{12,13},{... | collective-permute-start | bytes 6291464 | tf_op jit(solution)/shard_map/ppermute | solution.py:1170
  185.1 21.1 %forward_chunk.1 = (bf16[2560,2048]{1,0:T(8,128)(2,1)}, bf16[2560,1536]{1,0:T(8,128)(2,1)}, bf16[2560,2048]{1,0:T(8,128)(2,1)}, bf16[2560,2048]{1,0:T(8,128)(2,1)}) custom-call(s32[6]{0:T(128)} %stack.87.where_ref, bf16[512,2048]{1,0:T(8,128)(2,1)} %collective-permute-done.4.refs_0_, ...), custom_call_target="tpu_custom_call", output_to_operand_aliasing={{0}: (10, {}), {1}: (11, {}), {2}: (12, {}), {3}: (13, {})} | custom-call | flops 375809632 | bytes 734003 | tf_op jit(solution)/shard_map/forward_chunk/pallas_call | solution.py:322
  206.3 42.0 %attend.1 = (bf16[2048,512]{1,0:T(8,128)(2,1)}, f32[4,8,2048]{2,1,0:T(8,128)}) custom-call(s32[8]{0:T(128)} %and_select_fusion.2.first_ref, bf16[2560,1536]{1,0:T(8,128)(2,1)} %get-tuple-element.96.q_ref.k_ref.v_ref, bf16[2560,1536]{1,0:T(8,128)(2,1)} %get-tuple-element.96.q_ref.k_ref.v_ref, bf16[2560,1536]{1,0:T(8,128)(2,1)} %get-tuple-element.96.q_ref.k_ref.v_ref, ...), custom_call_target="tpu_custom_call" | custom-call | flops 1500000000 | bytes 419430 | tf_op jit(solution)/shard_map/attend/pallas_call | solution.py:607
  250.4 28.6 %mix.1 = bf16[2048,2048]{1,0:T(8,128)(2,1)} custom-call(bf16[2048,512]{1,0:T(8,128)(2,1)} %get-tuple-element.97.att_ref.o_ref, bf16[2560,2048]{1,0:T(8,128)(2,1)} %get-tuple-element.98.act_ref, bf16[8,512,256]{2,1,0:T(8,128)(2,1)} %bitcast.68, bf16[8,2048,256]{2,1,0:T(8,128)(2,1)} %bitcast.65), custom_call_target="tpu_custom_call" | custom-call | flops 1073741824 | bytes 838860 | tf_op jit(solution)/shard_map/mix/pallas_call | solution.py:783
  280.4 16.0 %collective-permute-done.9.refs_4_ = bf16[512,2048]{1,0:T(8,128)(2,1)} collective-permute-done((bf16[512,2048]{1,0:T(8,128)(2,1)}, bf16[512,2048]{1,0:T(8,128)(2,1)}, u32[]{:S(2)}, u32[]{:S(2)}) %collective-permute-start.9) | collective-permute-done | bytes 2097184 | tf_op jit(solution)/shard_map/ppermute | solution.py:1170
  298.5 28.9 %backward_early.1 = (bf16[2560,2048]{1,0:T(8,128)(2,1)}, bf16[2560,512]{1,0:T(8,128)(2,1)}, bf16[2560,2048]{1,0:T(8,128)(2,1)}) custom-call(s32[15]{0:T(128)} %pad_add_fusion.5.where_ref, bf16[512,2048]{1,0:T(8,128)(2,1)} %cot_ref, bf16[512,2048]{1,0:T(8,128)(2,1)} %collective-permute-done.6.refs_1_, bf16[512,2048]{1,0:T(8,128)(2,1)} %collective-permute-done.7.refs_2_, ...), custom_call_target="tpu_custom_call" | custom-call | flops 1073741824 | bytes 524288 | tf_op jit(solution)/shard_map/backward_early/pallas_call | solution.py:510
  327.5 16.1 %collective-permute-done.11.refs_1_ = bf16[512,2048]{1,0:T(8,128)(2,1)} collective-permute-done((bf16[512,2048]{1,0:T(8,128)(2,1)}, bf16[512,2048]{1,0:T(8,128)(2,1)}, u32[]{:S(2)}, u32[]{:S(2)}) %collective-permute-start.11) | collective-permute-done | bytes 2097184 | tf_op jit(solution)/shard_map/ppermute | solution.py:1170
  344.8 14.6 %backward_chunk.1 = (bf16[2560,2048]{1,0:T(8,128)(2,1)}, bf16[2560,512]{1,0:T(8,128)(2,1)}, bf16[2560,2048]{1,0:T(8,128)(2,1)}) custom-call(s32[6]{0:T(128)} %stack.87.where_ref, bf16[512,2048]{1,0:T(8,128)(2,1)} %copy-done.6, bf16[512,2048]{1,0:T(8,128)(2,1)} %collective-permute-done.11.refs_1_, ...), custom_call_target="tpu_custom_call", output_to_operand_aliasing={{0}: (6, {}), {1}: (7, {}), {2}: (8, {})} | custom-call | flops 268435456 | bytes 524288 | tf_op jit(solution)/shard_map/backward_chunk/pallas_call | solution.py:869
  359.3 18.0 %columns_send.1 = bf16[4,2560,256]{2,1,0:T(8,128)(2,1)} custom-call(s32[4]{0:T(128)} %broadcast_xor_fusion.where_ref, bf16[2048,512]{1,0:T(8,128)(2,1)} %get-tuple-element.97.att_ref.o_ref, bf16[2560,2048]{1,0:T(8,128)(2,1)} %get-tuple-element.98.act_ref, bf16[2560,2048]{1,0:T(8,128)(2,1)} %get-tuple-element.123.c_ref), custom_call_target="tpu_custom_call" | custom-call | flops 536870912 | bytes 524288 | tf_op jit(solution)/shard_map/columns_send/pallas_call | solution.py:1008
  377.3 16.2 %rows_send.2 = (bf16[4,256,2048]{2,1,0:T(8,128)(2,1)}, f32[8,2048]{1,0:T(8,128)}) custom-call(s32[4]{0:T(128)} %broadcast_xor_fusion.where_ref, bf16[2560,2048]{1,0:T(8,128)(2,1)} %get-tuple-element.134.x_ref, bf16[2560,2048]{1,0:T(8,128)(2,1)} %get-tuple-element.129.refs_0_.gh_ref), custom_call_target="tpu_custom_call" | custom-call | flops 429496736 | bytes 419430 | tf_op jit(solution)/shard_map/rows_send/pallas_call | solution.py:1046
  394.0 60.5 %attend_back.1 = (bf16[2048,512]{1,0:T(8,128)(2,1)}, bf16[2048,512]{1,0:T(8,128)(2,1)}, bf16[2048,512]{1,0:T(8,128)(2,1)}) custom-call(s32[8]{0:T(128)} %and_select_fusion.2.first_ref, bf16[2560,1536]{1,0:T(8,128)(2,1)} %get-tuple-element.96.q_ref.k_ref.v_ref, bf16[2560,1536]{1,0:T(8,128)(2,1)} %get-tuple-element.96.q_ref.k_ref.v_ref, ...), custom_call_target="tpu_custom_call" | custom-call | flops 2200000000 | bytes 1048576 | tf_op jit(solution)/shard_map/attend_back/pallas_call | solution.py:734
  454.6 39.2 %grad_normed.1 = bf16[2048,2048]{1,0:T(8,128)(2,1)} custom-call(bf16[2048,512]{1,0:T(8,128)(2,1)} %get-tuple-element.125.gq_ref.refs_0_, bf16[2048,512]{1,0:T(8,128)(2,1)} %get-tuple-element.126.gk_ref.refs_1_, bf16[2048,512]{1,0:T(8,128)(2,1)} %get-tuple-element.127.gv_ref.refs_2_, bf16[2560,2048]{1,0:T(8,128)(2,1)} %get-tuple-element.129.refs_0_.gh_ref, ...), custom_call_target="tpu_custom_call" | custom-call | flops 1503238528 | bytes 838860 | tf_op jit(solution)/shard_map/grad_normed/pallas_call | solution.py:902
  495.1 20.2 %columns_keep.1 = (bf16[4,1280,256]{2,1,0:T(8,128)(2,1)}, bf16[4,1280,256]{2,1,0:T(8,128)(2,1)}) custom-call(s32[16]{0:T(128)} %pad_add_fusion.6.where_ref, bf16[2048,512]{1,0:T(8,128)(2,1)} %get-tuple-element.97.att_ref.o_ref, bf16[2560,2048]{1,0:T(8,128)(2,1)} %get-tuple-element.98.act_ref, bf16[2560,2048]{1,0:T(8,128)(2,1)} %get-tuple-element.123.c_ref, ...), custom_call_target="tpu_custom_call" | custom-call | flops 536870912 | bytes 524288 | tf_op jit(solution)/shard_map/columns_keep/pallas_call | solution.py:1022
  515.3 14.8 %rows_send.3 = (bf16[4,256,1536]{2,1,0:T(8,128)(2,1)}, f32[8,1536]{1,0:T(8,128)}) custom-call(s32[4]{0:T(128)} %broadcast_xor_fusion.where_ref, bf16[2560,2048]{1,0:T(8,128)(2,1)} %get-tuple-element.134.x_ref, bf16[2048,512]{1,0:T(8,128)(2,1)} %get-tuple-element.125.gq_ref.refs_0_, bf16[2048,512]{1,0:T(8,128)(2,1)} %get-tuple-element.126.gk_ref.refs_1_, ...), custom_call_target="tpu_custom_call" | custom-call | flops 322122560 | bytes 314572 | tf_op jit(solution)/shard_map/rows_send/pallas_call | solution.py:1046
  533.4 5.9 collective-permute-start.15
  540.7 17.3 %rows_keep.2 = (bf16[4,256,1024]{2,1,0:T(8,128)(2,1)}, bf16[4,256,1024]{2,1,0:T(8,128)(2,1)}) custom-call(s32[16]{0:T(128)} %pad_add_fusion.6.where_ref, bf16[2560,2048]{1,0:T(8,128)(2,1)} %get-tuple-element.134.x_ref, bf16[2560,2048]{1,0:T(8,128)(2,1)} %get-tuple-element.129.refs_0_.gh_ref, bf16[4,256,2048]{2,1,0:T(8,128)(2,1)} %collective-permute-done.13.refs_1_), custom_call_target="tpu_custom_call" | custom-call | flops 429496736 | bytes 419430 | tf_op jit(solution)/shard_map/rows_keep/pallas_call | solution.py:1066
  568.5 5.3 collective-permute-start.21
  576.5 15.4 %rows_keep.3 = (bf16[4,256,768]{2,1,0:T(8,128)(2,1)}, bf16[4,256,768]{2,1,0:T(8,128)(2,1)}) custom-call(s32[16]{0:T(128)} %pad_add_fusion.6.where_ref, bf16[2560,2048]{1,0:T(8,128)(2,1)} %get-tuple-element.134.x_ref, bf16[2048,512]{1,0:T(8,128)(2,1)} %get-tuple-element.125.gq_ref.refs_0_, bf16[2048,512]{1,0:T(8,128)(2,1)} %get-tuple-element.126.gk_ref.refs_1_, ...), custom_call_target="tpu_custom_call" | custom-call | flops 322122560 | bytes 314572 | tf_op jit(solution)/shard_map/rows_keep/pallas_call | solution.py:1066
  600.2 5.0 collective-permute-done.21
  611.2 10.7 %collective-permute-done.18 = bf16[2,256,768]{2,1,0:T(8,128)(2,1)S(1)} collective-permute-done((bf16[2,256,768]{2,1,0:T(8,128)(2,1)S(1)}, bf16[2,256,768]{2,1,0:T(8,128)(2,1)S(1)}, u32[]{:S(2)}, u32[]{:S(2)}) %collective-permute-start.18) | collective-permute-done | bytes 786464 | tf_op jit(solution)/shard_map/ppermute | solution.py:1090
  626.9 4.2 collective-permute-done.25
  634.8 4.5 collective-permute-done.20
  647.4 7.0 %norm_back.1 = (bf16[512,2048]{1,0:T(8,128)(2,1)}, f32[8,2048]{1,0:T(8,128)}) custom-call(bf16[512,2048]{1,0:T(8,128)(2,1)} %x_ref.5, bf16[512,2048]{1,0:T(8,128)(2,1)} %cot_ref, bf16[512,2048]{1,0:T(8,128)(2,1)} %reduce-scatter.5.cloned.1.call-done.refs_0_, f32[1,2048]{1,0:T(1,128)} %bitcast.80), custom_call_target="tpu_custom_call" | custom-call | flops 1048576 | bytes 629145 | tf_op jit(solution)/shard_map/norm_back/pallas_call | solution.py:127
  655.9 15.8 %small_sums.1 = f32[80,128]{1,0:T(8,128)} custom-call(f32[80,128]{1,0:T(8,128)} %select_maximum_fusion.x_ref), custom_call_target="tpu_custom_call" | custom-call | tf_op jit(solution)/shard_map/small_sums/pallas_call | solution.py:1142
  (184 shorter events, 92.5 us)
Async XLA Ops:
  7.2 74.7 %all-gather.7.cloned.1.call-start = ((), (), s32[]{:S(2)}) async-start(), calls=%async_computation.2 | async-start | bytes 7077888 | tf_op jit(solution)/shard_map/all_gather | solution.py:1200
  9.8 117.1 %all-gather.9.cloned.1.call-start = ((), (), s32[]{:S(2)}) async-start(), calls=%async_computation.3 | async-start | bytes 9437184 | tf_op jit(solution)/shard_map/all_gather | solution.py:1201
  10.6 239.8 %all-gather.11.cloned.1.call-start = ((), (), s32[]{:S(2)}) async-start(), calls=%async_computation.6 | async-start | bytes 2359296 | tf_op jit(solution)/shard_map/all_gather | solution.py:1202
  11.3 239.1 %all-gather.13.cloned.1.call-start = ((), (), s32[]{:S(2)}) async-start(), calls=%async_computation.7 | async-start | bytes 9437184 | tf_op jit(solution)/shard_map/all_gather | solution.py:1203
  11.9 482.0 %reduce-scatter.3.cloned.1.call-start = ((), (), s32[]{:S(2)}) async-start(), calls=%async_computation.4 | async-start | bytes 10485760 | tf_op jit(solution)/shard_map/reduce_scatter | solution.py:1220
  15.7 50.1 %collective-permute-start = (bf16[512,2048]{1,0:T(8,128)(2,1)}, bf16[512,2048]{1,0:T(8,128)(2,1)S(1)}, u32[]{:S(2)}, u32[]{:S(2)}) collective-permute-start(bf16[512,2048]{1,0:T(8,128)(2,1)} %norm.1.refs_0_), channel_id=1, source_target_pairs={{0,1},{1,2},{2,3},{4,5},{5,6},{6,7},{8,9},{9,10},{10,11},{12,13},{... | collective-permute-start | bytes 6291464 | tf_op jit(solution)/shard_map/ppermute | solution.py:1170
  20.7 49.3 %collective-permute-start.2 = (bf16[512,2048]{1,0:T(8,128)(2,1)}, bf16[512,2048]{1,0:T(8,128)(2,1)}, u32[]{:S(2)}, u32[]{:S(2)}) collective-permute-start(bf16[512,2048]{1,0:T(8,128)(2,1)} %norm.1.refs_0_), channel_id=1, source_target_pairs={{1,0},{2,1},{3,2},{5,4},{6,5},{7,6},{9,8},{10,9},{11,10},{13,12},{... | collective-permute-start | bytes 6291464 | tf_op jit(solution)/shard_map/ppermute | solution.py:1170
  65.8 32.0 %collective-permute-start.1 = (bf16[512,2048]{1,0:T(8,128)(2,1)S(1)}, bf16[512,2048]{1,0:T(8,128)(2,1)}, u32[]{:S(2)}, u32[]{:S(2)}) collective-permute-start(bf16[512,2048]{1,0:T(8,128)(2,1)S(1)} %collective-permute-done.refs_1_), channel_id=1, source_target_pairs={{1,2},{2,3},{5,6},{6,7},{9,10},{10,11},{13,14},{14,15},{17,18},{18... | collective-permute-start | bytes 6291464 | tf_op jit(solution)/shard_map/ppermute | solution.py:1170
  70.0 49.7 %collective-permute-start.3 = (bf16[512,2048]{1,0:T(8,128)(2,1)}, bf16[512,2048]{1,0:T(8,128)(2,1)}, u32[]{:S(2)}, u32[]{:S(2)}) collective-permute-start(bf16[512,2048]{1,0:T(8,128)(2,1)} %collective-permute-done.2.refs_2_), channel_id=1, source_target_pairs={{1,0},{2,1},{5,4},{6,5},{9,8},{10,9},{13,12},{14,13},{17,16},{18,1... | collective-permute-start | bytes 6291464 | tf_op jit(solution)/shard_map/ppermute | solution.py:1170
  119.8 46.6 %collective-permute-start.4 = (bf16[512,2048]{1,0:T(8,128)(2,1)}, bf16[512,2048]{1,0:T(8,128)(2,1)}, u32[]{:S(2)}, u32[]{:S(2)}) collective-permute-start(bf16[512,2048]{1,0:T(8,128)(2,1)} %collective-permute-done.1.refs_3_.refs_0_), channel_id=1, source_target_pairs={{2,3},{6,7},{10,11},{14,15},{18,19},{22,23},{26,27},{30,31}} | collective-permute-start | bytes 6291464 | tf_op jit(solution)/shard_map/ppermute | solution.py:1170
  121.8 47.9 %collective-permute-start.5 = (bf16[512,2048]{1,0:T(8,128)(2,1)}, bf16[512,2048]{1,0:T(8,128)(2,1)}, u32[]{:S(2)}, u32[]{:S(2)}) collective-permute-start(bf16[512,2048]{1,0:T(8,128)(2,1)} %collective-permute-done.3.refs_4_.refs_1_), channel_id=1, source_target_pairs={{1,0},{5,4},{9,8},{13,12},{17,16},{21,20},{25,24},{29,28}} | collective-permute-start | bytes 6291464 | tf_op jit(solution)/shard_map/ppermute | solution.py:1170
  169.7 78.6 %collective-permute-start.6 = (bf16[512,2048]{1,0:T(8,128)(2,1)S(1)}, bf16[512,2048]{1,0:T(8,128)(2,1)}, u32[]{:S(2)}, u32[]{:S(2)}) collective-permute-start(bf16[512,2048]{1,0:T(8,128)(2,1)S(1)} %copy-done.1), channel_id=1, source_target_pairs={{0,1},{1,2},{2,3},{4,5},{5,6},{6,7},{8,9},{9,10},{10,11},{12,13},{... | collective-permute-start | bytes 6291464 | tf_op jit(solution)/shard_map/ppermute | solution.py:1170
  181.4 66.9 %collective-permute-start.7 = (bf16[512,2048]{1,0:T(8,128)(2,1)S(1)}, bf16[512,2048]{1,0:T(8,128)(2,1)}, u32[]{:S(2)}, u32[]{:S(2)}) collective-permute-start(bf16[512,2048]{1,0:T(8,128)(2,1)S(1)} %copy-done.1), channel_id=1, source_target_pairs={{1,0},{2,1},{3,2},{5,4},{6,5},{7,6},{9,8},{10,9},{11,10},{13,12},{... | collective-permute-start | bytes 6291464 | tf_op jit(solution)/shard_map/ppermute | solution.py:1170
  248.3 30.8 %collective-permute-start.8 = (bf16[512,2048]{1,0:T(8,128)(2,1)}, bf16[512,2048]{1,0:T(8,128)(2,1)S(1)}, u32[]{:S(2)}, u32[]{:S(2)}) collective-permute-start(bf16[512,2048]{1,0:T(8,128)(2,1)} %collective-permute-done.6.refs_1_), channel_id=1, source_target_pairs={{1,2},{2,3},{5,6},{6,7},{9,10},{10,11},{13,14},{14,15},{17,18},{18... | collective-permute-start | bytes 6291464 | tf_op jit(solution)/shard_map/ppermute | solution.py:1170
  249.1 47.3 %collective-permute-start.9 = (bf16[512,2048]{1,0:T(8,128)(2,1)}, bf16[512,2048]{1,0:T(8,128)(2,1)}, u32[]{:S(2)}, u32[]{:S(2)}) collective-permute-start(bf16[512,2048]{1,0:T(8,128)(2,1)} %collective-permute-done.7.refs_2_), channel_id=1, source_target_pairs={{1,0},{2,1},{5,4},{6,5},{9,8},{10,9},{13,12},{14,13},{17,16},{18,1... | collective-permute-start | bytes 6291464 | tf_op jit(solution)/shard_map/ppermute | solution.py:1170
  296.4 31.1 %collective-permute-start.10 = (bf16[512,2048]{1,0:T(8,128)(2,1)}, bf16[512,2048]{1,0:T(8,128)(2,1)S(1)}, u32[]{:S(2)}, u32[]{:S(2)}) collective-permute-start(bf16[512,2048]{1,0:T(8,128)(2,1)} %copy-done.7), channel_id=1, source_target_pairs={{2,3},{6,7},{10,11},{14,15},{18,19},{22,23},{26,27},{30,31}} | collective-permute-start | bytes 6291464 | tf_op jit(solution)/shard_map/ppermute | solution.py:1170
  297.2 46.4 %collective-permute-start.11 = (bf16[512,2048]{1,0:T(8,128)(2,1)}, bf16[512,2048]{1,0:T(8,128)(2,1)}, u32[]{:S(2)}, u32[]{:S(2)}) collective-permute-start(bf16[512,2048]{1,0:T(8,128)(2,1)} %collective-permute-done.9.refs_4_), channel_id=1, source_target_pairs={{1,0},{5,4},{9,8},{13,12},{17,16},{21,20},{25,24},{29,28}} | collective-permute-start | bytes 6291464 | tf_op jit(solution)/shard_map/ppermute | solution.py:1170
  343.6 303.8 %reduce-scatter.5.cloned.1.call-start = ((), (), s32[]{:S(2)}) async-start(), calls=%async_computation.5 | async-start | bytes 10485760 | tf_op jit(solution)/shard_map/reduce_scatter | solution.py:1220
  377.3 77.3 %collective-permute-start.12 = (bf16[4,2560,256]{2,1,0:T(8,128)(2,1)}, bf16[4,2560,256]{2,1,0:T(8,128)(2,1)}, u32[]{:S(2)}, u32[]{:S(2)}) collective-permute-start(bf16[4,2560,256]{2,1,0:T(8,128)(2,1)} %columns_send.1), channel_id=1, source_target_pairs={{0,4},{4,0},{8,12},{12,8},{16,20},{20,16},{24,28},{28,24},{1,5},{5... | collective-permute-start | bytes 15728648 | tf_op jit(solution)/shard_map/ppermute | solution.py:1090
  393.6 61.0 %collective-permute-start.13 = (bf16[4,256,2048]{2,1,0:T(8,128)(2,1)}, bf16[4,256,2048]{2,1,0:T(8,128)(2,1)}, u32[]{:S(2)}, u32[]{:S(2)}) collective-permute-start(bf16[4,256,2048]{2,1,0:T(8,128)(2,1)} %get-tuple-element.121), channel_id=1, source_target_pairs={{0,4},{4,0},{8,12},{12,8},{16,20},{20,16},{24,28},{28,24},{1,5},{5... | collective-permute-start | bytes 12582920 | tf_op jit(solution)/shard_map/ppermute | solution.py:1090
  530.0 46.4 %collective-permute-start.16 = (bf16[4,256,1536]{2,1,0:T(8,128)(2,1)}, bf16[4,256,1536]{2,1,0:T(8,128)(2,1)}, u32[]{:S(2)}, u32[]{:S(2)}) collective-permute-start(bf16[4,256,1536]{2,1,0:T(8,128)(2,1)} %get-tuple-element.135), channel_id=1, source_target_pairs={{0,4},{4,0},{8,12},{12,8},{16,20},{20,16},{24,28},{28,24},{1,5},{5... | collective-permute-start | bytes 9437192 | tf_op jit(solution)/shard_map/ppermute | solution.py:1090
  531.3 34.4 %collective-permute-start.14 = (bf16[2,1280,256]{2,1,0:T(8,128)(2,1)}, bf16[2,1280,256]{2,1,0:T(8,128)(2,1)}, u32[]{:S(2)}, u32[]{:S(2)}) collective-permute-start(bf16[2,1280,256]{2,1,0:T(8,128)(2,1)} %slice.145), channel_id=1, source_target_pairs={{0,8},{4,12},{8,0},{12,4},{16,24},{20,28},{24,16},{28,20},{1,9},{5... | collective-permute-start | bytes 3932168 | tf_op jit(solution)/shard_map/ppermute | solution.py:1090
  533.4 40.4 %collective-permute-start.15 = (bf16[2,1280,256]{2,1,0:T(8,128)(2,1)S(1)}, bf16[2,1280,256]{2,1,0:T(8,128)(2,1)}, u32[]{:S(2)}, u32[]{:S(2)}) collective-permute-start(bf16[2,1280,256]{2,1,0:T(8,128)(2,1)S(1)} %slice.147), channel_id=1, source_target_pairs={{0,16},{4,20},{8,24},{12,28},{16,0},{20,4},{24,8},{28,12},{1,17},{... | collective-permute-start | bytes 3932168 | tf_op jit(solution)/shard_map/ppermute | solution.py:1090
  562.7 33.8 %collective-permute-start.24 = (bf16[2,256,1024]{2,1,0:T(8,128)(2,1)}, bf16[2,256,1024]{2,1,0:T(8,128)(2,1)}, u32[]{:S(2)}, u32[]{:S(2)}) collective-permute-start(bf16[2,256,1024]{2,1,0:T(8,128)(2,1)} %slice.170), channel_id=1, source_target_pairs={{0,16},{4,20},{8,24},{12,28},{16,0},{20,4},{24,8},{28,12},{1,17},{... | collective-permute-start | bytes 3145736 | tf_op jit(solution)/shard_map/ppermute | solution.py:1090
  562.8 35.6 %collective-permute-start.22 = (bf16[2,256,1024]{2,1,0:T(8,128)(2,1)}, bf16[2,256,1024]{2,1,0:T(8,128)(2,1)}, u32[]{:S(2)}, u32[]{:S(2)}) collective-permute-start(bf16[2,256,1024]{2,1,0:T(8,128)(2,1)} %slice.166), channel_id=1, source_target_pairs={{0,8},{4,12},{8,0},{12,4},{16,24},{20,28},{24,16},{28,20},{1,9},{5... | collective-permute-start | bytes 3145736 | tf_op jit(solution)/shard_map/ppermute | solution.py:1090
  568.5 36.7 %collective-permute-start.21 = (bf16[1,1280,256]{2,1,0:T(8,128)(2,1)}, bf16[1,1280,256]{2,1,0:T(8,128)(2,1)}, u32[]{:S(2)}, u32[]{:S(2)}) collective-permute-start(bf16[1,1280,256]{2,1,0:T(8,128)(2,1)} %slice.185), channel_id=1, source_target_pairs={{0,16},{4,20},{8,24},{12,28},{16,0},{20,4},{24,8},{28,12},{1,17},{... | collective-permute-start | bytes 1966088 | tf_op jit(solution)/shard_map/ppermute | solution.py:1090
  576.4 32.3 %collective-permute-start.26 = (bf16[1,1280,256]{2,1,0:T(8,128)(2,1)}, bf16[1,1280,256]{2,1,0:T(8,128)(2,1)S(1)}, u32[]{:S(2)}, u32[]{:S(2)}) collective-permute-start(bf16[1,1280,256]{2,1,0:T(8,128)(2,1)} %slice.189), channel_id=1, source_target_pairs={{0,8},{4,12},{8,0},{12,4},{16,24},{20,28},{24,16},{28,20},{1,9},{5... | collective-permute-start | bytes 1966088 | tf_op jit(solution)/shard_map/ppermute | solution.py:1090
  593.2 29.0 %collective-permute-start.17 = (bf16[2,256,768]{2,1,0:T(8,128)(2,1)S(1)}, bf16[2,256,768]{2,1,0:T(8,128)(2,1)S(1)}, u32[]{:S(2)}, u32[]{:S(2)}) collective-permute-start(bf16[2,256,768]{2,1,0:T(8,128)(2,1)S(1)} %slice.149), channel_id=1, source_target_pairs={{0,8},{4,12},{8,0},{12,4},{16,24},{20,28},{24,16},{28,20},{1,9},{5... | collective-permute-start | bytes 2359304 | tf_op jit(solution)/shard_map/ppermute | solution.py:1090
  596.5 25.5 %collective-permute-start.18 = (bf16[2,256,768]{2,1,0:T(8,128)(2,1)S(1)}, bf16[2,256,768]{2,1,0:T(8,128)(2,1)S(1)}, u32[]{:S(2)}, u32[]{:S(2)}) collective-permute-start(bf16[2,256,768]{2,1,0:T(8,128)(2,1)S(1)} %slice.151), channel_id=1, source_target_pairs={{0,16},{4,20},{8,24},{12,28},{16,0},{20,4},{24,8},{28,12},{1,17},{... | collective-permute-start | bytes 2359304 | tf_op jit(solution)/shard_map/ppermute | solution.py:1090
  598.4 32.8 %collective-permute-start.25 = (bf16[1,256,1024]{2,1,0:T(8,128)(2,1)S(1)}, bf16[1,256,1024]{2,1,0:T(8,128)(2,1)S(1)}, u32[]{:S(2)}, u32[]{:S(2)}) collective-permute-start(bf16[1,256,1024]{2,1,0:T(8,128)(2,1)S(1)} %slice.188), channel_id=1, source_target_pairs={{0,8},{4,12},{8,0},{12,4},{16,24},{20,28},{24,16},{28,20},{1,9},{5... | collective-permute-start | bytes 1572872 | tf_op jit(solution)/shard_map/ppermute | solution.py:1090
  605.2 28.0 %collective-permute-start.23 = (bf16[1,256,1024]{2,1,0:T(8,128)(2,1)S(1)}, bf16[1,256,1024]{2,1,0:T(8,128)(2,1)S(1)}, u32[]{:S(2)}, u32[]{:S(2)}) collective-permute-start(bf16[1,256,1024]{2,1,0:T(8,128)(2,1)S(1)} %slice.187), channel_id=1, source_target_pairs={{0,16},{4,20},{8,24},{12,28},{16,0},{20,4},{24,8},{28,12},{1,17},{... | collective-permute-start | bytes 1572872 | tf_op jit(solution)/shard_map/ppermute | solution.py:1090
  622.4 16.9 %collective-permute-start.20 = (bf16[1,256,768]{2,1,0:T(8,128)(2,1)S(1)}, bf16[1,256,768]{2,1,0:T(8,128)(2,1)S(1)}, u32[]{:S(2)}, u32[]{:S(2)}) collective-permute-start(bf16[1,256,768]{2,1,0:T(8,128)(2,1)S(1)} %slice.184), channel_id=1, source_target_pairs={{0,8},{4,12},{8,0},{12,4},{16,24},{20,28},{24,16},{28,20},{1,9},{5... | collective-permute-start | bytes 1179656 | tf_op jit(solution)/shard_map/ppermute | solution.py:1090
  (21 other events, 223.6 us)
Sparse Core Ops, SparseCore 0:
  10.5 48.2 all-gather.6
  60.6 54.3 all-gather.8
  116.9 28.0 all-gather.10
  146.8 54.3 all-gather.12
  343.8 144.9 reduce-scatter.2
  494.0 147.3 reduce-scatter.4

commit v2 on v1

--- a/solution.py
+++ b/solution.py
@@ -540,10 +540,10 @@
 
 
 def attend_kernel(
-    first_ref, q_ref, k_ref, v_ref, segc_ref, segr_ref, *refs
+    skipped, first_ref, q_ref, k_ref, v_ref, segc_ref, segr_ref, *refs
 ):
     o_ref, lse_ref, max_ref, acc_ref, bias_ref = refs[-5:]
-    i = pl.program_id(0)
+    i = pl.program_id(0) + skipped
     block, width = q_ref.shape
     pairs = width // 128
     low = low_lanes(block)
@@ -600,26 +600,27 @@
 
 def attend(qkv, segc, segr, first, part, parts, bufs):
     count = segr.shape[1]
-    whole_width = qkv.shape[1] // 3
-    width = whole_width // parts
+    width = qkv.shape[1] // 3
     pairs = width // 128
+    steps = count // BLOCK // parts
+    skipped = part * steps
     in_place = [] if bufs is None else [pl.BlockSpec(memory_space=pl.ANY)] * 2
     return pl.pallas_call(
-        attend_kernel,
+        functools.partial(attend_kernel, skipped),
         grid_spec=pltpu.PrefetchScalarGridSpec(
             num_scalar_prefetch=1,
-            grid=(count // BLOCK,),
+            grid=(steps,),
             in_specs=[
-                pl.BlockSpec((BLOCK, width), lambda i, f: (i, part)),
-                pl.BlockSpec((count, width), lambda i, f: (0, parts + part)),
-                pl.BlockSpec((count, width), lambda i, f: (0, 2 * parts + part)),
+                pl.BlockSpec((BLOCK, width), lambda i, f: (i + skipped, 0)),
+                pl.BlockSpec((count, width), lambda i, f: (0, 1)),
+                pl.BlockSpec((count, width), lambda i, f: (0, 2)),
                 whole(segc),
                 whole(segr),
             ]
             + in_place,
             out_specs=[
-                pl.BlockSpec((BLOCK, width), lambda i, f: (i, part)),
-                pl.BlockSpec((pairs, 8, BLOCK), lambda i, f: (part, 0, i)),
+                pl.BlockSpec((BLOCK, width), lambda i, f: (i + skipped, 0)),
+                pl.BlockSpec((pairs, 8, BLOCK), lambda i, f: (0, 0, i + skipped)),
             ],
             scratch_shapes=[
                 pltpu.VMEM((2 * pairs, 1, BLOCK), F32),
@@ -628,8 +629,8 @@
             ],
         ),
         out_shape=[
-            jax.ShapeDtypeStruct((count, whole_width), BF16),
-            jax.ShapeDtypeStruct((parts * pairs, 8, count), F32),
+            jax.ShapeDtypeStruct((count, width), BF16),
+            jax.ShapeDtypeStruct((pairs, 8, count), F32),
         ],
         input_output_aliases={} if bufs is None else {6: 0, 7: 1},
         cost_estimate=cost(30e9 * width / 512, count * width * 8),
@@ -1178,10 +1179,8 @@
         values = [one, jnp.where(has_left, 0, 1), right, 1, busy, last]
         return jnp.stack([jnp.asarray(v, jnp.int32) for v in values])
 
-    def present_shards(steps):
-        offsets = [0] + [d * s for s in range(1, steps + 1) for d in (-1, 1)]
-        shards = jnp.stack([me + d for d in offsets])
-        present = (shards >= 0) & (shards < n)
+    def places_of(shards, present):
+        shards, present = jnp.stack(shards), jnp.stack(present)
         order = jnp.sort(jnp.where(present, shards, n))
         order = jnp.concatenate([order, jnp.full((n,), n, order.dtype)])[:n]
         return jnp.concatenate(
@@ -1192,6 +1191,10 @@
             ]
         ).astype(jnp.int32)
 
+    def present_shards(steps):
+        shards = [me] + [me + d * s for s in range(1, steps + 1) for d in (-1, 1)]
+        return places_of(shards, [(x >= 0) & (x < n) for x in shards])
+
     early = present_shards(n - 2)
     late = turns(n - 1)
 
@@ -1227,25 +1230,51 @@
     normed, qkv = queries_early(
         after(present_shards(1), first, segc), [own_normed] + normed_in[0], w_qkv, bias_qkv, tables, n
     )
+    early_qkv = qkv
     for s in range(2, n):
         normed_in.append(line_step(after(tuple(normed_in[-1]), qkv) if s == 3 else normed_in[-1], s))
+    for s in range(2, n - 1):
+        normed, qkv = queries_chunk(turns(s), normed_in[s - 1], w_qkv, bias_qkv, tables, (normed, qkv), n)
     act, slope = units_early(
         after(early, qkv), [own_normed] + flat(normed_in[:-1]), w_up, bias_up, width, n
     )
-    normed, qkv = after((normed, qkv), act)
-    for s in range(2, n - 1):
-        normed, qkv = queries_chunk(turns(s), normed_in[s - 1], w_qkv, bias_qkv, tables, (normed, qkv), n)
-    cot_in = [line_step([after(cotangent, *normed_in[-1], qkv)] * 2, 1)]
+    def inner_step(pair, s):
+        right, left = pair
+        return [
+            shift(right, [(i, i + 1) for i in range(s - 1, n - 2)]),
+            shift(left, [(i, i - 1) for i in range(2, n - s + 1)]),
+        ]
+
+    def end_step(pair):
+        right, left = pair
+        return [shift(right, [(n - 2, n - 1)]), shift(left, [(1, 0)])]
+
+    inner = [inner_step([after(cotangent, *normed_in[-2], early_qkv)] * 2, 1)]
+    ready = after(tuple(inner[0]), *normed_in[-1], act)
+    ends = [end_step([after(cotangent, *ready)] * 2)]
+    inner.append(inner_step(ready, 2))
+    cot_from, cot_shards, cot_there = [cotangent], [me], [me >= 0]
     normed, qkv, act, slope = forward_chunk(late, normed_in[-1], *project, (normed, qkv, act, slope), n)
 
-    att, lse = attend(qkv, segc, segr, first, 0, 1, None)
-    cot_in.append(line_step(after(tuple(cot_in[-1]), att), 2))
+    att_half = attend(qkv, segc, segr, first, 0, 2, None)
+    ends.append(end_step(after(tuple(ready), *ends[0], *inner[1], att_half[0])))
+    att, lse = attend(qkv, segc, segr, first, 1, 2, att_half)
+    for s in range(3, n):
+        ready = after(tuple(inner[-1]), att)
+        ends.append(end_step(ready))
+        if s < n - 1:
+            inner.append(inner_step(ready, s))
+    for s in range(1, n - 1):
+        for direction in range(2):
+            at_end = me == (n - 1, 0)[direction]
+            shard = me + (-s, s)[direction]
+            cot_from += [inner[s - 1][direction], ends[s - 1][direction]]
+            cot_shards += [shard, shard]
+            cot_there += [(shard >= 0) & (shard < n) & jnp.logical_not(at_end), at_end]
     part = mix(att, act, w_out, w_down)
-    for s in range(3, n):
-        cot_in.append(line_step(after(tuple(cot_in[-1]), part), s))
-    bufs = backward_early(after(early, part), [cotangent] + flat(cot_in[:-1]), w_out, w_down, slope, n)
-    block_sum = line_sum(after(part, bufs[2], *cot_in[-1]))
-    cot, grad_att, grad_hid = backward_chunk(late, cot_in[-1], w_out, w_down, slope, bufs, n)
+    bufs = backward_early(after(places_of(cot_shards, cot_there), part), cot_from, w_out, w_down, slope, n)
+    block_sum = line_sum(after(part, bufs[2], *ends[-1]))
+    cot, grad_att, grad_hid = backward_chunk(late, ends[-1], w_out, w_down, slope, bufs, n)
     bits = [b for b in range(1, pieces.bit_length() - 1)]
     places = pieces // 2
     mine = lax.axis_index("dp")

time: 689 us -> 689 us (level)
  waiting for transfers between devices: 134 us -> 117 us
  Pallas kernels: 422 us -> 437 us
    ppermute x12 -> x16, waiting for transfers between devices: 103 us -> 79.4 us  [shift(): return lax.ppermute(x, 'tensor', pairs)]
    ppermute x15, starting transfers between devices: 24.8 us -> 13.3 us  [swap(): return lax.ppermute(x, 'dp', [(i, i ^ 1 << bit) for i in range(size)])]
    reduce_scatter x2, starting transfers between devices: 0.25 us -> 8.58 us  [line_sum(): return lax.psum_scatter(x, 'tensor', scatter_dimension=0, tiled=True)]
    pallas_call x1 -> x2, Pallas kernels: 42 us -> 47.6 us  [attend(): pl.pallas_call(functools.partial(attend_kernel, skipped), grid_spec=pltpu...]
    ppermute x12 -> x16, starting transfers between devices: 30.5 us -> 32.6 us  [shift(): return lax.ppermute(x, 'tensor', pairs)]
  transfers between devices with their start and end apart: 33 -> 37, of which waited for: 12 -> 13; matrix products, arithmetic and copies ran while one was open for 7% -> 7% of each run, Pallas kernels for 59% -> 60%
where the time goes in v2:
time: 689 us; the launch traced here: 681 us
  Pallas kernels  437 us (63%)
  waiting for transfers between devices  117 us (17%)
  starting transfers between devices  54.6 us (8%)
  other arithmetic  30.3 us (4%)
  local copies, waits for them, and re-layouts  27.2 us (4%)
  between operations  15.2 us (2%)
    ppermute x16, waiting for transfers between devices, shift(): return lax.ppermute(x, 'tensor', pairs)  79.4 us
    pallas_call x1, Pallas kernels, attend_back(): pl.pallas_call(attend_back_kernel, grid_spec=pltpu.PrefetchScalarGridSpec...  62.5 us
    pallas_call x2, Pallas kernels, attend(): pl.pallas_call(functools.partial(attend_kernel, skipped), grid_spec=pltpu...  47.6 us
    pallas_call x1, Pallas kernels, grad_normed(): pl.pallas_call(grad_kernel, grid=((stop - start) // tile,), in_specs=[onc...  39.2 us
    ppermute x15, waiting for transfers between devices, swap(): return lax.ppermute(x, 'dp', [(i, i ^ 1 << bit) for i in range(size)])  35.2 us
    pallas_call x2, Pallas kernels, row_grads(): pl.pallas_call(functools.partial(rows_keep_kernel, len(gs)), grid_spec=pl...  32.6 us
    ppermute x16, starting transfers between devices, shift(): return lax.ppermute(x, 'tensor', pairs)  32.6 us
    pallas_call x2, Pallas kernels, row_grads(): pl.pallas_call(functools.partial(rows_send_kernel, len(gs)), grid_spec=pl...  30.9 us
  transfers between devices with their start and end apart: 37, of which 13 were waited for; matrix products, arithmetic and copies ran while one was open for 7% of the time, Pallas kernels for 60%

profile of v2, /device:TPU:0, one launch (start us, length us, event | category | flops | bytes accessed | tf_op | source)
XLA Modules:
  0.0 681.0 jit_solution(14430350812562755401)
XLA Ops:
  11.9 3.7 norm.1.refs_0_
  15.7 5.0 collective-permute-start
  22.4 43.4 %collective-permute-done.refs_1_ = bf16[512,2048]{1,0:T(8,128)(2,1)S(1)} collective-permute-done((bf16[512,2048]{1,0:T(8,128)(2,1)}, bf16[512,2048]{1,0:T(8,128)(2,1)S(1)}, u32[]{:S(2)}, u32[]{:S(2)}) %collective-permute-start) | collective-permute-done | bytes 2097184 | tf_op jit(solution)/shard_map/ppermute | solution.py:1171
  76.1 5.8 fusion
  81.9 15.9 %queries_early.1 = (bf16[2560,2048]{1,0:T(8,128)(2,1)}, bf16[2560,1536]{1,0:T(8,128)(2,1)}) custom-call(s32[11]{0:T(128)} %pad_add_fusion.4.where_ref, bf16[512,2048]{1,0:T(8,128)(2,1)} %norm.1.refs_0_, bf16[512,2048]{1,0:T(8,128)(2,1)} %copy-done, bf16[512,2048]{1,0:T(8,128)(2,1)} %collective-permute-done.2.refs_2_, ...), custom_call_target="tpu_custom_call" | custom-call | flops 644245120 | bytes 314572 | tf_op jit(solution)/shard_map/queries_early/pallas_call | solution.py:415
  97.9 21.9 %collective-permute-done.3.refs_1_.refs_4_ = bf16[512,2048]{1,0:T(8,128)(2,1)} collective-permute-done((bf16[512,2048]{1,0:T(8,128)(2,1)}, bf16[512,2048]{1,0:T(8,128)(2,1)}, u32[]{:S(2)}, u32[]{:S(2)}) %collective-permute-start.3) | collective-permute-done | bytes 2097184 | tf_op jit(solution)/shard_map/ppermute | solution.py:1171
  119.8 5.0 collective-permute-start.6
  134.1 11.0 %queries_chunk.1 = (bf16[2560,2048]{1,0:T(8,128)(2,1)}, bf16[2560,1536]{1,0:T(8,128)(2,1)}) custom-call(s32[6]{0:T(128)} %stack.209.where_ref, bf16[512,2048]{1,0:T(8,128)(2,1)} %collective-permute-done.1.refs_0_.refs_3_, bf16[512,2048]{1,0:T(8,128)(2,1)} %collective-permute-done.3.refs_1_.refs_4_, ...), custom_call_target="tpu_custom_call", output_to_operand_aliasing={{0}: (8, {}), {1}: (9, {})} | custom-call | flops 161061280 | bytes 314572 | tf_op jit(solution)/shard_map/queries_chunk/pallas_call | solution.py:265
  145.2 28.9 %units_early.1 = (bf16[2560,2048]{1,0:T(8,128)(2,1)}, bf16[2560,2048]{1,0:T(8,128)(2,1)}) custom-call(s32[15]{0:T(128)} %pad_add_fusion.5.where_ref, bf16[512,2048]{1,0:T(8,128)(2,1)} %norm.1.refs_0_, bf16[512,2048]{1,0:T(8,128)(2,1)} %copy-done, bf16[512,2048]{1,0:T(8,128)(2,1)} %collective-permute-done.2.refs_2_, ...), custom_call_target="tpu_custom_call" | custom-call | flops 858993472 | bytes 419430 | tf_op jit(solution)/shard_map/units_early/pallas_call | solution.py:443
  185.5 21.2 %forward_chunk.1 = (bf16[2560,2048]{1,0:T(8,128)(2,1)}, bf16[2560,1536]{1,0:T(8,128)(2,1)}, bf16[2560,2048]{1,0:T(8,128)(2,1)}, bf16[2560,2048]{1,0:T(8,128)(2,1)}) custom-call(s32[6]{0:T(128)} %stack.186.where_ref, bf16[512,2048]{1,0:T(8,128)(2,1)} %collective-permute-done.4.refs_0_, ...), custom_call_target="tpu_custom_call", output_to_operand_aliasing={{0}: (10, {}), {1}: (11, {}), {2}: (12, {}), {3}: (13, {})} | custom-call | flops 375809632 | bytes 734003 | tf_op jit(solution)/shard_map/forward_chunk/pallas_call | solution.py:322
  206.7 18.9 %attend.2 = (bf16[2048,512]{1,0:T(8,128)(2,1)}, f32[4,8,2048]{2,1,0:T(8,128)}) custom-call(s32[8]{0:T(128)} %and_select_fusion.2.first_ref, bf16[2560,1536]{1,0:T(8,128)(2,1)} %get-tuple-element.99.q_ref.k_ref.v_ref, bf16[2560,1536]{1,0:T(8,128)(2,1)} %get-tuple-element.99.q_ref.k_ref.v_ref, bf16[2560,1536]{1,0:T(8,128)(2,1)} %get-tuple-element.99.q_ref.k_ref.v_ref, ...), custom_call_target="tpu_custom_call" | custom-call | flops 1500000000 | bytes 419430 | tf_op jit(solution)/shard_map/attend/pallas_call | solution.py:608
  225.5 6.6 collective-permute-done.9.refs_4_
  235.4 28.7 %attend.3 = (bf16[2048,512]{1,0:T(8,128)(2,1)}, f32[4,8,2048]{2,1,0:T(8,128)}) custom-call(s32[8]{0:T(128)} %and_select_fusion.2.first_ref, bf16[2560,1536]{1,0:T(8,128)(2,1)} %get-tuple-element.99.q_ref.k_ref.v_ref, bf16[2560,1536]{1,0:T(8,128)(2,1)} %get-tuple-element.99.q_ref.k_ref.v_ref, ...), custom_call_target="tpu_custom_call", output_to_operand_aliasing={{0}: (6, {}), {1}: (7, {})} | custom-call | flops 1500000000 | bytes 419430 | tf_op jit(solution)/shard_map/attend/pallas_call | solution.py:608
  270.0 28.7 %mix.1 = bf16[2048,2048]{1,0:T(8,128)(2,1)} custom-call(bf16[2048,512]{1,0:T(8,128)(2,1)} %get-tuple-element.102.att_ref.o_ref, bf16[2560,2048]{1,0:T(8,128)(2,1)} %get-tuple-element.103.act_ref, bf16[8,512,256]{2,1,0:T(8,128)(2,1)} %bitcast.94, bf16[8,2048,256]{2,1,0:T(8,128)(2,1)} %bitcast.91), custom_call_target="tpu_custom_call" | custom-call | flops 1073741824 | bytes 838860 | tf_op jit(solution)/shard_map/mix/pallas_call | solution.py:784
  298.6 29.0 %backward_early.1 = (bf16[2560,2048]{1,0:T(8,128)(2,1)}, bf16[2560,512]{1,0:T(8,128)(2,1)}, bf16[2560,2048]{1,0:T(8,128)(2,1)}) custom-call(s32[23]{0:T(128)} %pad_add_fusion.6.where_ref, bf16[512,2048]{1,0:T(8,128)(2,1)} %cot_ref, bf16[512,2048]{1,0:T(8,128)(2,1)} %collective-permute-done.6.refs_1_, bf16[512,2048]{1,0:T(8,128)(2,1)} %collective-permute-done.8.refs_2_, ...), custom_call_target="tpu_custom_call" | custom-call | flops 1073741824 | bytes 524288 | tf_op jit(solution)/shard_map/backward_early/pallas_call | solution.py:510
  331.0 8.5 %reduce-scatter.5.cloned.1.call-start = ((), (), s32[]{:S(2)}) async-start(), calls=%async_computation.5 | async-start | bytes 10485760 | tf_op jit(solution)/shard_map/reduce_scatter | solution.py:1223
  340.0 14.7 %backward_chunk.1 = (bf16[2560,2048]{1,0:T(8,128)(2,1)}, bf16[2560,512]{1,0:T(8,128)(2,1)}, bf16[2560,2048]{1,0:T(8,128)(2,1)}) custom-call(s32[6]{0:T(128)} %stack.186.where_ref, bf16[512,2048]{1,0:T(8,128)(2,1)} %copy-done.6, bf16[512,2048]{1,0:T(8,128)(2,1)} %collective-permute-done.15.refs_1_, ...), custom_call_target="tpu_custom_call", output_to_operand_aliasing={{0}: (6, {}), {1}: (7, {}), {2}: (8, {})} | custom-call | flops 268435456 | bytes 524288 | tf_op jit(solution)/shard_map/backward_chunk/pallas_call | solution.py:870
  354.8 18.1 %columns_send.1 = bf16[4,2560,256]{2,1,0:T(8,128)(2,1)} custom-call(s32[4]{0:T(128)} %broadcast_xor_fusion.where_ref, bf16[2048,512]{1,0:T(8,128)(2,1)} %get-tuple-element.102.att_ref.o_ref, bf16[2560,2048]{1,0:T(8,128)(2,1)} %get-tuple-element.103.act_ref, bf16[2560,2048]{1,0:T(8,128)(2,1)} %get-tuple-element.132.c_ref), custom_call_target="tpu_custom_call" | custom-call | flops 536870912 | bytes 524288 | tf_op jit(solution)/shard_map/columns_send/pallas_call | solution.py:1009
  372.8 16.1 %rows_send.2 = (bf16[4,256,2048]{2,1,0:T(8,128)(2,1)}, f32[8,2048]{1,0:T(8,128)}) custom-call(s32[4]{0:T(128)} %broadcast_xor_fusion.where_ref, bf16[2560,2048]{1,0:T(8,128)(2,1)} %get-tuple-element.143.x_ref, bf16[2560,2048]{1,0:T(8,128)(2,1)} %get-tuple-element.138.refs_0_.gh_ref), custom_call_target="tpu_custom_call" | custom-call | flops 429496736 | bytes 419430 | tf_op jit(solution)/shard_map/rows_send/pallas_call | solution.py:1047
  389.5 62.5 %attend_back.1 = (bf16[2048,512]{1,0:T(8,128)(2,1)}, bf16[2048,512]{1,0:T(8,128)(2,1)}, bf16[2048,512]{1,0:T(8,128)(2,1)}) custom-call(s32[8]{0:T(128)} %and_select_fusion.2.first_ref, bf16[2560,1536]{1,0:T(8,128)(2,1)} %get-tuple-element.99.q_ref.k_ref.v_ref, bf16[2560,1536]{1,0:T(8,128)(2,1)} %get-tuple-element.99.q_ref.k_ref.v_ref, ...), custom_call_target="tpu_custom_call" | custom-call | flops 2200000000 | bytes 1048576 | tf_op jit(solution)/shard_map/attend_back/pallas_call | solution.py:735
  452.0 39.2 %grad_normed.1 = bf16[2048,2048]{1,0:T(8,128)(2,1)} custom-call(bf16[2048,512]{1,0:T(8,128)(2,1)} %get-tuple-element.134.gq_ref.refs_0_, bf16[2048,512]{1,0:T(8,128)(2,1)} %get-tuple-element.135.gk_ref.refs_1_, bf16[2048,512]{1,0:T(8,128)(2,1)} %get-tuple-element.136.gv_ref.refs_2_, bf16[2560,2048]{1,0:T(8,128)(2,1)} %get-tuple-element.138.refs_0_.gh_ref, ...), custom_call_target="tpu_custom_call" | custom-call | flops 1503238528 | bytes 838860 | tf_op jit(solution)/shard_map/grad_normed/pallas_call | solution.py:903
  492.5 20.0 %columns_keep.1 = (bf16[4,1280,256]{2,1,0:T(8,128)(2,1)}, bf16[4,1280,256]{2,1,0:T(8,128)(2,1)}) custom-call(s32[16]{0:T(128)} %pad_add_fusion.7.where_ref, bf16[2048,512]{1,0:T(8,128)(2,1)} %get-tuple-element.102.att_ref.o_ref, bf16[2560,2048]{1,0:T(8,128)(2,1)} %get-tuple-element.103.act_ref, bf16[2560,2048]{1,0:T(8,128)(2,1)} %get-tuple-element.132.c_ref, ...), custom_call_target="tpu_custom_call" | custom-call | flops 536870912 | bytes 524288 | tf_op jit(solution)/shard_map/columns_keep/pallas_call | solution.py:1023
  512.5 14.8 %rows_send.3 = (bf16[4,256,1536]{2,1,0:T(8,128)(2,1)}, f32[8,1536]{1,0:T(8,128)}) custom-call(s32[4]{0:T(128)} %broadcast_xor_fusion.where_ref, bf16[2560,2048]{1,0:T(8,128)(2,1)} %get-tuple-element.143.x_ref, bf16[2048,512]{1,0:T(8,128)(2,1)} %get-tuple-element.134.gq_ref.refs_0_, bf16[2048,512]{1,0:T(8,128)(2,1)} %get-tuple-element.135.gk_ref.refs_1_, ...), custom_call_target="tpu_custom_call" | custom-call | flops 322122560 | bytes 314572 | tf_op jit(solution)/shard_map/rows_send/pallas_call | solution.py:1047
  532.5 17.3 %rows_keep.2 = (bf16[4,256,1024]{2,1,0:T(8,128)(2,1)}, bf16[4,256,1024]{2,1,0:T(8,128)(2,1)}) custom-call(s32[16]{0:T(128)} %pad_add_fusion.7.where_ref, bf16[2560,2048]{1,0:T(8,128)(2,1)} %get-tuple-element.143.x_ref, bf16[2560,2048]{1,0:T(8,128)(2,1)} %get-tuple-element.138.refs_0_.gh_ref, bf16[4,256,2048]{2,1,0:T(8,128)(2,1)} %collective-permute-done.17.refs_1_), custom_call_target="tpu_custom_call" | custom-call | flops 429496736 | bytes 419430 | tf_op jit(solution)/shard_map/rows_keep/pallas_call | solution.py:1067
  556.9 3.5 collective-permute-done.18
  567.2 15.3 %rows_keep.3 = (bf16[4,256,768]{2,1,0:T(8,128)(2,1)}, bf16[4,256,768]{2,1,0:T(8,128)(2,1)}) custom-call(s32[16]{0:T(128)} %pad_add_fusion.7.where_ref, bf16[2560,2048]{1,0:T(8,128)(2,1)} %get-tuple-element.143.x_ref, bf16[2048,512]{1,0:T(8,128)(2,1)} %get-tuple-element.134.gq_ref.refs_0_, bf16[2048,512]{1,0:T(8,128)(2,1)} %get-tuple-element.135.gk_ref.refs_1_, ...), custom_call_target="tpu_custom_call" | custom-call | flops 322122560 | bytes 314572 | tf_op jit(solution)/shard_map/rows_keep/pallas_call | solution.py:1067
  592.9 5.5 collective-permute-done.25
  603.0 12.2 %collective-permute-done.22 = bf16[2,256,768]{2,1,0:T(8,128)(2,1)S(1)} collective-permute-done((bf16[2,256,768]{2,1,0:T(8,128)(2,1)S(1)}, bf16[2,256,768]{2,1,0:T(8,128)(2,1)S(1)}, u32[]{:S(2)}, u32[]{:S(2)}) %collective-permute-start.22) | collective-permute-done | bytes 786464 | tf_op jit(solution)/shard_map/ppermute | solution.py:1091
  617.7 7.2 %collective-permute-done.29 = bf16[1,256,1024]{2,1,0:T(8,128)(2,1)S(1)} collective-permute-done((bf16[1,256,1024]{2,1,0:T(8,128)(2,1)S(1)}, bf16[1,256,1024]{2,1,0:T(8,128)(2,1)S(1)}, u32[]{:S(2)}, u32[]{:S(2)}) %collective-permute-start.29) | collective-permute-done | bytes 524320 | tf_op jit(solution)/shard_map/ppermute | solution.py:1091
  628.0 4.9 collective-permute-done.24
  639.4 7.0 %norm_back.1 = (bf16[512,2048]{1,0:T(8,128)(2,1)}, f32[8,2048]{1,0:T(8,128)}) custom-call(bf16[512,2048]{1,0:T(8,128)(2,1)} %x_ref.5, bf16[512,2048]{1,0:T(8,128)(2,1)} %cot_ref, bf16[512,2048]{1,0:T(8,128)(2,1)} %reduce-scatter.5.cloned.1.call-done.refs_0_, f32[1,2048]{1,0:T(1,128)} %bitcast.106), custom_call_target="tpu_custom_call" | custom-call | flops 1048576 | bytes 629145 | tf_op jit(solution)/shard_map/norm_back/pallas_call | solution.py:127
  647.8 22.6 %small_sums.1 = f32[80,128]{1,0:T(8,128)} custom-call(f32[80,128]{1,0:T(8,128)} %select_maximum_fusion.x_ref), custom_call_target="tpu_custom_call" | custom-call | tf_op jit(solution)/shard_map/small_sums/pallas_call | solution.py:1143
  (206 shorter events, 102.7 us)
Async XLA Ops:
  7.2 74.7 %all-gather.7.cloned.1.call-start = ((), (), s32[]{:S(2)}) async-start(), calls=%async_computation.2 | async-start | bytes 7077888 | tf_op jit(solution)/shard_map/all_gather | solution.py:1203
  9.8 135.4 %all-gather.9.cloned.1.call-start = ((), (), s32[]{:S(2)}) async-start(), calls=%async_computation.3 | async-start | bytes 9437184 | tf_op jit(solution)/shard_map/all_gather | solution.py:1204
  10.6 259.4 %all-gather.11.cloned.1.call-start = ((), (), s32[]{:S(2)}) async-start(), calls=%async_computation.6 | async-start | bytes 2359296 | tf_op jit(solution)/shard_map/all_gather | solution.py:1205
  11.3 258.7 %all-gather.13.cloned.1.call-start = ((), (), s32[]{:S(2)}) async-start(), calls=%async_computation.7 | async-start | bytes 9437184 | tf_op jit(solution)/shard_map/all_gather | solution.py:1206
  11.9 479.4 %reduce-scatter.3.cloned.1.call-start = ((), (), s32[]{:S(2)}) async-start(), calls=%async_computation.4 | async-start | bytes 10485760 | tf_op jit(solution)/shard_map/reduce_scatter | solution.py:1223
  15.7 50.1 %collective-permute-start = (bf16[512,2048]{1,0:T(8,128)(2,1)}, bf16[512,2048]{1,0:T(8,128)(2,1)S(1)}, u32[]{:S(2)}, u32[]{:S(2)}) collective-permute-start(bf16[512,2048]{1,0:T(8,128)(2,1)} %norm.1.refs_0_), channel_id=1, source_target_pairs={{0,1},{1,2},{2,3},{4,5},{5,6},{6,7},{8,9},{9,10},{10,11},{12,13},{... | collective-permute-start | bytes 6291464 | tf_op jit(solution)/shard_map/ppermute | solution.py:1171
  20.7 49.3 %collective-permute-start.2 = (bf16[512,2048]{1,0:T(8,128)(2,1)}, bf16[512,2048]{1,0:T(8,128)(2,1)}, u32[]{:S(2)}, u32[]{:S(2)}) collective-permute-start(bf16[512,2048]{1,0:T(8,128)(2,1)} %norm.1.refs_0_), channel_id=1, source_target_pairs={{1,0},{2,1},{3,2},{5,4},{6,5},{7,6},{9,8},{10,9},{11,10},{13,12},{... | collective-permute-start | bytes 6291464 | tf_op jit(solution)/shard_map/ppermute | solution.py:1171
  65.8 32.1 %collective-permute-start.1 = (bf16[512,2048]{1,0:T(8,128)(2,1)S(1)}, bf16[512,2048]{1,0:T(8,128)(2,1)}, u32[]{:S(2)}, u32[]{:S(2)}) collective-permute-start(bf16[512,2048]{1,0:T(8,128)(2,1)S(1)} %collective-permute-done.refs_1_), channel_id=1, source_target_pairs={{1,2},{2,3},{5,6},{6,7},{9,10},{10,11},{13,14},{14,15},{17,18},{18... | collective-permute-start | bytes 6291464 | tf_op jit(solution)/shard_map/ppermute | solution.py:1171
  70.0 49.7 %collective-permute-start.3 = (bf16[512,2048]{1,0:T(8,128)(2,1)}, bf16[512,2048]{1,0:T(8,128)(2,1)}, u32[]{:S(2)}, u32[]{:S(2)}) collective-permute-start(bf16[512,2048]{1,0:T(8,128)(2,1)} %collective-permute-done.2.refs_2_), channel_id=1, source_target_pairs={{1,0},{2,1},{5,4},{6,5},{9,8},{10,9},{13,12},{14,13},{17,16},{18,1... | collective-permute-start | bytes 6291464 | tf_op jit(solution)/shard_map/ppermute | solution.py:1171
  119.8 54.3 %collective-permute-start.6 = (bf16[512,2048]{1,0:T(8,128)(2,1)}, bf16[512,2048]{1,0:T(8,128)(2,1)}, u32[]{:S(2)}, u32[]{:S(2)}) collective-permute-start(bf16[512,2048]{1,0:T(8,128)(2,1)} %cot_ref), channel_id=1, source_target_pairs={{0,1},{1,2},{4,5},{5,6},{8,9},{9,10},{12,13},{13,14},{16,17},{17,1... | collective-permute-start | bytes 6291464 | tf_op jit(solution)/shard_map/ppermute | solution.py:1171
  124.8 49.3 %collective-permute-start.7 = (bf16[512,2048]{1,0:T(8,128)(2,1)}, bf16[512,2048]{1,0:T(8,128)(2,1)}, u32[]{:S(2)}, u32[]{:S(2)}) collective-permute-start(bf16[512,2048]{1,0:T(8,128)(2,1)} %cot_ref), channel_id=1, source_target_pairs={{2,1},{3,2},{6,5},{7,6},{10,9},{11,10},{14,13},{15,14},{18,17},{19... | collective-permute-start | bytes 6291464 | tf_op jit(solution)/shard_map/ppermute | solution.py:1171
  126.8 47.3 %collective-permute-start.4 = (bf16[512,2048]{1,0:T(8,128)(2,1)}, bf16[512,2048]{1,0:T(8,128)(2,1)}, u32[]{:S(2)}, u32[]{:S(2)}) collective-permute-start(bf16[512,2048]{1,0:T(8,128)(2,1)} %collective-permute-done.1.refs_0_.refs_3_), channel_id=1, source_target_pairs={{2,3},{6,7},{10,11},{14,15},{18,19},{22,23},{26,27},{30,31}} | collective-permute-start | bytes 6291464 | tf_op jit(solution)/shard_map/ppermute | solution.py:1171
  128.8 47.3 %collective-permute-start.5 = (bf16[512,2048]{1,0:T(8,128)(2,1)}, bf16[512,2048]{1,0:T(8,128)(2,1)}, u32[]{:S(2)}, u32[]{:S(2)}) collective-permute-start(bf16[512,2048]{1,0:T(8,128)(2,1)} %collective-permute-done.3.refs_1_.refs_4_), channel_id=1, source_target_pairs={{1,0},{5,4},{9,8},{13,12},{17,16},{21,20},{25,24},{29,28}} | collective-permute-start | bytes 6291464 | tf_op jit(solution)/shard_map/ppermute | solution.py:1171
  176.1 49.4 %collective-permute-start.8 = (bf16[512,2048]{1,0:T(8,128)(2,1)S(1)}, bf16[512,2048]{1,0:T(8,128)(2,1)}, u32[]{:S(2)}, u32[]{:S(2)}) collective-permute-start(bf16[512,2048]{1,0:T(8,128)(2,1)S(1)} %copy-done.1), channel_id=1, source_target_pairs={{2,3},{6,7},{10,11},{14,15},{18,19},{22,23},{26,27},{30,31}} | collective-permute-start | bytes 6291464 | tf_op jit(solution)/shard_map/ppermute | solution.py:1171
  178.1 54.1 %collective-permute-start.9 = (bf16[512,2048]{1,0:T(8,128)(2,1)S(1)}, bf16[512,2048]{1,0:T(8,128)(2,1)}, u32[]{:S(2)}, u32[]{:S(2)}) collective-permute-start(bf16[512,2048]{1,0:T(8,128)(2,1)S(1)} %copy-done.1), channel_id=1, source_target_pairs={{1,0},{5,4},{9,8},{13,12},{17,16},{21,20},{25,24},{29,28}} | collective-permute-start | bytes 6291464 | tf_op jit(solution)/shard_map/ppermute | solution.py:1171
  179.3 52.8 %collective-permute-start.10 = (bf16[512,2048]{1,0:T(8,128)(2,1)}, bf16[512,2048]{1,0:T(8,128)(2,1)}, u32[]{:S(2)}, u32[]{:S(2)}) collective-permute-start(bf16[512,2048]{1,0:T(8,128)(2,1)} %collective-permute-done.6.refs_1_), channel_id=1, source_target_pairs={{1,2},{5,6},{9,10},{13,14},{17,18},{21,22},{25,26},{29,30}} | collective-permute-start | bytes 6291464 | tf_op jit(solution)/shard_map/ppermute | solution.py:1171
  181.3 50.8 %collective-permute-start.11 = (bf16[512,2048]{1,0:T(8,128)(2,1)}, bf16[512,2048]{1,0:T(8,128)(2,1)}, u32[]{:S(2)}, u32[]{:S(2)}) collective-permute-start(bf16[512,2048]{1,0:T(8,128)(2,1)} %collective-permute-done.7.refs_3_), channel_id=1, source_target_pairs={{2,1},{6,5},{10,9},{14,13},{18,17},{22,21},{26,25},{30,29}} | collective-permute-start | bytes 6291464 | tf_op jit(solution)/shard_map/ppermute | solution.py:1171
  232.1 66.5 %collective-permute-start.12 = (bf16[512,2048]{1,0:T(8,128)(2,1)}, bf16[512,2048]{1,0:T(8,128)(2,1)}, u32[]{:S(2)}, u32[]{:S(2)}) collective-permute-start(bf16[512,2048]{1,0:T(8,128)(2,1)} %collective-permute-done.6.refs_1_), channel_id=1, source_target_pairs={{2,3},{6,7},{10,11},{14,15},{18,19},{22,23},{26,27},{30,31}} | collective-permute-start | bytes 6291464 | tf_op jit(solution)/shard_map/ppermute | solution.py:1171
  234.1 64.5 %collective-permute-start.13 = (bf16[512,2048]{1,0:T(8,128)(2,1)}, bf16[512,2048]{1,0:T(8,128)(2,1)}, u32[]{:S(2)}, u32[]{:S(2)}) collective-permute-start(bf16[512,2048]{1,0:T(8,128)(2,1)} %collective-permute-done.7.refs_3_), channel_id=1, source_target_pairs={{1,0},{5,4},{9,8},{13,12},{17,16},{21,20},{25,24},{29,28}} | collective-permute-start | bytes 6291464 | tf_op jit(solution)/shard_map/ppermute | solution.py:1171
  264.1 63.5 %collective-permute-start.14 = (bf16[512,2048]{1,0:T(8,128)(2,1)}, bf16[512,2048]{1,0:T(8,128)(2,1)S(1)}, u32[]{:S(2)}, u32[]{:S(2)}) collective-permute-start(bf16[512,2048]{1,0:T(8,128)(2,1)} %collective-permute-done.10.refs_5_), channel_id=1, source_target_pairs={{2,3},{6,7},{10,11},{14,15},{18,19},{22,23},{26,27},{30,31}} | collective-permute-start | bytes 6291464 | tf_op jit(solution)/shard_map/ppermute | solution.py:1171
  264.9 66.0 %collective-permute-start.15 = (bf16[512,2048]{1,0:T(8,128)(2,1)}, bf16[512,2048]{1,0:T(8,128)(2,1)}, u32[]{:S(2)}, u32[]{:S(2)}) collective-permute-start(bf16[512,2048]{1,0:T(8,128)(2,1)} %collective-permute-done.11.refs_7_), channel_id=1, source_target_pairs={{1,0},{5,4},{9,8},{13,12},{17,16},{21,20},{25,24},{29,28}} | collective-permute-start | bytes 6291464 | tf_op jit(solution)/shard_map/ppermute | solution.py:1171
  331.0 308.4 %reduce-scatter.5.cloned.1.call-start = ((), (), s32[]{:S(2)}) async-start(), calls=%async_computation.5 | async-start | bytes 10485760 | tf_op jit(solution)/shard_map/reduce_scatter | solution.py:1223
  372.8 79.2 %collective-permute-start.16 = (bf16[4,2560,256]{2,1,0:T(8,128)(2,1)}, bf16[4,2560,256]{2,1,0:T(8,128)(2,1)}, u32[]{:S(2)}, u32[]{:S(2)}) collective-permute-start(bf16[4,2560,256]{2,1,0:T(8,128)(2,1)} %columns_send.1), channel_id=1, source_target_pairs={{0,4},{4,0},{8,12},{12,8},{16,20},{20,16},{24,28},{28,24},{1,5},{5... | collective-permute-start | bytes 15728648 | tf_op jit(solution)/shard_map/ppermute | solution.py:1091
  389.0 63.0 %collective-permute-start.17 = (bf16[4,256,2048]{2,1,0:T(8,128)(2,1)}, bf16[4,256,2048]{2,1,0:T(8,128)(2,1)}, u32[]{:S(2)}, u32[]{:S(2)}) collective-permute-start(bf16[4,256,2048]{2,1,0:T(8,128)(2,1)} %get-tuple-element.130), channel_id=1, source_target_pairs={{0,4},{4,0},{8,12},{12,8},{16,20},{20,16},{24,28},{28,24},{1,5},{5... | collective-permute-start | bytes 12582920 | tf_op jit(solution)/shard_map/ppermute | solution.py:1091
  527.3 40.0 %collective-permute-start.20 = (bf16[4,256,1536]{2,1,0:T(8,128)(2,1)}, bf16[4,256,1536]{2,1,0:T(8,128)(2,1)}, u32[]{:S(2)}, u32[]{:S(2)}) collective-permute-start(bf16[4,256,1536]{2,1,0:T(8,128)(2,1)} %get-tuple-element.144), channel_id=1, source_target_pairs={{0,4},{4,0},{8,12},{12,8},{16,20},{20,16},{24,28},{28,24},{1,5},{5... | collective-permute-start | bytes 9437192 | tf_op jit(solution)/shard_map/ppermute | solution.py:1091
  528.5 31.9 %collective-permute-start.18 = (bf16[2,1280,256]{2,1,0:T(8,128)(2,1)}, bf16[2,1280,256]{2,1,0:T(8,128)(2,1)}, u32[]{:S(2)}, u32[]{:S(2)}) collective-permute-start(bf16[2,1280,256]{2,1,0:T(8,128)(2,1)} %slice.149), channel_id=1, source_target_pairs={{0,8},{4,12},{8,0},{12,4},{16,24},{20,28},{24,16},{28,20},{1,9},{5... | collective-permute-start | bytes 3932168 | tf_op jit(solution)/shard_map/ppermute | solution.py:1091
  530.1 34.5 %collective-permute-start.19 = (bf16[2,1280,256]{2,1,0:T(8,128)(2,1)S(1)}, bf16[2,1280,256]{2,1,0:T(8,128)(2,1)}, u32[]{:S(2)}, u32[]{:S(2)}) collective-permute-start(bf16[2,1280,256]{2,1,0:T(8,128)(2,1)S(1)} %slice.151), channel_id=1, source_target_pairs={{0,16},{4,20},{8,24},{12,28},{16,0},{20,4},{24,8},{28,12},{1,17},{... | collective-permute-start | bytes 3932168 | tf_op jit(solution)/shard_map/ppermute | solution.py:1091
  554.5 32.7 %collective-permute-start.28 = (bf16[2,256,1024]{2,1,0:T(8,128)(2,1)}, bf16[2,256,1024]{2,1,0:T(8,128)(2,1)}, u32[]{:S(2)}, u32[]{:S(2)}) collective-permute-start(bf16[2,256,1024]{2,1,0:T(8,128)(2,1)} %slice.174), channel_id=1, source_target_pairs={{0,16},{4,20},{8,24},{12,28},{16,0},{20,4},{24,8},{28,12},{1,17},{... | collective-permute-start | bytes 3145736 | tf_op jit(solution)/shard_map/ppermute | solution.py:1091
  555.6 34.0 %collective-permute-start.26 = (bf16[2,256,1024]{2,1,0:T(8,128)(2,1)}, bf16[2,256,1024]{2,1,0:T(8,128)(2,1)}, u32[]{:S(2)}, u32[]{:S(2)}) collective-permute-start(bf16[2,256,1024]{2,1,0:T(8,128)(2,1)} %slice.170), channel_id=1, source_target_pairs={{0,8},{4,12},{8,0},{12,4},{16,24},{20,28},{24,16},{28,20},{1,9},{5... | collective-permute-start | bytes 3145736 | tf_op jit(solution)/shard_map/ppermute | solution.py:1091
  563.1 35.3 %collective-permute-start.25 = (bf16[1,1280,256]{2,1,0:T(8,128)(2,1)}, bf16[1,1280,256]{2,1,0:T(8,128)(2,1)}, u32[]{:S(2)}, u32[]{:S(2)}) collective-permute-start(bf16[1,1280,256]{2,1,0:T(8,128)(2,1)} %slice.189), channel_id=1, source_target_pairs={{0,16},{4,20},{8,24},{12,28},{16,0},{20,4},{24,8},{28,12},{1,17},{... | collective-permute-start | bytes 1966088 | tf_op jit(solution)/shard_map/ppermute | solution.py:1091
  567.2 33.4 %collective-permute-start.30 = (bf16[1,1280,256]{2,1,0:T(8,128)(2,1)}, bf16[1,1280,256]{2,1,0:T(8,128)(2,1)S(1)}, u32[]{:S(2)}, u32[]{:S(2)}) collective-permute-start(bf16[1,1280,256]{2,1,0:T(8,128)(2,1)} %slice.193), channel_id=1, source_target_pairs={{0,8},{4,12},{8,0},{12,4},{16,24},{20,28},{24,16},{28,20},{1,9},{5... | collective-permute-start | bytes 1966088 | tf_op jit(solution)/shard_map/ppermute | solution.py:1091
  589.6 35.3 %collective-permute-start.29 = (bf16[1,256,1024]{2,1,0:T(8,128)(2,1)S(1)}, bf16[1,256,1024]{2,1,0:T(8,128)(2,1)S(1)}, u32[]{:S(2)}, u32[]{:S(2)}) collective-permute-start(bf16[1,256,1024]{2,1,0:T(8,128)(2,1)S(1)} %slice.192), channel_id=1, source_target_pairs={{0,8},{4,12},{8,0},{12,4},{16,24},{20,28},{24,16},{28,20},{1,9},{5... | collective-permute-start | bytes 1572872 | tf_op jit(solution)/shard_map/ppermute | solution.py:1091
  (24 other events, 335.9 us)
Sparse Core Ops, SparseCore 0:
  10.5 48.2 all-gather.6
  60.6 54.4 all-gather.8
  117.0 27.9 all-gather.10
  146.7 54.3 all-gather.12
  331.1 156.3 reduce-scatter.2
  491.4 147.7 reduce-scatter.4

commit v3 on v2

--- a/solution.py
+++ b/solution.py
@@ -1197,6 +1197,27 @@
 
     early = present_shards(n - 2)
     late = turns(n - 1)
+    middle = [turns(s) for s in range(2, n - 1)]
+    cot_shards, cot_there = [me], [me >= 0]
+    for s in range(1, n - 1):
+        for direction in range(2):
+            at_end = me == (n - 1, 0)[direction]
+            shard = me + (-s, s)[direction]
+            cot_shards += [shard, shard]
+            cot_there += [(shard >= 0) & (shard < n) & jnp.logical_not(at_end), at_end]
+    cot_early = places_of(cot_shards, cot_there)
+
+    bits = [b for b in range(1, pieces.bit_length() - 1)]
+    places = pieces // 2
+    mine = lax.axis_index("dp")
+
+    def place_of(r, order):
+        return sum(((r >> (len(order) - 1 - k)) & 1) << bit for k, bit in enumerate(order))
+
+    kept = [place_of(r, bits) for r in range(places)] + [place_of(r, bits[::-1]) for r in range(places)]
+    send_where = mine ^ jnp.array([2 * q + 1 for q in range(places)], jnp.int32)
+    keep_where = jnp.concatenate([mine ^ jnp.array(kept, jnp.int32), jnp.array(kept, jnp.int32) // 2])
+    plans = [early, late, *middle, cot_early, send_where, keep_where]
 
     own_normed = norm(tokens, ln_gain[None], ln_shift[None])
 
@@ -1227,14 +1248,17 @@
 
     project = (w_qkv, w_up, bias_qkv, bias_up, tables)
     normed_in = [line_step([own_normed] * 2, 1)]
+    plans = lax.optimization_barrier(plans)
+    early, late, cot_early, send_where, keep_where = plans[0], plans[1], *plans[-3:]
+    middle = plans[2:-3]
     normed, qkv = queries_early(
-        after(present_shards(1), first, segc), [own_normed] + normed_in[0], w_qkv, bias_qkv, tables, n
+        after(present_shards(1), *plans, first, segc), [own_normed] + normed_in[0], w_qkv, bias_qkv, tables, n
     )
     early_qkv = qkv
     for s in range(2, n):
         normed_in.append(line_step(after(tuple(normed_in[-1]), qkv) if s == 3 else normed_in[-1], s))
     for s in range(2, n - 1):
-        normed, qkv = queries_chunk(turns(s), normed_in[s - 1], w_qkv, bias_qkv, tables, (normed, qkv), n)
+        normed, qkv = queries_chunk(middle[s - 2], normed_in[s - 1], w_qkv, bias_qkv, tables, (normed, qkv), n)
     act, slope = units_early(
         after(early, qkv), [own_normed] + flat(normed_in[:-1]), w_up, bias_up, width, n
     )
@@ -1253,7 +1277,7 @@
     ready = after(tuple(inner[0]), *normed_in[-1], act)
     ends = [end_step([after(cotangent, *ready)] * 2)]
     inner.append(inner_step(ready, 2))
-    cot_from, cot_shards, cot_there = [cotangent], [me], [me >= 0]
+    cot_from = [cotangent]
     normed, qkv, act, slope = forward_chunk(late, normed_in[-1], *project, (normed, qkv, act, slope), n)
 
     att_half = attend(qkv, segc, segr, first, 0, 2, None)
@@ -1266,26 +1290,11 @@
             inner.append(inner_step(ready, s))
     for s in range(1, n - 1):
         for direction in range(2):
-            at_end = me == (n - 1, 0)[direction]
-            shard = me + (-s, s)[direction]
             cot_from += [inner[s - 1][direction], ends[s - 1][direction]]
-            cot_shards += [shard, shard]
-            cot_there += [(shard >= 0) & (shard < n) & jnp.logical_not(at_end), at_end]
     part = mix(att, act, w_out, w_down)
-    bufs = backward_early(after(places_of(cot_shards, cot_there), part), cot_from, w_out, w_down, slope, n)
+    bufs = backward_early(after(cot_early, part), cot_from, w_out, w_down, slope, n)
     block_sum = line_sum(after(part, bufs[2], *ends[-1]))
     cot, grad_att, grad_hid = backward_chunk(late, ends[-1], w_out, w_down, slope, bufs, n)
-    bits = [b for b in range(1, pieces.bit_length() - 1)]
-    places = pieces // 2
-    mine = lax.axis_index("dp")
-
-    def place_of(r, order):
-        return sum(((r >> (len(order) - 1 - k)) & 1) << bit for k, bit in enumerate(order))
-
-    kept = [place_of(r, bits) for r in range(places)] + [place_of(r, bits[::-1]) for r in range(places)]
-    send_where = mine ^ jnp.array([2 * q + 1 for q in range(places)], jnp.int32)
-    keep_where = jnp.concatenate([mine ^ jnp.array(kept, jnp.int32), jnp.array(kept, jnp.int32) // 2])
-
     orders = (bits, bits[::-1])
 
     def finish(pair, axis, *marks):

time: 689 us -> 678 us (0.984)
  Pallas kernels: 437 us -> 427 us
where the time goes in v3:
time: 678 us; the launch traced here: 668 us
  Pallas kernels  427 us (63%)
  waiting for transfers between devices  114 us (17%)
  starting transfers between devices  54.8 us (8%)
  other arithmetic  30.6 us (5%)
  local copies, waits for them, and re-layouts  26.8 us (4%)
  between operations  15.2 us (2%)
    ppermute x16, waiting for transfers between devices, shift(): return lax.ppermute(x, 'tensor', pairs)  74.1 us
    pallas_call x1, Pallas kernels, attend_back(): pl.pallas_call(attend_back_kernel, grid_spec=pltpu.PrefetchScalarGridSpec...  60.5 us
    pallas_call x2, Pallas kernels, attend(): pl.pallas_call(functools.partial(attend_kernel, skipped), grid_spec=pltpu...  46 us
    pallas_call x1, Pallas kernels, grad_normed(): pl.pallas_call(grad_kernel, grid=((stop - start) // tile,), in_specs=[onc...  39.2 us
    ppermute x15, waiting for transfers between devices, swap(): return lax.ppermute(x, 'dp', [(i, i ^ 1 << bit) for i in range(size)])  37.9 us
    ppermute x16, starting transfers between devices, shift(): return lax.ppermute(x, 'tensor', pairs)  32.7 us
    pallas_call x2, Pallas kernels, row_grads(): pl.pallas_call(functools.partial(rows_keep_kernel, len(gs)), grid_spec=pl...  32.5 us
    pallas_call x2, Pallas kernels, row_grads(): pl.pallas_call(functools.partial(rows_send_kernel, len(gs)), grid_spec=pl...  30.9 us
  transfers between devices with their start and end apart: 37, of which 13 were waited for; matrix products, arithmetic and copies ran while one was open for 7% of the time, Pallas kernels for 60%

profile of v3, /device:TPU:0, one launch (start us, length us, event | category | flops | bytes accessed | tf_op | source)
XLA Modules:
  0.0 668.2 jit_solution(9617783891417703543)
XLA Ops:
  15.7 5.0 collective-permute-start
  29.7 36.1 %collective-permute-done.refs_1_ = bf16[512,2048]{1,0:T(8,128)(2,1)S(1)} collective-permute-done((bf16[512,2048]{1,0:T(8,128)(2,1)}, bf16[512,2048]{1,0:T(8,128)(2,1)S(1)}, u32[]{:S(2)}, u32[]{:S(2)}) %collective-permute-start) | collective-permute-done | bytes 2097184 | tf_op jit(solution)/shard_map/ppermute | solution.py:1171
  78.7 5.8 fusion
  84.5 17.2 %queries_early.1 = (bf16[2560,2048]{1,0:T(8,128)(2,1)}, bf16[2560,1536]{1,0:T(8,128)(2,1)}) custom-call(s32[11]{0:T(128)} %pad_add_fusion.7.where_ref, bf16[512,2048]{1,0:T(8,128)(2,1)} %norm.1.refs_0_, bf16[512,2048]{1,0:T(8,128)(2,1)} %copy-done, bf16[512,2048]{1,0:T(8,128)(2,1)} %collective-permute-done.2.refs_2_, ...), custom_call_target="tpu_custom_call" | custom-call | flops 644245120 | bytes 314572 | tf_op jit(solution)/shard_map/queries_early/pallas_call | solution.py:415
  101.7 18.2 %collective-permute-done.3.refs_1_.refs_4_ = bf16[512,2048]{1,0:T(8,128)(2,1)} collective-permute-done((bf16[512,2048]{1,0:T(8,128)(2,1)}, bf16[512,2048]{1,0:T(8,128)(2,1)}, u32[]{:S(2)}, u32[]{:S(2)}) %collective-permute-start.3) | collective-permute-done | bytes 2097184 | tf_op jit(solution)/shard_map/ppermute | solution.py:1171
  119.8 5.0 collective-permute-start.6
  130.1 10.7 %queries_chunk.1 = (bf16[2560,2048]{1,0:T(8,128)(2,1)}, bf16[2560,1536]{1,0:T(8,128)(2,1)}) custom-call(s32[6]{0:T(128)} %stack.216.where_ref, bf16[512,2048]{1,0:T(8,128)(2,1)} %collective-permute-done.1.refs_0_.refs_3_, bf16[512,2048]{1,0:T(8,128)(2,1)} %collective-permute-done.3.refs_1_.refs_4_, ...), custom_call_target="tpu_custom_call", output_to_operand_aliasing={{0}: (8, {}), {1}: (9, {})} | custom-call | flops 161061280 | bytes 314572 | tf_op jit(solution)/shard_map/queries_chunk/pallas_call | solution.py:265
  140.8 28.9 %units_early.1 = (bf16[2560,2048]{1,0:T(8,128)(2,1)}, bf16[2560,2048]{1,0:T(8,128)(2,1)}) custom-call(s32[15]{0:T(128)} %pad_add_fusion.4.where_ref, bf16[512,2048]{1,0:T(8,128)(2,1)} %norm.1.refs_0_, bf16[512,2048]{1,0:T(8,128)(2,1)} %copy-done, bf16[512,2048]{1,0:T(8,128)(2,1)} %collective-permute-done.2.refs_2_, ...), custom_call_target="tpu_custom_call" | custom-call | flops 858993472 | bytes 419430 | tf_op jit(solution)/shard_map/units_early/pallas_call | solution.py:443
  169.8 6.4 collective-permute-done.5.refs_1_
  184.9 21.1 %forward_chunk.1 = (bf16[2560,2048]{1,0:T(8,128)(2,1)}, bf16[2560,1536]{1,0:T(8,128)(2,1)}, bf16[2560,2048]{1,0:T(8,128)(2,1)}, bf16[2560,2048]{1,0:T(8,128)(2,1)}) custom-call(s32[6]{0:T(128)} %stack.211.where_ref, bf16[512,2048]{1,0:T(8,128)(2,1)} %collective-permute-done.4.refs_0_, ...), custom_call_target="tpu_custom_call", output_to_operand_aliasing={{0}: (10, {}), {1}: (11, {}), {2}: (12, {}), {3}: (13, {})} | custom-call | flops 375809632 | bytes 734003 | tf_op jit(solution)/shard_map/forward_chunk/pallas_call | solution.py:322
  206.0 17.2 %attend.2 = (bf16[2048,512]{1,0:T(8,128)(2,1)}, f32[4,8,2048]{2,1,0:T(8,128)}) custom-call(s32[8]{0:T(128)} %and_select_fusion.2.first_ref, bf16[2560,1536]{1,0:T(8,128)(2,1)} %get-tuple-element.112.q_ref.k_ref.v_ref, bf16[2560,1536]{1,0:T(8,128)(2,1)} %get-tuple-element.112.q_ref.k_ref.v_ref, bf16[2560,1536]{1,0:T(8,128)(2,1)} %get-tuple-element.112.q_ref.k_ref.v_ref, ...), custom_call_target="tpu_custom_call" | custom-call | flops 1500000000 | bytes 419430 | tf_op jit(solution)/shard_map/attend/pallas_call | solution.py:608
  223.2 4.7 collective-permute-done.9.refs_4_
  231.2 28.7 %attend.3 = (bf16[2048,512]{1,0:T(8,128)(2,1)}, f32[4,8,2048]{2,1,0:T(8,128)}) custom-call(s32[8]{0:T(128)} %and_select_fusion.2.first_ref, bf16[2560,1536]{1,0:T(8,128)(2,1)} %get-tuple-element.112.q_ref.k_ref.v_ref, bf16[2560,1536]{1,0:T(8,128)(2,1)} %get-tuple-element.112.q_ref.k_ref.v_ref, ...), custom_call_target="tpu_custom_call", output_to_operand_aliasing={{0}: (6, {}), {1}: (7, {})} | custom-call | flops 1500000000 | bytes 419430 | tf_op jit(solution)/shard_map/attend/pallas_call | solution.py:608
  262.1 28.7 %mix.1 = bf16[2048,2048]{1,0:T(8,128)(2,1)} custom-call(bf16[2048,512]{1,0:T(8,128)(2,1)} %get-tuple-element.115.att_ref.o_ref, bf16[2560,2048]{1,0:T(8,128)(2,1)} %get-tuple-element.116.act_ref, bf16[8,512,256]{2,1,0:T(8,128)(2,1)} %bitcast.94, bf16[8,2048,256]{2,1,0:T(8,128)(2,1)} %bitcast.91), custom_call_target="tpu_custom_call" | custom-call | flops 1073741824 | bytes 838860 | tf_op jit(solution)/shard_map/mix/pallas_call | solution.py:784
  290.7 29.0 %backward_early.1 = (bf16[2560,2048]{1,0:T(8,128)(2,1)}, bf16[2560,512]{1,0:T(8,128)(2,1)}, bf16[2560,2048]{1,0:T(8,128)(2,1)}) custom-call(s32[23]{0:T(128)} %pad_add_fusion.5.where_ref, bf16[512,2048]{1,0:T(8,128)(2,1)} %cot_ref, bf16[512,2048]{1,0:T(8,128)(2,1)} %collective-permute-done.6.refs_1_, bf16[512,2048]{1,0:T(8,128)(2,1)} %collective-permute-done.8.refs_2_, ...), custom_call_target="tpu_custom_call" | custom-call | flops 1073741824 | bytes 524288 | tf_op jit(solution)/shard_map/backward_early/pallas_call | solution.py:510
  319.7 6.6 collective-permute-done.15.refs_1_
  326.4 8.5 %reduce-scatter.5.cloned.1.call-start = ((), (), s32[]{:S(2)}) async-start(), calls=%async_computation.5 | async-start | bytes 10485760 | tf_op jit(solution)/shard_map/reduce_scatter | solution.py:1244
  334.9 14.5 %backward_chunk.1 = (bf16[2560,2048]{1,0:T(8,128)(2,1)}, bf16[2560,512]{1,0:T(8,128)(2,1)}, bf16[2560,2048]{1,0:T(8,128)(2,1)}) custom-call(s32[6]{0:T(128)} %stack.211.where_ref, bf16[512,2048]{1,0:T(8,128)(2,1)} %copy-done.6, bf16[512,2048]{1,0:T(8,128)(2,1)} %collective-permute-done.15.refs_1_, ...), custom_call_target="tpu_custom_call", output_to_operand_aliasing={{0}: (6, {}), {1}: (7, {}), {2}: (8, {})} | custom-call | flops 268435456 | bytes 524288 | tf_op jit(solution)/shard_map/backward_chunk/pallas_call | solution.py:870
  349.4 18.0 %columns_send.1 = bf16[4,2560,256]{2,1,0:T(8,128)(2,1)} custom-call(s32[4]{0:T(128)} %broadcast_xor_fusion.1.where_ref, bf16[2048,512]{1,0:T(8,128)(2,1)} %get-tuple-element.115.att_ref.o_ref, bf16[2560,2048]{1,0:T(8,128)(2,1)} %get-tuple-element.116.act_ref, bf16[2560,2048]{1,0:T(8,128)(2,1)} %get-tuple-element.144.c_ref), custom_call_target="tpu_custom_call" | custom-call | flops 536870912 | bytes 524288 | tf_op jit(solution)/shard_map/columns_send/pallas_call | solution.py:1009
  367.4 16.1 %rows_send.2 = (bf16[4,256,2048]{2,1,0:T(8,128)(2,1)}, f32[8,2048]{1,0:T(8,128)}) custom-call(s32[4]{0:T(128)} %broadcast_xor_fusion.1.where_ref, bf16[2560,2048]{1,0:T(8,128)(2,1)} %get-tuple-element.155.x_ref, bf16[2560,2048]{1,0:T(8,128)(2,1)} %get-tuple-element.150.refs_0_.gh_ref), custom_call_target="tpu_custom_call" | custom-call | flops 429496736 | bytes 419430 | tf_op jit(solution)/shard_map/rows_send/pallas_call | solution.py:1047
  384.0 60.5 %attend_back.1 = (bf16[2048,512]{1,0:T(8,128)(2,1)}, bf16[2048,512]{1,0:T(8,128)(2,1)}, bf16[2048,512]{1,0:T(8,128)(2,1)}) custom-call(s32[8]{0:T(128)} %and_select_fusion.2.first_ref, bf16[2560,1536]{1,0:T(8,128)(2,1)} %get-tuple-element.112.q_ref.k_ref.v_ref, bf16[2560,1536]{1,0:T(8,128)(2,1)} %get-tuple-element.112.q_ref.k_ref.v_ref, ...), custom_call_target="tpu_custom_call" | custom-call | flops 2200000000 | bytes 1048576 | tf_op jit(solution)/shard_map/attend_back/pallas_call | solution.py:735
  444.6 39.2 %grad_normed.1 = bf16[2048,2048]{1,0:T(8,128)(2,1)} custom-call(bf16[2048,512]{1,0:T(8,128)(2,1)} %get-tuple-element.146.gq_ref.refs_0_, bf16[2048,512]{1,0:T(8,128)(2,1)} %get-tuple-element.147.gk_ref.refs_1_, bf16[2048,512]{1,0:T(8,128)(2,1)} %get-tuple-element.148.gv_ref.refs_2_, bf16[2560,2048]{1,0:T(8,128)(2,1)} %get-tuple-element.150.refs_0_.gh_ref, ...), custom_call_target="tpu_custom_call" | custom-call | flops 1503238528 | bytes 838860 | tf_op jit(solution)/shard_map/grad_normed/pallas_call | solution.py:903
  483.8 19.7 %columns_keep.1 = (bf16[4,1280,256]{2,1,0:T(8,128)(2,1)}, bf16[4,1280,256]{2,1,0:T(8,128)(2,1)}) custom-call(s32[16]{0:T(128)} %pad_add_fusion.6.where_ref, bf16[2048,512]{1,0:T(8,128)(2,1)} %get-tuple-element.115.att_ref.o_ref, bf16[2560,2048]{1,0:T(8,128)(2,1)} %get-tuple-element.116.act_ref, bf16[2560,2048]{1,0:T(8,128)(2,1)} %get-tuple-element.144.c_ref, ...), custom_call_target="tpu_custom_call" | custom-call | flops 536870912 | bytes 524288 | tf_op jit(solution)/shard_map/columns_keep/pallas_call | solution.py:1023
  503.6 14.7 %rows_send.3 = (bf16[4,256,1536]{2,1,0:T(8,128)(2,1)}, f32[8,1536]{1,0:T(8,128)}) custom-call(s32[4]{0:T(128)} %broadcast_xor_fusion.1.where_ref, bf16[2560,2048]{1,0:T(8,128)(2,1)} %get-tuple-element.155.x_ref, bf16[2048,512]{1,0:T(8,128)(2,1)} %get-tuple-element.146.gq_ref.refs_0_, bf16[2048,512]{1,0:T(8,128)(2,1)} %get-tuple-element.147.gk_ref.refs_1_, ...), custom_call_target="tpu_custom_call" | custom-call | flops 322122560 | bytes 314572 | tf_op jit(solution)/shard_map/rows_send/pallas_call | solution.py:1047
  519.5 4.3 collective-permute-start.18
  525.5 17.2 %rows_keep.2 = (bf16[4,256,1024]{2,1,0:T(8,128)(2,1)}, bf16[4,256,1024]{2,1,0:T(8,128)(2,1)}) custom-call(s32[16]{0:T(128)} %pad_add_fusion.6.where_ref, bf16[2560,2048]{1,0:T(8,128)(2,1)} %get-tuple-element.155.x_ref, bf16[2560,2048]{1,0:T(8,128)(2,1)} %get-tuple-element.150.refs_0_.gh_ref, bf16[4,256,2048]{2,1,0:T(8,128)(2,1)} %collective-permute-done.17.refs_1_), custom_call_target="tpu_custom_call" | custom-call | flops 429496736 | bytes 419430 | tf_op jit(solution)/shard_map/rows_keep/pallas_call | solution.py:1067
  561.2 15.3 %rows_keep.3 = (bf16[4,256,768]{2,1,0:T(8,128)(2,1)}, bf16[4,256,768]{2,1,0:T(8,128)(2,1)}) custom-call(s32[16]{0:T(128)} %pad_add_fusion.6.where_ref, bf16[2560,2048]{1,0:T(8,128)(2,1)} %get-tuple-element.155.x_ref, bf16[2048,512]{1,0:T(8,128)(2,1)} %get-tuple-element.146.gq_ref.refs_0_, bf16[2048,512]{1,0:T(8,128)(2,1)} %get-tuple-element.147.gk_ref.refs_1_, ...), custom_call_target="tpu_custom_call" | custom-call | flops 322122560 | bytes 314572 | tf_op jit(solution)/shard_map/rows_keep/pallas_call | solution.py:1067
  586.7 5.6 collective-permute-done.25
  596.0 13.0 %collective-permute-done.22 = bf16[2,256,768]{2,1,0:T(8,128)(2,1)S(1)} collective-permute-done((bf16[2,256,768]{2,1,0:T(8,128)(2,1)S(1)}, bf16[2,256,768]{2,1,0:T(8,128)(2,1)S(1)}, u32[]{:S(2)}, u32[]{:S(2)}) %collective-permute-start.22) | collective-permute-done | bytes 786464 | tf_op jit(solution)/shard_map/ppermute | solution.py:1091
  609.7 8.5 %collective-permute-done.29 = bf16[1,256,1024]{2,1,0:T(8,128)(2,1)S(1)} collective-permute-done((bf16[1,256,1024]{2,1,0:T(8,128)(2,1)S(1)}, bf16[1,256,1024]{2,1,0:T(8,128)(2,1)S(1)}, u32[]{:S(2)}, u32[]{:S(2)}) %collective-permute-start.29) | collective-permute-done | bytes 524320 | tf_op jit(solution)/shard_map/ppermute | solution.py:1091
  633.3 7.0 %norm_back.1 = (bf16[512,2048]{1,0:T(8,128)(2,1)}, f32[8,2048]{1,0:T(8,128)}) custom-call(bf16[512,2048]{1,0:T(8,128)(2,1)} %x_ref.5, bf16[512,2048]{1,0:T(8,128)(2,1)} %cot_ref, bf16[512,2048]{1,0:T(8,128)(2,1)} %reduce-scatter.5.cloned.1.call-done.refs_0_, f32[1,2048]{1,0:T(1,128)} %bitcast.106), custom_call_target="tpu_custom_call" | custom-call | flops 1048576 | bytes 629145 | tf_op jit(solution)/shard_map/norm_back/pallas_call | solution.py:127
  641.7 15.9 %small_sums.1 = f32[80,128]{1,0:T(8,128)} custom-call(f32[80,128]{1,0:T(8,128)} %select_maximum_fusion.x_ref), custom_call_target="tpu_custom_call" | custom-call | tf_op jit(solution)/shard_map/small_sums/pallas_call | solution.py:1143
  (206 shorter events, 105.6 us)
Async XLA Ops:
  7.2 77.3 %all-gather.7.cloned.1.call-start = ((), (), s32[]{:S(2)}) async-start(), calls=%async_computation.2 | async-start | bytes 7077888 | tf_op jit(solution)/shard_map/all_gather | solution.py:1224
  9.8 131.0 %all-gather.9.cloned.1.call-start = ((), (), s32[]{:S(2)}) async-start(), calls=%async_computation.3 | async-start | bytes 9437184 | tf_op jit(solution)/shard_map/all_gather | solution.py:1225
  10.6 251.5 %all-gather.11.cloned.1.call-start = ((), (), s32[]{:S(2)}) async-start(), calls=%async_computation.6 | async-start | bytes 2359296 | tf_op jit(solution)/shard_map/all_gather | solution.py:1226
  11.3 250.8 %all-gather.13.cloned.1.call-start = ((), (), s32[]{:S(2)}) async-start(), calls=%async_computation.7 | async-start | bytes 9437184 | tf_op jit(solution)/shard_map/all_gather | solution.py:1227
  11.9 471.9 %reduce-scatter.3.cloned.1.call-start = ((), (), s32[]{:S(2)}) async-start(), calls=%async_computation.4 | async-start | bytes 10485760 | tf_op jit(solution)/shard_map/reduce_scatter | solution.py:1244
  15.7 50.1 %collective-permute-start = (bf16[512,2048]{1,0:T(8,128)(2,1)}, bf16[512,2048]{1,0:T(8,128)(2,1)S(1)}, u32[]{:S(2)}, u32[]{:S(2)}) collective-permute-start(bf16[512,2048]{1,0:T(8,128)(2,1)} %norm.1.refs_0_), channel_id=1, source_target_pairs={{0,1},{1,2},{2,3},{4,5},{5,6},{6,7},{8,9},{9,10},{10,11},{12,13},{... | collective-permute-start | bytes 6291464 | tf_op jit(solution)/shard_map/ppermute | solution.py:1171
  20.8 49.3 %collective-permute-start.2 = (bf16[512,2048]{1,0:T(8,128)(2,1)}, bf16[512,2048]{1,0:T(8,128)(2,1)}, u32[]{:S(2)}, u32[]{:S(2)}) collective-permute-start(bf16[512,2048]{1,0:T(8,128)(2,1)} %norm.1.refs_0_), channel_id=1, source_target_pairs={{1,0},{2,1},{3,2},{5,4},{6,5},{7,6},{9,8},{10,9},{11,10},{13,12},{... | collective-permute-start | bytes 6291464 | tf_op jit(solution)/shard_map/ppermute | solution.py:1171
  65.8 35.8 %collective-permute-start.1 = (bf16[512,2048]{1,0:T(8,128)(2,1)S(1)}, bf16[512,2048]{1,0:T(8,128)(2,1)}, u32[]{:S(2)}, u32[]{:S(2)}) collective-permute-start(bf16[512,2048]{1,0:T(8,128)(2,1)S(1)} %collective-permute-done.refs_1_), channel_id=1, source_target_pairs={{1,2},{2,3},{5,6},{6,7},{9,10},{10,11},{13,14},{14,15},{17,18},{18... | collective-permute-start | bytes 6291464 | tf_op jit(solution)/shard_map/ppermute | solution.py:1171
  70.1 49.8 %collective-permute-start.3 = (bf16[512,2048]{1,0:T(8,128)(2,1)}, bf16[512,2048]{1,0:T(8,128)(2,1)}, u32[]{:S(2)}, u32[]{:S(2)}) collective-permute-start(bf16[512,2048]{1,0:T(8,128)(2,1)} %collective-permute-done.2.refs_2_), channel_id=1, source_target_pairs={{1,0},{2,1},{5,4},{6,5},{9,8},{10,9},{13,12},{14,13},{17,16},{18,1... | collective-permute-start | bytes 6291464 | tf_op jit(solution)/shard_map/ppermute | solution.py:1171
  119.8 49.9 %collective-permute-start.6 = (bf16[512,2048]{1,0:T(8,128)(2,1)}, bf16[512,2048]{1,0:T(8,128)(2,1)}, u32[]{:S(2)}, u32[]{:S(2)}) collective-permute-start(bf16[512,2048]{1,0:T(8,128)(2,1)} %cot_ref), channel_id=1, source_target_pairs={{0,1},{1,2},{4,5},{5,6},{8,9},{9,10},{12,13},{13,14},{16,17},{17,1... | collective-permute-start | bytes 6291464 | tf_op jit(solution)/shard_map/ppermute | solution.py:1171
  124.8 44.9 %collective-permute-start.7 = (bf16[512,2048]{1,0:T(8,128)(2,1)}, bf16[512,2048]{1,0:T(8,128)(2,1)}, u32[]{:S(2)}, u32[]{:S(2)}) collective-permute-start(bf16[512,2048]{1,0:T(8,128)(2,1)} %cot_ref), channel_id=1, source_target_pairs={{2,1},{3,2},{6,5},{7,6},{10,9},{11,10},{14,13},{15,14},{18,17},{19... | collective-permute-start | bytes 6291464 | tf_op jit(solution)/shard_map/ppermute | solution.py:1171
  126.8 43.0 %collective-permute-start.4 = (bf16[512,2048]{1,0:T(8,128)(2,1)}, bf16[512,2048]{1,0:T(8,128)(2,1)}, u32[]{:S(2)}, u32[]{:S(2)}) collective-permute-start(bf16[512,2048]{1,0:T(8,128)(2,1)} %collective-permute-done.1.refs_0_.refs_3_), channel_id=1, source_target_pairs={{2,3},{6,7},{10,11},{14,15},{18,19},{22,23},{26,27},{30,31}} | collective-permute-start | bytes 6291464 | tf_op jit(solution)/shard_map/ppermute | solution.py:1171
  128.8 47.3 %collective-permute-start.5 = (bf16[512,2048]{1,0:T(8,128)(2,1)}, bf16[512,2048]{1,0:T(8,128)(2,1)}, u32[]{:S(2)}, u32[]{:S(2)}) collective-permute-start(bf16[512,2048]{1,0:T(8,128)(2,1)} %collective-permute-done.3.refs_1_.refs_4_), channel_id=1, source_target_pairs={{1,0},{5,4},{9,8},{13,12},{17,16},{21,20},{25,24},{29,28}} | collective-permute-start | bytes 6291464 | tf_op jit(solution)/shard_map/ppermute | solution.py:1171
  176.1 47.1 %collective-permute-start.8 = (bf16[512,2048]{1,0:T(8,128)(2,1)S(1)}, bf16[512,2048]{1,0:T(8,128)(2,1)}, u32[]{:S(2)}, u32[]{:S(2)}) collective-permute-start(bf16[512,2048]{1,0:T(8,128)(2,1)S(1)} %copy-done.1), channel_id=1, source_target_pairs={{2,3},{6,7},{10,11},{14,15},{18,19},{22,23},{26,27},{30,31}} | collective-permute-start | bytes 6291464 | tf_op jit(solution)/shard_map/ppermute | solution.py:1171
  178.1 49.8 %collective-permute-start.9 = (bf16[512,2048]{1,0:T(8,128)(2,1)S(1)}, bf16[512,2048]{1,0:T(8,128)(2,1)}, u32[]{:S(2)}, u32[]{:S(2)}) collective-permute-start(bf16[512,2048]{1,0:T(8,128)(2,1)S(1)} %copy-done.1), channel_id=1, source_target_pairs={{1,0},{5,4},{9,8},{13,12},{17,16},{21,20},{25,24},{29,28}} | collective-permute-start | bytes 6291464 | tf_op jit(solution)/shard_map/ppermute | solution.py:1171
  179.4 48.5 %collective-permute-start.10 = (bf16[512,2048]{1,0:T(8,128)(2,1)}, bf16[512,2048]{1,0:T(8,128)(2,1)}, u32[]{:S(2)}, u32[]{:S(2)}) collective-permute-start(bf16[512,2048]{1,0:T(8,128)(2,1)} %collective-permute-done.6.refs_1_), channel_id=1, source_target_pairs={{1,2},{5,6},{9,10},{13,14},{17,18},{21,22},{25,26},{29,30}} | collective-permute-start | bytes 6291464 | tf_op jit(solution)/shard_map/ppermute | solution.py:1171
  181.4 46.6 %collective-permute-start.11 = (bf16[512,2048]{1,0:T(8,128)(2,1)}, bf16[512,2048]{1,0:T(8,128)(2,1)}, u32[]{:S(2)}, u32[]{:S(2)}) collective-permute-start(bf16[512,2048]{1,0:T(8,128)(2,1)} %collective-permute-done.7.refs_3_), channel_id=1, source_target_pairs={{2,1},{6,5},{10,9},{14,13},{18,17},{22,21},{26,25},{30,29}} | collective-permute-start | bytes 6291464 | tf_op jit(solution)/shard_map/ppermute | solution.py:1171
  227.9 62.8 %collective-permute-start.12 = (bf16[512,2048]{1,0:T(8,128)(2,1)}, bf16[512,2048]{1,0:T(8,128)(2,1)}, u32[]{:S(2)}, u32[]{:S(2)}) collective-permute-start(bf16[512,2048]{1,0:T(8,128)(2,1)} %collective-permute-done.6.refs_1_), channel_id=1, source_target_pairs={{2,3},{6,7},{10,11},{14,15},{18,19},{22,23},{26,27},{30,31}} | collective-permute-start | bytes 6291464 | tf_op jit(solution)/shard_map/ppermute | solution.py:1171
  229.9 60.8 %collective-permute-start.13 = (bf16[512,2048]{1,0:T(8,128)(2,1)}, bf16[512,2048]{1,0:T(8,128)(2,1)}, u32[]{:S(2)}, u32[]{:S(2)}) collective-permute-start(bf16[512,2048]{1,0:T(8,128)(2,1)} %collective-permute-done.7.refs_3_), channel_id=1, source_target_pairs={{1,0},{5,4},{9,8},{13,12},{17,16},{21,20},{25,24},{29,28}} | collective-permute-start | bytes 6291464 | tf_op jit(solution)/shard_map/ppermute | solution.py:1171
  259.9 59.8 %collective-permute-start.14 = (bf16[512,2048]{1,0:T(8,128)(2,1)}, bf16[512,2048]{1,0:T(8,128)(2,1)S(1)}, u32[]{:S(2)}, u32[]{:S(2)}) collective-permute-start(bf16[512,2048]{1,0:T(8,128)(2,1)} %collective-permute-done.10.refs_5_), channel_id=1, source_target_pairs={{2,3},{6,7},{10,11},{14,15},{18,19},{22,23},{26,27},{30,31}} | collective-permute-start | bytes 6291464 | tf_op jit(solution)/shard_map/ppermute | solution.py:1171
  260.7 65.6 %collective-permute-start.15 = (bf16[512,2048]{1,0:T(8,128)(2,1)}, bf16[512,2048]{1,0:T(8,128)(2,1)}, u32[]{:S(2)}, u32[]{:S(2)}) collective-permute-start(bf16[512,2048]{1,0:T(8,128)(2,1)} %collective-permute-done.11.refs_7_), channel_id=1, source_target_pairs={{1,0},{5,4},{9,8},{13,12},{17,16},{21,20},{25,24},{29,28}} | collective-permute-start | bytes 6291464 | tf_op jit(solution)/shard_map/ppermute | solution.py:1171
  326.4 306.9 %reduce-scatter.5.cloned.1.call-start = ((), (), s32[]{:S(2)}) async-start(), calls=%async_computation.5 | async-start | bytes 10485760 | tf_op jit(solution)/shard_map/reduce_scatter | solution.py:1244
  367.4 77.1 %collective-permute-start.16 = (bf16[4,2560,256]{2,1,0:T(8,128)(2,1)}, bf16[4,2560,256]{2,1,0:T(8,128)(2,1)}, u32[]{:S(2)}, u32[]{:S(2)}) collective-permute-start(bf16[4,2560,256]{2,1,0:T(8,128)(2,1)} %columns_send.1), channel_id=1, source_target_pairs={{0,4},{4,0},{8,12},{12,8},{16,20},{20,16},{24,28},{28,24},{1,5},{5... | collective-permute-start | bytes 15728648 | tf_op jit(solution)/shard_map/ppermute | solution.py:1091
  383.6 61.0 %collective-permute-start.17 = (bf16[4,256,2048]{2,1,0:T(8,128)(2,1)}, bf16[4,256,2048]{2,1,0:T(8,128)(2,1)}, u32[]{:S(2)}, u32[]{:S(2)}) collective-permute-start(bf16[4,256,2048]{2,1,0:T(8,128)(2,1)} %get-tuple-element.142), channel_id=1, source_target_pairs={{0,4},{4,0},{8,12},{12,8},{16,20},{20,16},{24,28},{28,24},{1,5},{5... | collective-permute-start | bytes 12582920 | tf_op jit(solution)/shard_map/ppermute | solution.py:1091
  518.3 42.9 %collective-permute-start.20 = (bf16[4,256,1536]{2,1,0:T(8,128)(2,1)}, bf16[4,256,1536]{2,1,0:T(8,128)(2,1)}, u32[]{:S(2)}, u32[]{:S(2)}) collective-permute-start(bf16[4,256,1536]{2,1,0:T(8,128)(2,1)} %get-tuple-element.156), channel_id=1, source_target_pairs={{0,4},{4,0},{8,12},{12,8},{16,20},{20,16},{24,28},{28,24},{1,5},{5... | collective-permute-start | bytes 9437192 | tf_op jit(solution)/shard_map/ppermute | solution.py:1091
  519.5 34.2 %collective-permute-start.18 = (bf16[2,1280,256]{2,1,0:T(8,128)(2,1)}, bf16[2,1280,256]{2,1,0:T(8,128)(2,1)}, u32[]{:S(2)}, u32[]{:S(2)}) collective-permute-start(bf16[2,1280,256]{2,1,0:T(8,128)(2,1)} %slice.149), channel_id=1, source_target_pairs={{0,8},{4,12},{8,0},{12,4},{16,24},{20,28},{24,16},{28,20},{1,9},{5... | collective-permute-start | bytes 3932168 | tf_op jit(solution)/shard_map/ppermute | solution.py:1091
  524.0 32.6 %collective-permute-start.19 = (bf16[2,1280,256]{2,1,0:T(8,128)(2,1)S(1)}, bf16[2,1280,256]{2,1,0:T(8,128)(2,1)}, u32[]{:S(2)}, u32[]{:S(2)}) collective-permute-start(bf16[2,1280,256]{2,1,0:T(8,128)(2,1)S(1)} %slice.151), channel_id=1, source_target_pairs={{0,16},{4,20},{8,24},{12,28},{16,0},{20,4},{24,8},{28,12},{1,17},{... | collective-permute-start | bytes 3932168 | tf_op jit(solution)/shard_map/ppermute | solution.py:1091
  547.6 31.6 %collective-permute-start.28 = (bf16[2,256,1024]{2,1,0:T(8,128)(2,1)}, bf16[2,256,1024]{2,1,0:T(8,128)(2,1)}, u32[]{:S(2)}, u32[]{:S(2)}) collective-permute-start(bf16[2,256,1024]{2,1,0:T(8,128)(2,1)} %slice.174), channel_id=1, source_target_pairs={{0,16},{4,20},{8,24},{12,28},{16,0},{20,4},{24,8},{28,12},{1,17},{... | collective-permute-start | bytes 3145736 | tf_op jit(solution)/shard_map/ppermute | solution.py:1091
  549.5 33.5 %collective-permute-start.26 = (bf16[2,256,1024]{2,1,0:T(8,128)(2,1)}, bf16[2,256,1024]{2,1,0:T(8,128)(2,1)}, u32[]{:S(2)}, u32[]{:S(2)}) collective-permute-start(bf16[2,256,1024]{2,1,0:T(8,128)(2,1)} %slice.170), channel_id=1, source_target_pairs={{0,8},{4,12},{8,0},{12,4},{16,24},{20,28},{24,16},{28,20},{1,9},{5... | collective-permute-start | bytes 3145736 | tf_op jit(solution)/shard_map/ppermute | solution.py:1091
  556.5 35.8 %collective-permute-start.25 = (bf16[1,1280,256]{2,1,0:T(8,128)(2,1)}, bf16[1,1280,256]{2,1,0:T(8,128)(2,1)}, u32[]{:S(2)}, u32[]{:S(2)}) collective-permute-start(bf16[1,1280,256]{2,1,0:T(8,128)(2,1)} %slice.189), channel_id=1, source_target_pairs={{0,16},{4,20},{8,24},{12,28},{16,0},{20,4},{24,8},{28,12},{1,17},{... | collective-permute-start | bytes 1966088 | tf_op jit(solution)/shard_map/ppermute | solution.py:1091
  559.1 34.4 %collective-permute-start.30 = (bf16[1,1280,256]{2,1,0:T(8,128)(2,1)}, bf16[1,1280,256]{2,1,0:T(8,128)(2,1)S(1)}, u32[]{:S(2)}, u32[]{:S(2)}) collective-permute-start(bf16[1,1280,256]{2,1,0:T(8,128)(2,1)} %slice.193), channel_id=1, source_target_pairs={{0,8},{4,12},{8,0},{12,4},{16,24},{20,28},{24,16},{28,20},{1,9},{5... | collective-permute-start | bytes 1966088 | tf_op jit(solution)/shard_map/ppermute | solution.py:1091
  583.0 35.3 %collective-permute-start.29 = (bf16[1,256,1024]{2,1,0:T(8,128)(2,1)S(1)}, bf16[1,256,1024]{2,1,0:T(8,128)(2,1)S(1)}, u32[]{:S(2)}, u32[]{:S(2)}) collective-permute-start(bf16[1,256,1024]{2,1,0:T(8,128)(2,1)S(1)} %slice.192), channel_id=1, source_target_pairs={{0,8},{4,12},{8,0},{12,4},{16,24},{20,28},{24,16},{28,20},{1,9},{5... | collective-permute-start | bytes 1572872 | tf_op jit(solution)/shard_map/ppermute | solution.py:1091
  (24 other events, 403.4 us)
Sparse Core Ops, SparseCore 0:
  10.5 48.2 all-gather.6
  60.6 54.3 all-gather.8
  116.9 27.8 all-gather.10
  146.6 54.4 all-gather.12
  326.5 151.2 reduce-scatter.2
  483.9 143.9 reduce-scatter.4

commit v4 on v3

--- a/solution.py
+++ b/solution.py
@@ -1205,6 +1205,10 @@
             shard = me + (-s, s)[direction]
             cot_shards += [shard, shard]
             cot_there += [(shard >= 0) & (shard < n) & jnp.logical_not(at_end), at_end]
+    if n == 4:
+        table = jnp.array([[-1, 0, 3, -1], [-1, 2, 1, -1], [1, -1, -1, 2], [2, -1, -1, 1], [-1, 3, 0, -1]])[:, me]
+        cot_shards = [me] + [table[k] for k in range(5)]
+        cot_there = [x >= 0 for x in cot_shards]
     cot_early = places_of(cot_shards, cot_there)
 
     bits = [b for b in range(1, pieces.bit_length() - 1)]
@@ -1273,28 +1277,43 @@
         right, left = pair
         return [shift(right, [(n - 2, n - 1)]), shift(left, [(1, 0)])]
 
-    inner = [inner_step([after(cotangent, *normed_in[-2], early_qkv)] * 2, 1)]
-    ready = after(tuple(inner[0]), *normed_in[-1], act)
-    ends = [end_step([after(cotangent, *ready)] * 2)]
-    inner.append(inner_step(ready, 2))
-    cot_from = [cotangent]
+    soon = after(cotangent, *normed_in[-2], early_qkv)
+    if n == 4:
+        cross, out = [(1, 2), (2, 1)], [(2, 3), (1, 0)]
+        outside, across = shift(soon, [(0, 1), (3, 2)]), shift(soon, cross)
+        outside, across = after((outside, across), *normed_in[-1], act)
+        near = shift(after(cotangent, outside), out)
+        next_ = shift(across, out)
+        over = shift(outside, cross)
+        cot_from = [cotangent, outside, across, near, next_, over]
+    else:
+        inner = [inner_step([soon] * 2, 1)]
+        ready = after(tuple(inner[0]), *normed_in[-1], act)
+        ends = [end_step([after(cotangent, *ready)] * 2)]
+        inner.append(inner_step(ready, 2))
+        cot_from = [cotangent]
     normed, qkv, act, slope = forward_chunk(late, normed_in[-1], *project, (normed, qkv, act, slope), n)
 
-    att_half = attend(qkv, segc, segr, first, 0, 2, None)
-    ends.append(end_step(after(tuple(ready), *ends[0], *inner[1], att_half[0])))
-    att, lse = attend(qkv, segc, segr, first, 1, 2, att_half)
-    for s in range(3, n):
-        ready = after(tuple(inner[-1]), att)
-        ends.append(end_step(ready))
-        if s < n - 1:
-            inner.append(inner_step(ready, s))
-    for s in range(1, n - 1):
-        for direction in range(2):
-            cot_from += [inner[s - 1][direction], ends[s - 1][direction]]
+    if n == 4:
+        att, lse = attend(qkv, segc, segr, first, 0, 1, None)
+        last_in = [shift(after(over, att), out)] * 2
+    else:
+        att_half = attend(qkv, segc, segr, first, 0, 2, None)
+        ends.append(end_step(after(tuple(ready), *ends[0], *inner[1], att_half[0])))
+        att, lse = attend(qkv, segc, segr, first, 1, 2, att_half)
+        for s in range(3, n):
+            ready = after(tuple(inner[-1]), att)
+            ends.append(end_step(ready))
+            if s < n - 1:
+                inner.append(inner_step(ready, s))
+        for s in range(1, n - 1):
+            for direction in range(2):
+                cot_from += [inner[s - 1][direction], ends[s - 1][direction]]
+        last_in = ends[-1]
     part = mix(att, act, w_out, w_down)
     bufs = backward_early(after(cot_early, part), cot_from, w_out, w_down, slope, n)
-    block_sum = line_sum(after(part, bufs[2], *ends[-1]))
-    cot, grad_att, grad_hid = backward_chunk(late, ends[-1], w_out, w_down, slope, bufs, n)
+    block_sum = line_sum(after(part, bufs[2], *last_in))
+    cot, grad_att, grad_hid = backward_chunk(late, last_in, w_out, w_down, slope, bufs, n)
     orders = (bits, bits[::-1])
 
     def finish(pair, axis, *marks):
@@ -1322,8 +1341,8 @@
     up_pair = halve([after(u, qkv_pair[0]) for u in up_pair], orders, 0, up_pair)
     qkv_kept = qkv_pair[0]
     qkv_pair = halve(qkv_pair, orders, 0)
-    mixed = mixed_out(tokens, after(block_sum, *qkv_pair), (out_bias + fc2_bias)[None])
-    input_grad, sums = norm_back(tokens, after(cotangent, mixed), [grad_sum], ln_gain[None])
+    mixed = mixed_out(tokens, after(block_sum, qkv_kept), (out_bias + fc2_bias)[None])
+    input_grad, sums = norm_back(tokens, after(cotangent, mixed, *qkv_pair), [grad_sum], ln_gain[None])
     common = 3 * depth // 128
     pack = jnp.concatenate([a.reshape(-1, 128) for a in (sums[:3], up_sum[0], qkv_sum[0])])
     pack = jnp.pad(pack, ((0, -pack.shape[0] % 8), (0, 0)))

time: 678 us -> 663 us (0.978)
  starting transfers between devices: 54.8 us -> 42 us
  waiting for transfers between devices: 114 us -> 105 us
    reduce_scatter x2, starting transfers between devices: 8.56 us -> 0.21 us  [line_sum(): return lax.psum_scatter(x, 'tensor', scatter_dimension=0, tiled=True)]
    ppermute x16 -> x12, starting transfers between devices: 32.7 us -> 25 us  [shift(): return lax.ppermute(x, 'tensor', pairs)]
    pallas_call x2 -> x1, Pallas kernels: 46 us -> 42 us  [attend(): pl.pallas_call(functools.partial(attend_kernel, skipped), grid_spec=pltpu...]
    ppermute x16 -> x12, waiting for transfers between devices: 74.1 us -> 70.5 us  [shift(): return lax.ppermute(x, 'tensor', pairs)]
  transfers between devices with their start and end apart: 37 -> 33, of which waited for: 13 -> 13; matrix products, arithmetic and copies ran while one was open for 7% -> 8% of each run, Pallas kernels for 60% -> 61%
where the time goes in v4:
time: 663 us; the launch traced here: 652 us
  Pallas kernels  425 us (64%)
  waiting for transfers between devices  105 us (16%)
  starting transfers between devices  42 us (6%)
  local copies, waits for them, and re-layouts  32.2 us (5%)
  other arithmetic  30.2 us (5%)
  between operations  18.2 us (3%)
    ppermute x12, waiting for transfers between devices, shift(): return lax.ppermute(x, 'tensor', pairs)  70.5 us
    pallas_call x1, Pallas kernels, attend_back(): pl.pallas_call(attend_back_kernel, grid_spec=pltpu.PrefetchScalarGridSpec...  60.5 us
    pallas_call x1, Pallas kernels, attend(): pl.pallas_call(functools.partial(attend_kernel, skipped), grid_spec=pltpu...  42 us
    pallas_call x1, Pallas kernels, grad_normed(): pl.pallas_call(grad_kernel, grid=((stop - start) // tile,), in_specs=[onc...  39.2 us
    pallas_call x2, Pallas kernels, row_grads(): pl.pallas_call(functools.partial(rows_keep_kernel, len(gs)), grid_spec=pl...  32.9 us
    ppermute x15, waiting for transfers between devices, swap(): return lax.ppermute(x, 'dp', [(i, i ^ 1 << bit) for i in range(size)])  32.2 us
    pallas_call x2, Pallas kernels, row_grads(): pl.pallas_call(functools.partial(rows_send_kernel, len(gs)), grid_spec=pl...  31 us
    pallas_call x1, Pallas kernels, backward_early(): pl.pallas_call(functools.partial(backward_early_kernel, len(cots), parts)...  28.9 us
  transfers between devices with their start and end apart: 33, of which 13 were waited for; matrix products, arithmetic and copies ran while one was open for 8% of the time, Pallas kernels for 61%

profile of v4, /device:TPU:0, one launch (start us, length us, event | category | flops | bytes accessed | tf_op | source)
XLA Modules:
  0.0 652.4 jit_solution(1311633727875766340)
XLA Ops:
  12.0 3.7 norm.1.refs_0_
  15.7 5.0 collective-permute-start
  29.1 3.2 stack.199
  36.9 28.9 %collective-permute-done.refs_1_ = bf16[512,2048]{1,0:T(8,128)(2,1)S(1)} collective-permute-done((bf16[512,2048]{1,0:T(8,128)(2,1)}, bf16[512,2048]{1,0:T(8,128)(2,1)S(1)}, u32[]{:S(2)}, u32[]{:S(2)}) %collective-permute-start) | collective-permute-done | bytes 2097184 | tf_op jit(solution)/shard_map/ppermute | solution.py:1171
  78.6 5.8 fusion
  84.3 16.8 %queries_early.1 = (bf16[2560,2048]{1,0:T(8,128)(2,1)}, bf16[2560,1536]{1,0:T(8,128)(2,1)}) custom-call(s32[11]{0:T(128)} %pad_add_fusion.7.where_ref, bf16[512,2048]{1,0:T(8,128)(2,1)} %norm.1.refs_0_, bf16[512,2048]{1,0:T(8,128)(2,1)} %copy-done, bf16[512,2048]{1,0:T(8,128)(2,1)} %collective-permute-done.2.refs_2_, ...), custom_call_target="tpu_custom_call" | custom-call | flops 644245120 | bytes 314572 | tf_op jit(solution)/shard_map/queries_early/pallas_call | solution.py:415
  101.2 18.7 %collective-permute-done.3.refs_1_.refs_4_ = bf16[512,2048]{1,0:T(8,128)(2,1)} collective-permute-done((bf16[512,2048]{1,0:T(8,128)(2,1)}, bf16[512,2048]{1,0:T(8,128)(2,1)}, u32[]{:S(2)}, u32[]{:S(2)}) %collective-permute-start.3) | collective-permute-done | bytes 2097184 | tf_op jit(solution)/shard_map/ppermute | solution.py:1171
  119.8 3.8 collective-permute-start.6
  128.9 11.0 %queries_chunk.1 = (bf16[2560,2048]{1,0:T(8,128)(2,1)}, bf16[2560,1536]{1,0:T(8,128)(2,1)}) custom-call(s32[6]{0:T(128)} %stack.191.where_ref, bf16[512,2048]{1,0:T(8,128)(2,1)} %collective-permute-done.1.refs_0_.refs_3_, bf16[512,2048]{1,0:T(8,128)(2,1)} %collective-permute-done.3.refs_1_.refs_4_, ...), custom_call_target="tpu_custom_call", output_to_operand_aliasing={{0}: (8, {}), {1}: (9, {})} | custom-call | flops 161061280 | bytes 314572 | tf_op jit(solution)/shard_map/queries_chunk/pallas_call | solution.py:265
  139.9 28.7 %units_early.1 = (bf16[2560,2048]{1,0:T(8,128)(2,1)}, bf16[2560,2048]{1,0:T(8,128)(2,1)}) custom-call(s32[15]{0:T(128)} %pad_add_fusion.4.where_ref, bf16[512,2048]{1,0:T(8,128)(2,1)} %norm.1.refs_0_, bf16[512,2048]{1,0:T(8,128)(2,1)} %copy-done, bf16[512,2048]{1,0:T(8,128)(2,1)} %collective-permute-done.2.refs_2_, ...), custom_call_target="tpu_custom_call" | custom-call | flops 858993472 | bytes 419430 | tf_op jit(solution)/shard_map/units_early/pallas_call | solution.py:443
  168.6 6.2 collective-permute-done.5.refs_1_
  181.3 21.2 %forward_chunk.1 = (bf16[2560,2048]{1,0:T(8,128)(2,1)}, bf16[2560,1536]{1,0:T(8,128)(2,1)}, bf16[2560,2048]{1,0:T(8,128)(2,1)}, bf16[2560,2048]{1,0:T(8,128)(2,1)}) custom-call(s32[6]{0:T(128)} %stack.186.where_ref, bf16[512,2048]{1,0:T(8,128)(2,1)} %collective-permute-done.4.refs_0_, ...), custom_call_target="tpu_custom_call", output_to_operand_aliasing={{0}: (10, {}), {1}: (11, {}), {2}: (12, {}), {3}: (13, {})} | custom-call | flops 375809632 | bytes 734003 | tf_op jit(solution)/shard_map/forward_chunk/pallas_call | solution.py:322
  202.5 42.0 %attend.1 = (bf16[2048,512]{1,0:T(8,128)(2,1)}, f32[4,8,2048]{2,1,0:T(8,128)}) custom-call(s32[8]{0:T(128)} %and_select_fusion.2.first_ref, bf16[2560,1536]{1,0:T(8,128)(2,1)} %get-tuple-element.107.q_ref.k_ref.v_ref, bf16[2560,1536]{1,0:T(8,128)(2,1)} %get-tuple-element.107.q_ref.k_ref.v_ref, bf16[2560,1536]{1,0:T(8,128)(2,1)} %get-tuple-element.107.q_ref.k_ref.v_ref, ...), custom_call_target="tpu_custom_call" | custom-call | flops 1500000000 | bytes 419430 | tf_op jit(solution)/shard_map/attend/pallas_call | solution.py:608
  245.8 28.7 %mix.1 = bf16[2048,2048]{1,0:T(8,128)(2,1)} custom-call(bf16[2048,512]{1,0:T(8,128)(2,1)} %get-tuple-element.108.att_ref.o_ref, bf16[2560,2048]{1,0:T(8,128)(2,1)} %get-tuple-element.109.act_ref, bf16[8,512,256]{2,1,0:T(8,128)(2,1)} %bitcast.92, bf16[8,2048,256]{2,1,0:T(8,128)(2,1)} %bitcast.89), custom_call_target="tpu_custom_call" | custom-call | flops 1073741824 | bytes 838860 | tf_op jit(solution)/shard_map/mix/pallas_call | solution.py:784
  276.3 28.9 %backward_early.1 = (bf16[2560,2048]{1,0:T(8,128)(2,1)}, bf16[2560,512]{1,0:T(8,128)(2,1)}, bf16[2560,2048]{1,0:T(8,128)(2,1)}) custom-call(s32[17]{0:T(128)} %pad_add_fusion.5.where_ref, bf16[512,2048]{1,0:T(8,128)(2,1)} %cot_ref, bf16[512,2048]{1,0:T(8,128)(2,1)} %copy-done.6, bf16[512,2048]{1,0:T(8,128)(2,1)} %collective-permute-done.7.refs_2_, ...), custom_call_target="tpu_custom_call" | custom-call | flops 1073741824 | bytes 524288 | tf_op jit(solution)/shard_map/backward_early/pallas_call | solution.py:510
  305.2 12.6 %collective-permute-done.11.refs_0_.refs_1_ = bf16[512,2048]{1,0:T(8,128)(2,1)S(1)} collective-permute-done((bf16[512,2048]{1,0:T(8,128)(2,1)}, bf16[512,2048]{1,0:T(8,128)(2,1)S(1)}, u32[]{:S(2)}, u32[]{:S(2)}) %collective-permute-start.11) | collective-permute-done | bytes 2097184 | tf_op jit(solution)/shard_map/ppermute | solution.py:1171
  319.3 14.5 %backward_chunk.1 = (bf16[2560,2048]{1,0:T(8,128)(2,1)}, bf16[2560,512]{1,0:T(8,128)(2,1)}, bf16[2560,2048]{1,0:T(8,128)(2,1)}) custom-call(s32[6]{0:T(128)} %stack.186.where_ref, bf16[512,2048]{1,0:T(8,128)(2,1)} %copy-done.1, bf16[512,2048]{1,0:T(8,128)(2,1)} %copy-done.1, ...), custom_call_target="tpu_custom_call", output_to_operand_aliasing={{0}: (6, {}), {1}: (7, {}), {2}: (8, {})} | custom-call | flops 268435456 | bytes 524288 | tf_op jit(solution)/shard_map/backward_chunk/pallas_call | solution.py:870
  333.8 18.0 %columns_send.1 = bf16[4,2560,256]{2,1,0:T(8,128)(2,1)} custom-call(s32[4]{0:T(128)} %broadcast_xor_fusion.1.where_ref, bf16[2048,512]{1,0:T(8,128)(2,1)} %get-tuple-element.108.att_ref.o_ref, bf16[2560,2048]{1,0:T(8,128)(2,1)} %get-tuple-element.109.act_ref, bf16[2560,2048]{1,0:T(8,128)(2,1)} %get-tuple-element.134.c_ref), custom_call_target="tpu_custom_call" | custom-call | flops 536870912 | bytes 524288 | tf_op jit(solution)/shard_map/columns_send/pallas_call | solution.py:1009
  351.8 16.2 %rows_send.2 = (bf16[4,256,2048]{2,1,0:T(8,128)(2,1)}, f32[8,2048]{1,0:T(8,128)}) custom-call(s32[4]{0:T(128)} %broadcast_xor_fusion.1.where_ref, bf16[2560,2048]{1,0:T(8,128)(2,1)} %get-tuple-element.145.x_ref, bf16[2560,2048]{1,0:T(8,128)(2,1)} %get-tuple-element.140.refs_0_.gh_ref), custom_call_target="tpu_custom_call" | custom-call | flops 429496736 | bytes 419430 | tf_op jit(solution)/shard_map/rows_send/pallas_call | solution.py:1047
  368.4 60.5 %attend_back.1 = (bf16[2048,512]{1,0:T(8,128)(2,1)}, bf16[2048,512]{1,0:T(8,128)(2,1)}, bf16[2048,512]{1,0:T(8,128)(2,1)}) custom-call(s32[8]{0:T(128)} %and_select_fusion.2.first_ref, bf16[2560,1536]{1,0:T(8,128)(2,1)} %get-tuple-element.107.q_ref.k_ref.v_ref, bf16[2560,1536]{1,0:T(8,128)(2,1)} %get-tuple-element.107.q_ref.k_ref.v_ref, ...), custom_call_target="tpu_custom_call" | custom-call | flops 2200000000 | bytes 1048576 | tf_op jit(solution)/shard_map/attend_back/pallas_call | solution.py:735
  429.0 39.2 %grad_normed.1 = bf16[2048,2048]{1,0:T(8,128)(2,1)} custom-call(bf16[2048,512]{1,0:T(8,128)(2,1)} %get-tuple-element.136.gq_ref.refs_0_, bf16[2048,512]{1,0:T(8,128)(2,1)} %get-tuple-element.137.gk_ref.refs_1_, bf16[2048,512]{1,0:T(8,128)(2,1)} %get-tuple-element.138.gv_ref.refs_2_, bf16[2560,2048]{1,0:T(8,128)(2,1)} %get-tuple-element.140.refs_0_.gh_ref, ...), custom_call_target="tpu_custom_call" | custom-call | flops 1503238528 | bytes 838860 | tf_op jit(solution)/shard_map/grad_normed/pallas_call | solution.py:903
  468.2 20.1 %columns_keep.1 = (bf16[4,1280,256]{2,1,0:T(8,128)(2,1)}, bf16[4,1280,256]{2,1,0:T(8,128)(2,1)}) custom-call(s32[16]{0:T(128)} %pad_add_fusion.6.where_ref, bf16[2048,512]{1,0:T(8,128)(2,1)} %get-tuple-element.108.att_ref.o_ref, bf16[2560,2048]{1,0:T(8,128)(2,1)} %get-tuple-element.109.act_ref, bf16[2560,2048]{1,0:T(8,128)(2,1)} %get-tuple-element.134.c_ref, ...), custom_call_target="tpu_custom_call" | custom-call | flops 536870912 | bytes 524288 | tf_op jit(solution)/shard_map/columns_keep/pallas_call | solution.py:1023
  488.3 14.8 %rows_send.3 = (bf16[4,256,1536]{2,1,0:T(8,128)(2,1)}, f32[8,1536]{1,0:T(8,128)}) custom-call(s32[4]{0:T(128)} %broadcast_xor_fusion.1.where_ref, bf16[2560,2048]{1,0:T(8,128)(2,1)} %get-tuple-element.145.x_ref, bf16[2048,512]{1,0:T(8,128)(2,1)} %get-tuple-element.136.gq_ref.refs_0_, bf16[2048,512]{1,0:T(8,128)(2,1)} %get-tuple-element.137.gk_ref.refs_1_, ...), custom_call_target="tpu_custom_call" | custom-call | flops 322122560 | bytes 314572 | tf_op jit(solution)/shard_map/rows_send/pallas_call | solution.py:1047
  510.1 17.2 %rows_keep.2 = (bf16[4,256,1024]{2,1,0:T(8,128)(2,1)}, bf16[4,256,1024]{2,1,0:T(8,128)(2,1)}) custom-call(s32[16]{0:T(128)} %pad_add_fusion.6.where_ref, bf16[2560,2048]{1,0:T(8,128)(2,1)} %get-tuple-element.145.x_ref, bf16[2560,2048]{1,0:T(8,128)(2,1)} %get-tuple-element.140.refs_0_.gh_ref, bf16[4,256,2048]{2,1,0:T(8,128)(2,1)} %collective-permute-done.13.refs_1_), custom_call_target="tpu_custom_call" | custom-call | flops 429496736 | bytes 419430 | tf_op jit(solution)/shard_map/rows_keep/pallas_call | solution.py:1067
  544.9 15.7 %rows_keep.3 = (bf16[4,256,768]{2,1,0:T(8,128)(2,1)}, bf16[4,256,768]{2,1,0:T(8,128)(2,1)}) custom-call(s32[16]{0:T(128)} %pad_add_fusion.6.where_ref, bf16[2560,2048]{1,0:T(8,128)(2,1)} %get-tuple-element.145.x_ref, bf16[2048,512]{1,0:T(8,128)(2,1)} %get-tuple-element.136.gq_ref.refs_0_, bf16[2048,512]{1,0:T(8,128)(2,1)} %get-tuple-element.137.gk_ref.refs_1_, ...), custom_call_target="tpu_custom_call" | custom-call | flops 322122560 | bytes 314572 | tf_op jit(solution)/shard_map/rows_keep/pallas_call | solution.py:1067
  569.0 5.9 collective-permute-done.21
  580.7 11.0 %collective-permute-done.18 = bf16[2,256,768]{2,1,0:T(8,128)(2,1)S(1)} collective-permute-done((bf16[2,256,768]{2,1,0:T(8,128)(2,1)S(1)}, bf16[2,256,768]{2,1,0:T(8,128)(2,1)S(1)}, u32[]{:S(2)}, u32[]{:S(2)}) %collective-permute-start.18) | collective-permute-done | bytes 786464 | tf_op jit(solution)/shard_map/ppermute | solution.py:1091
  595.2 5.6 collective-permute-done.25
  604.6 4.2 collective-permute-done.20
  612.5 3.5 mixed_out.1
  616.0 7.0 %norm_back.1 = (bf16[512,2048]{1,0:T(8,128)(2,1)}, f32[8,2048]{1,0:T(8,128)}) custom-call(bf16[512,2048]{1,0:T(8,128)(2,1)} %x_ref.5, bf16[512,2048]{1,0:T(8,128)(2,1)} %cot_ref, bf16[512,2048]{1,0:T(8,128)(2,1)} %reduce-scatter.5.cloned.1.call-done.refs_0_, f32[1,2048]{1,0:T(1,128)} %bitcast.104), custom_call_target="tpu_custom_call" | custom-call | flops 1048576 | bytes 629145 | tf_op jit(solution)/shard_map/norm_back/pallas_call | solution.py:127
  624.4 17.4 %small_sums.1 = f32[80,128]{1,0:T(8,128)} custom-call(f32[80,128]{1,0:T(8,128)} %select_maximum_fusion.x_ref), custom_call_target="tpu_custom_call" | custom-call | tf_op jit(solution)/shard_map/small_sums/pallas_call | solution.py:1143
  (198 shorter events, 98.1 us)
Async XLA Ops:
  7.2 77.1 %all-gather.7.cloned.1.call-start = ((), (), s32[]{:S(2)}) async-start(), calls=%async_computation.2 | async-start | bytes 7077888 | tf_op jit(solution)/shard_map/all_gather | solution.py:1228
  9.8 130.1 %all-gather.9.cloned.1.call-start = ((), (), s32[]{:S(2)}) async-start(), calls=%async_computation.3 | async-start | bytes 9437184 | tf_op jit(solution)/shard_map/all_gather | solution.py:1229
  10.6 235.2 %all-gather.11.cloned.1.call-start = ((), (), s32[]{:S(2)}) async-start(), calls=%async_computation.6 | async-start | bytes 2359296 | tf_op jit(solution)/shard_map/all_gather | solution.py:1230
  11.3 234.5 %all-gather.13.cloned.1.call-start = ((), (), s32[]{:S(2)}) async-start(), calls=%async_computation.7 | async-start | bytes 9437184 | tf_op jit(solution)/shard_map/all_gather | solution.py:1231
  11.9 456.3 %reduce-scatter.3.cloned.1.call-start = ((), (), s32[]{:S(2)}) async-start(), calls=%async_computation.4 | async-start | bytes 10485760 | tf_op jit(solution)/shard_map/reduce_scatter | solution.py:1248
  15.7 50.1 %collective-permute-start = (bf16[512,2048]{1,0:T(8,128)(2,1)}, bf16[512,2048]{1,0:T(8,128)(2,1)S(1)}, u32[]{:S(2)}, u32[]{:S(2)}) collective-permute-start(bf16[512,2048]{1,0:T(8,128)(2,1)} %norm.1.refs_0_), channel_id=1, source_target_pairs={{0,1},{1,2},{2,3},{4,5},{5,6},{6,7},{8,9},{9,10},{10,11},{12,13},{... | collective-permute-start | bytes 6291464 | tf_op jit(solution)/shard_map/ppermute | solution.py:1171
  20.8 49.3 %collective-permute-start.2 = (bf16[512,2048]{1,0:T(8,128)(2,1)}, bf16[512,2048]{1,0:T(8,128)(2,1)}, u32[]{:S(2)}, u32[]{:S(2)}) collective-permute-start(bf16[512,2048]{1,0:T(8,128)(2,1)} %norm.1.refs_0_), channel_id=1, source_target_pairs={{1,0},{2,1},{3,2},{5,4},{6,5},{7,6},{9,8},{10,9},{11,10},{13,12},{... | collective-permute-start | bytes 6291464 | tf_op jit(solution)/shard_map/ppermute | solution.py:1171
  65.8 35.3 %collective-permute-start.1 = (bf16[512,2048]{1,0:T(8,128)(2,1)S(1)}, bf16[512,2048]{1,0:T(8,128)(2,1)}, u32[]{:S(2)}, u32[]{:S(2)}) collective-permute-start(bf16[512,2048]{1,0:T(8,128)(2,1)S(1)} %collective-permute-done.refs_1_), channel_id=1, source_target_pairs={{1,2},{2,3},{5,6},{6,7},{9,10},{10,11},{13,14},{14,15},{17,18},{18... | collective-permute-start | bytes 6291464 | tf_op jit(solution)/shard_map/ppermute | solution.py:1171
  70.1 49.8 %collective-permute-start.3 = (bf16[512,2048]{1,0:T(8,128)(2,1)}, bf16[512,2048]{1,0:T(8,128)(2,1)}, u32[]{:S(2)}, u32[]{:S(2)}) collective-permute-start(bf16[512,2048]{1,0:T(8,128)(2,1)} %collective-permute-done.2.refs_2_), channel_id=1, source_target_pairs={{1,0},{2,1},{5,4},{6,5},{9,8},{10,9},{13,12},{14,13},{17,16},{18,1... | collective-permute-start | bytes 6291464 | tf_op jit(solution)/shard_map/ppermute | solution.py:1171
  119.8 48.8 %collective-permute-start.6 = (bf16[512,2048]{1,0:T(8,128)(2,1)}, bf16[512,2048]{1,0:T(8,128)(2,1)S(1)}, u32[]{:S(2)}, u32[]{:S(2)}) collective-permute-start(bf16[512,2048]{1,0:T(8,128)(2,1)} %cot_ref), channel_id=1, source_target_pairs={{0,1},{3,2},{4,5},{7,6},{8,9},{11,10},{12,13},{15,14},{16,17},{19,... | collective-permute-start | bytes 6291464 | tf_op jit(solution)/shard_map/ppermute | solution.py:1171
  123.6 45.0 %collective-permute-start.7 = (bf16[512,2048]{1,0:T(8,128)(2,1)}, bf16[512,2048]{1,0:T(8,128)(2,1)}, u32[]{:S(2)}, u32[]{:S(2)}) collective-permute-start(bf16[512,2048]{1,0:T(8,128)(2,1)} %cot_ref), channel_id=1, source_target_pairs={{1,2},{2,1},{5,6},{6,5},{9,10},{10,9},{13,14},{14,13},{17,18},{18,... | collective-permute-start | bytes 6291464 | tf_op jit(solution)/shard_map/ppermute | solution.py:1171
  125.6 43.0 %collective-permute-start.4 = (bf16[512,2048]{1,0:T(8,128)(2,1)}, bf16[512,2048]{1,0:T(8,128)(2,1)}, u32[]{:S(2)}, u32[]{:S(2)}) collective-permute-start(bf16[512,2048]{1,0:T(8,128)(2,1)} %collective-permute-done.1.refs_0_.refs_3_), channel_id=1, source_target_pairs={{2,3},{6,7},{10,11},{14,15},{18,19},{22,23},{26,27},{30,31}} | collective-permute-start | bytes 6291464 | tf_op jit(solution)/shard_map/ppermute | solution.py:1171
  127.6 47.3 %collective-permute-start.5 = (bf16[512,2048]{1,0:T(8,128)(2,1)}, bf16[512,2048]{1,0:T(8,128)(2,1)}, u32[]{:S(2)}, u32[]{:S(2)}) collective-permute-start(bf16[512,2048]{1,0:T(8,128)(2,1)} %collective-permute-done.3.refs_1_.refs_4_), channel_id=1, source_target_pairs={{1,0},{5,4},{9,8},{13,12},{17,16},{21,20},{25,24},{29,28}} | collective-permute-start | bytes 6291464 | tf_op jit(solution)/shard_map/ppermute | solution.py:1171
  174.9 69.6 %collective-permute-start.10 = (bf16[512,2048]{1,0:T(8,128)(2,1)S(1)}, bf16[512,2048]{1,0:T(8,128)(2,1)}, u32[]{:S(2)}, u32[]{:S(2)}) collective-permute-start(bf16[512,2048]{1,0:T(8,128)(2,1)S(1)} %collective-permute-done.6.refs_1_), channel_id=1, source_target_pairs={{1,2},{2,1},{5,6},{6,5},{9,10},{10,9},{13,14},{14,13},{17,18},{18,... | collective-permute-start | bytes 6291464 | tf_op jit(solution)/shard_map/ppermute | solution.py:1171
  178.2 96.3 %collective-permute-start.8 = (bf16[512,2048]{1,0:T(8,128)(2,1)}, bf16[512,2048]{1,0:T(8,128)(2,1)}, u32[]{:S(2)}, u32[]{:S(2)}) collective-permute-start(bf16[512,2048]{1,0:T(8,128)(2,1)} %cot_ref), channel_id=1, source_target_pairs={{2,3},{1,0},{6,7},{5,4},{10,11},{9,8},{14,15},{13,12},{18,19},{17,... | collective-permute-start | bytes 6291464 | tf_op jit(solution)/shard_map/ppermute | solution.py:1171
  179.5 96.8 %collective-permute-start.9 = (bf16[512,2048]{1,0:T(8,128)(2,1)}, bf16[512,2048]{1,0:T(8,128)(2,1)}, u32[]{:S(2)}, u32[]{:S(2)}) collective-permute-start(bf16[512,2048]{1,0:T(8,128)(2,1)} %collective-permute-done.7.refs_2_), channel_id=1, source_target_pairs={{2,3},{1,0},{6,7},{5,4},{10,11},{9,8},{14,15},{13,12},{18,19},{17,... | collective-permute-start | bytes 6291464 | tf_op jit(solution)/shard_map/ppermute | solution.py:1171
  244.5 73.3 %collective-permute-start.11 = (bf16[512,2048]{1,0:T(8,128)(2,1)}, bf16[512,2048]{1,0:T(8,128)(2,1)S(1)}, u32[]{:S(2)}, u32[]{:S(2)}) collective-permute-start(bf16[512,2048]{1,0:T(8,128)(2,1)} %collective-permute-done.10.refs_5_), channel_id=1, source_target_pairs={{2,3},{1,0},{6,7},{5,4},{10,11},{9,8},{14,15},{13,12},{18,19},{17,... | collective-permute-start | bytes 6291464 | tf_op jit(solution)/shard_map/ppermute | solution.py:1171
  319.1 296.9 %reduce-scatter.5.cloned.1.call-start = ((), (), s32[]{:S(2)}) async-start(), calls=%async_computation.5 | async-start | bytes 10485760 | tf_op jit(solution)/shard_map/reduce_scatter | solution.py:1248
  351.8 77.2 %collective-permute-start.12 = (bf16[4,2560,256]{2,1,0:T(8,128)(2,1)}, bf16[4,2560,256]{2,1,0:T(8,128)(2,1)}, u32[]{:S(2)}, u32[]{:S(2)}) collective-permute-start(bf16[4,2560,256]{2,1,0:T(8,128)(2,1)} %columns_send.1), channel_id=1, source_target_pairs={{0,4},{4,0},{8,12},{12,8},{16,20},{20,16},{24,28},{28,24},{1,5},{5... | collective-permute-start | bytes 15728648 | tf_op jit(solution)/shard_map/ppermute | solution.py:1091
  368.0 61.0 %collective-permute-start.13 = (bf16[4,256,2048]{2,1,0:T(8,128)(2,1)}, bf16[4,256,2048]{2,1,0:T(8,128)(2,1)}, u32[]{:S(2)}, u32[]{:S(2)}) collective-permute-start(bf16[4,256,2048]{2,1,0:T(8,128)(2,1)} %get-tuple-element.132), channel_id=1, source_target_pairs={{0,4},{4,0},{8,12},{12,8},{16,20},{20,16},{24,28},{28,24},{1,5},{5... | collective-permute-start | bytes 12582920 | tf_op jit(solution)/shard_map/ppermute | solution.py:1091
  503.1 41.8 %collective-permute-start.16 = (bf16[4,256,1536]{2,1,0:T(8,128)(2,1)}, bf16[4,256,1536]{2,1,0:T(8,128)(2,1)}, u32[]{:S(2)}, u32[]{:S(2)}) collective-permute-start(bf16[4,256,1536]{2,1,0:T(8,128)(2,1)} %get-tuple-element.146), channel_id=1, source_target_pairs={{0,4},{4,0},{8,12},{12,8},{16,20},{20,16},{24,28},{28,24},{1,5},{5... | collective-permute-start | bytes 9437192 | tf_op jit(solution)/shard_map/ppermute | solution.py:1091
  504.4 31.9 %collective-permute-start.14 = (bf16[2,1280,256]{2,1,0:T(8,128)(2,1)}, bf16[2,1280,256]{2,1,0:T(8,128)(2,1)}, u32[]{:S(2)}, u32[]{:S(2)}) collective-permute-start(bf16[2,1280,256]{2,1,0:T(8,128)(2,1)} %slice.190), channel_id=1, source_target_pairs={{0,8},{4,12},{8,0},{12,4},{16,24},{20,28},{24,16},{28,20},{1,9},{5... | collective-permute-start | bytes 3932168 | tf_op jit(solution)/shard_map/ppermute | solution.py:1091
  505.9 36.1 %collective-permute-start.15 = (bf16[2,1280,256]{2,1,0:T(8,128)(2,1)S(1)}, bf16[2,1280,256]{2,1,0:T(8,128)(2,1)}, u32[]{:S(2)}, u32[]{:S(2)}) collective-permute-start(bf16[2,1280,256]{2,1,0:T(8,128)(2,1)S(1)} %slice.192), channel_id=1, source_target_pairs={{0,16},{4,20},{8,24},{12,28},{16,0},{20,4},{24,8},{28,12},{1,17},{... | collective-permute-start | bytes 3932168 | tf_op jit(solution)/shard_map/ppermute | solution.py:1091
  532.0 33.0 %collective-permute-start.24 = (bf16[2,256,1024]{2,1,0:T(8,128)(2,1)}, bf16[2,256,1024]{2,1,0:T(8,128)(2,1)}, u32[]{:S(2)}, u32[]{:S(2)}) collective-permute-start(bf16[2,256,1024]{2,1,0:T(8,128)(2,1)} %slice.215), channel_id=1, source_target_pairs={{0,16},{4,20},{8,24},{12,28},{16,0},{20,4},{24,8},{28,12},{1,17},{... | collective-permute-start | bytes 3145736 | tf_op jit(solution)/shard_map/ppermute | solution.py:1091
  532.1 35.0 %collective-permute-start.22 = (bf16[2,256,1024]{2,1,0:T(8,128)(2,1)}, bf16[2,256,1024]{2,1,0:T(8,128)(2,1)}, u32[]{:S(2)}, u32[]{:S(2)}) collective-permute-start(bf16[2,256,1024]{2,1,0:T(8,128)(2,1)} %slice.211), channel_id=1, source_target_pairs={{0,8},{4,12},{8,0},{12,4},{16,24},{20,28},{24,16},{28,20},{1,9},{5... | collective-permute-start | bytes 3145736 | tf_op jit(solution)/shard_map/ppermute | solution.py:1091
  539.0 35.9 %collective-permute-start.21 = (bf16[1,1280,256]{2,1,0:T(8,128)(2,1)}, bf16[1,1280,256]{2,1,0:T(8,128)(2,1)}, u32[]{:S(2)}, u32[]{:S(2)}) collective-permute-start(bf16[1,1280,256]{2,1,0:T(8,128)(2,1)} %slice.230), channel_id=1, source_target_pairs={{0,16},{4,20},{8,24},{12,28},{16,0},{20,4},{24,8},{28,12},{1,17},{... | collective-permute-start | bytes 1966088 | tf_op jit(solution)/shard_map/ppermute | solution.py:1091
  544.7 33.6 %collective-permute-start.26 = (bf16[1,1280,256]{2,1,0:T(8,128)(2,1)}, bf16[1,1280,256]{2,1,0:T(8,128)(2,1)S(1)}, u32[]{:S(2)}, u32[]{:S(2)}) collective-permute-start(bf16[1,1280,256]{2,1,0:T(8,128)(2,1)} %slice.234), channel_id=1, source_target_pairs={{0,8},{4,12},{8,0},{12,4},{16,24},{20,28},{24,16},{28,20},{1,9},{5... | collective-permute-start | bytes 1966088 | tf_op jit(solution)/shard_map/ppermute | solution.py:1091
  562.0 29.9 %collective-permute-start.17 = (bf16[2,256,768]{2,1,0:T(8,128)(2,1)S(1)}, bf16[2,256,768]{2,1,0:T(8,128)(2,1)S(1)}, u32[]{:S(2)}, u32[]{:S(2)}) collective-permute-start(bf16[2,256,768]{2,1,0:T(8,128)(2,1)S(1)} %slice.194), channel_id=1, source_target_pairs={{0,8},{4,12},{8,0},{12,4},{16,24},{20,28},{24,16},{28,20},{1,9},{5... | collective-permute-start | bytes 2359304 | tf_op jit(solution)/shard_map/ppermute | solution.py:1091
  565.0 26.7 %collective-permute-start.18 = (bf16[2,256,768]{2,1,0:T(8,128)(2,1)S(1)}, bf16[2,256,768]{2,1,0:T(8,128)(2,1)S(1)}, u32[]{:S(2)}, u32[]{:S(2)}) collective-permute-start(bf16[2,256,768]{2,1,0:T(8,128)(2,1)S(1)} %slice.196), channel_id=1, source_target_pairs={{0,16},{4,20},{8,24},{12,28},{16,0},{20,4},{24,8},{28,12},{1,17},{... | collective-permute-start | bytes 2359304 | tf_op jit(solution)/shard_map/ppermute | solution.py:1091
  567.0 33.8 %collective-permute-start.25 = (bf16[1,256,1024]{2,1,0:T(8,128)(2,1)S(1)}, bf16[1,256,1024]{2,1,0:T(8,128)(2,1)S(1)}, u32[]{:S(2)}, u32[]{:S(2)}) collective-permute-start(bf16[1,256,1024]{2,1,0:T(8,128)(2,1)S(1)} %slice.233), channel_id=1, source_target_pairs={{0,8},{4,12},{8,0},{12,4},{16,24},{20,28},{24,16},{28,20},{1,9},{5... | collective-permute-start | bytes 1572872 | tf_op jit(solution)/shard_map/ppermute | solution.py:1091
  574.9 28.0 %collective-permute-start.23 = (bf16[1,256,1024]{2,1,0:T(8,128)(2,1)S(1)}, bf16[1,256,1024]{2,1,0:T(8,128)(2,1)S(1)}, u32[]{:S(2)}, u32[]{:S(2)}) collective-permute-start(bf16[1,256,1024]{2,1,0:T(8,128)(2,1)S(1)} %slice.232), channel_id=1, source_target_pairs={{0,16},{4,20},{8,24},{12,28},{16,0},{20,4},{24,8},{28,12},{1,17},{... | collective-permute-start | bytes 1572872 | tf_op jit(solution)/shard_map/ppermute | solution.py:1091
  593.2 17.0 %collective-permute-start.19 = (bf16[1,256,768]{2,1,0:T(8,128)(2,1)S(1)}, bf16[1,256,768]{2,1,0:T(8,128)(2,1)S(1)}, u32[]{:S(2)}, u32[]{:S(2)}) collective-permute-start(bf16[1,256,768]{2,1,0:T(8,128)(2,1)S(1)} %slice.227), channel_id=1, source_target_pairs={{0,16},{4,20},{8,24},{12,28},{16,0},{20,4},{24,8},{28,12},{1,17},{... | collective-permute-start | bytes 1179656 | tf_op jit(solution)/shard_map/ppermute | solution.py:1091
  (20 other events, 307.1 us)
Sparse Core Ops, SparseCore 0:
  10.5 48.2 all-gather.6
  60.6 54.4 all-gather.8
  117.0 27.8 all-gather.10
  146.6 54.4 all-gather.12
  317.9 144.7 reduce-scatter.2
  468.3 146.1 reduce-scatter.4

commit v5 on v4

--- a/solution.py
+++ b/solution.py
@@ -1340,8 +1340,8 @@
     )
     up_pair = halve([after(u, qkv_pair[0]) for u in up_pair], orders, 0, up_pair)
     qkv_kept = qkv_pair[0]
-    qkv_pair = halve(qkv_pair, orders, 0)
     mixed = mixed_out(tokens, after(block_sum, qkv_kept), (out_bias + fc2_bias)[None])
+    qkv_pair = halve([after(half, mixed) for half in qkv_pair], orders, 0, qkv_pair)
     input_grad, sums = norm_back(tokens, after(cotangent, mixed, *qkv_pair), [grad_sum], ln_gain[None])
     common = 3 * depth // 128
     pack = jnp.concatenate([a.reshape(-1, 128) for a in (sums[:3], up_sum[0], qkv_sum[0])])

time: 663 us -> 662 us (level)
  waiting for transfers between devices: 105 us -> 95.5 us
    ppermute x15, waiting for transfers between devices: 32.2 us -> 22.2 us  [swap(): return lax.ppermute(x, 'dp', [(i, i ^ 1 << bit) for i in range(size)])]
  transfers between devices with their start and end apart: 33 -> 33, of which waited for: 13 -> 14; matrix products, arithmetic and copies ran while one was open for 8% -> 10% of each run, Pallas kernels for 61% -> 62%
where the time goes in v5:
time: 662 us; the launch traced here: 651 us
  Pallas kernels  426 us (64%)
  waiting for transfers between devices  95.5 us (14%)
  starting transfers between devices  39.9 us (6%)
  other arithmetic  35.9 us (5%)
  local copies, waits for them, and re-layouts  35 us (5%)
  between operations  18.3 us (3%)
    ppermute x12, waiting for transfers between devices, shift(): return lax.ppermute(x, 'tensor', pairs)  69.7 us
    pallas_call x1, Pallas kernels, attend_back(): pl.pallas_call(attend_back_kernel, grid_spec=pltpu.PrefetchScalarGridSpec...  60.5 us
    pallas_call x1, Pallas kernels, attend(): pl.pallas_call(functools.partial(attend_kernel, skipped), grid_spec=pltpu...  42 us
    pallas_call x1, Pallas kernels, grad_normed(): pl.pallas_call(grad_kernel, grid=((stop - start) // tile,), in_specs=[onc...  39.2 us
    pallas_call x2, Pallas kernels, row_grads(): pl.pallas_call(functools.partial(rows_keep_kernel, len(gs)), grid_spec=pl...  32.8 us
    pallas_call x2, Pallas kernels, row_grads(): pl.pallas_call(functools.partial(rows_send_kernel, len(gs)), grid_spec=pl...  31 us
    pallas_call x1, Pallas kernels, backward_early(): pl.pallas_call(functools.partial(backward_early_kernel, len(cots), parts)...  28.9 us
    pallas_call x1, Pallas kernels, units_early(): pl.pallas_call(functools.partial(units_early_kernel, len(xs), parts), gri...  28.7 us
  transfers between devices with their start and end apart: 33, of which 14 were waited for; matrix products, arithmetic and copies ran while one was open for 10% of the time, Pallas kernels for 62%

profile of v5, /device:TPU:0, one launch (start us, length us, event | category | flops | bytes accessed | tf_op | source)
XLA Modules:
  0.0 650.9 jit_solution(6893366295540143610)
XLA Ops:
  12.0 3.7 norm.1.refs_0_
  15.7 5.0 collective-permute-start
  29.2 3.3 stack.199
  37.1 28.8 %collective-permute-done.refs_1_ = bf16[512,2048]{1,0:T(8,128)(2,1)S(1)} collective-permute-done((bf16[512,2048]{1,0:T(8,128)(2,1)}, bf16[512,2048]{1,0:T(8,128)(2,1)S(1)}, u32[]{:S(2)}, u32[]{:S(2)}) %collective-permute-start) | collective-permute-done | bytes 2097184 | tf_op jit(solution)/shard_map/ppermute | solution.py:1171
  78.7 5.8 fusion
  84.5 17.2 %queries_early.1 = (bf16[2560,2048]{1,0:T(8,128)(2,1)}, bf16[2560,1536]{1,0:T(8,128)(2,1)}) custom-call(s32[11]{0:T(128)} %pad_add_fusion.7.where_ref, bf16[512,2048]{1,0:T(8,128)(2,1)} %norm.1.refs_0_, bf16[512,2048]{1,0:T(8,128)(2,1)} %copy-done, bf16[512,2048]{1,0:T(8,128)(2,1)} %collective-permute-done.2.refs_2_, ...), custom_call_target="tpu_custom_call" | custom-call | flops 644245120 | bytes 314572 | tf_op jit(solution)/shard_map/queries_early/pallas_call | solution.py:415
  101.6 18.2 %collective-permute-done.3.refs_1_.refs_4_ = bf16[512,2048]{1,0:T(8,128)(2,1)} collective-permute-done((bf16[512,2048]{1,0:T(8,128)(2,1)}, bf16[512,2048]{1,0:T(8,128)(2,1)}, u32[]{:S(2)}, u32[]{:S(2)}) %collective-permute-start.3) | collective-permute-done | bytes 2097184 | tf_op jit(solution)/shard_map/ppermute | solution.py:1171
  119.8 3.8 collective-permute-start.6
  128.9 11.0 %queries_chunk.1 = (bf16[2560,2048]{1,0:T(8,128)(2,1)}, bf16[2560,1536]{1,0:T(8,128)(2,1)}) custom-call(s32[6]{0:T(128)} %stack.191.where_ref, bf16[512,2048]{1,0:T(8,128)(2,1)} %collective-permute-done.1.refs_0_.refs_3_, bf16[512,2048]{1,0:T(8,128)(2,1)} %collective-permute-done.3.refs_1_.refs_4_, ...), custom_call_target="tpu_custom_call", output_to_operand_aliasing={{0}: (8, {}), {1}: (9, {})} | custom-call | flops 161061280 | bytes 314572 | tf_op jit(solution)/shard_map/queries_chunk/pallas_call | solution.py:265
  139.9 28.7 %units_early.1 = (bf16[2560,2048]{1,0:T(8,128)(2,1)}, bf16[2560,2048]{1,0:T(8,128)(2,1)}) custom-call(s32[15]{0:T(128)} %pad_add_fusion.4.where_ref, bf16[512,2048]{1,0:T(8,128)(2,1)} %norm.1.refs_0_, bf16[512,2048]{1,0:T(8,128)(2,1)} %copy-done, bf16[512,2048]{1,0:T(8,128)(2,1)} %collective-permute-done.2.refs_2_, ...), custom_call_target="tpu_custom_call" | custom-call | flops 858993472 | bytes 419430 | tf_op jit(solution)/shard_map/units_early/pallas_call | solution.py:443
  168.7 6.2 collective-permute-done.5.refs_1_
  181.3 21.3 %forward_chunk.1 = (bf16[2560,2048]{1,0:T(8,128)(2,1)}, bf16[2560,1536]{1,0:T(8,128)(2,1)}, bf16[2560,2048]{1,0:T(8,128)(2,1)}, bf16[2560,2048]{1,0:T(8,128)(2,1)}) custom-call(s32[6]{0:T(128)} %stack.186.where_ref, bf16[512,2048]{1,0:T(8,128)(2,1)} %collective-permute-done.4.refs_0_, ...), custom_call_target="tpu_custom_call", output_to_operand_aliasing={{0}: (10, {}), {1}: (11, {}), {2}: (12, {}), {3}: (13, {})} | custom-call | flops 375809632 | bytes 734003 | tf_op jit(solution)/shard_map/forward_chunk/pallas_call | solution.py:322
  202.6 42.0 %attend.1 = (bf16[2048,512]{1,0:T(8,128)(2,1)}, f32[4,8,2048]{2,1,0:T(8,128)}) custom-call(s32[8]{0:T(128)} %and_select_fusion.2.first_ref, bf16[2560,1536]{1,0:T(8,128)(2,1)} %get-tuple-element.109.q_ref.k_ref.v_ref, bf16[2560,1536]{1,0:T(8,128)(2,1)} %get-tuple-element.109.q_ref.k_ref.v_ref, bf16[2560,1536]{1,0:T(8,128)(2,1)} %get-tuple-element.109.q_ref.k_ref.v_ref, ...), custom_call_target="tpu_custom_call" | custom-call | flops 1500000000 | bytes 419430 | tf_op jit(solution)/shard_map/attend/pallas_call | solution.py:608
  245.9 28.7 %mix.1 = bf16[2048,2048]{1,0:T(8,128)(2,1)} custom-call(bf16[2048,512]{1,0:T(8,128)(2,1)} %get-tuple-element.110.att_ref.o_ref, bf16[2560,2048]{1,0:T(8,128)(2,1)} %get-tuple-element.111.act_ref, bf16[8,512,256]{2,1,0:T(8,128)(2,1)} %bitcast.92, bf16[8,2048,256]{2,1,0:T(8,128)(2,1)} %bitcast.89), custom_call_target="tpu_custom_call" | custom-call | flops 1073741824 | bytes 838860 | tf_op jit(solution)/shard_map/mix/pallas_call | solution.py:784
  276.3 28.9 %backward_early.1 = (bf16[2560,2048]{1,0:T(8,128)(2,1)}, bf16[2560,512]{1,0:T(8,128)(2,1)}, bf16[2560,2048]{1,0:T(8,128)(2,1)}) custom-call(s32[17]{0:T(128)} %pad_add_fusion.5.where_ref, bf16[512,2048]{1,0:T(8,128)(2,1)} %cot_ref, bf16[512,2048]{1,0:T(8,128)(2,1)} %copy-done.10, bf16[512,2048]{1,0:T(8,128)(2,1)} %collective-permute-done.7.refs_2_, ...), custom_call_target="tpu_custom_call" | custom-call | flops 1073741824 | bytes 524288 | tf_op jit(solution)/shard_map/backward_early/pallas_call | solution.py:510
  305.2 12.6 %collective-permute-done.11.refs_0_.refs_1_ = bf16[512,2048]{1,0:T(8,128)(2,1)S(1)} collective-permute-done((bf16[512,2048]{1,0:T(8,128)(2,1)}, bf16[512,2048]{1,0:T(8,128)(2,1)S(1)}, u32[]{:S(2)}, u32[]{:S(2)}) %collective-permute-start.11) | collective-permute-done | bytes 2097184 | tf_op jit(solution)/shard_map/ppermute | solution.py:1171
  319.2 14.5 %backward_chunk.1 = (bf16[2560,2048]{1,0:T(8,128)(2,1)}, bf16[2560,512]{1,0:T(8,128)(2,1)}, bf16[2560,2048]{1,0:T(8,128)(2,1)}) custom-call(s32[6]{0:T(128)} %stack.186.where_ref, bf16[512,2048]{1,0:T(8,128)(2,1)} %copy-done.1, bf16[512,2048]{1,0:T(8,128)(2,1)} %copy-done.1, ...), custom_call_target="tpu_custom_call", output_to_operand_aliasing={{0}: (6, {}), {1}: (7, {}), {2}: (8, {})} | custom-call | flops 268435456 | bytes 524288 | tf_op jit(solution)/shard_map/backward_chunk/pallas_call | solution.py:870
  333.7 18.0 %columns_send.1 = bf16[4,2560,256]{2,1,0:T(8,128)(2,1)} custom-call(s32[4]{0:T(128)} %broadcast_xor_fusion.1.where_ref, bf16[2048,512]{1,0:T(8,128)(2,1)} %get-tuple-element.110.att_ref.o_ref, bf16[2560,2048]{1,0:T(8,128)(2,1)} %get-tuple-element.111.act_ref, bf16[2560,2048]{1,0:T(8,128)(2,1)} %get-tuple-element.136.c_ref), custom_call_target="tpu_custom_call" | custom-call | flops 536870912 | bytes 524288 | tf_op jit(solution)/shard_map/columns_send/pallas_call | solution.py:1009
  351.7 16.2 %rows_send.2 = (bf16[4,256,2048]{2,1,0:T(8,128)(2,1)}, f32[8,2048]{1,0:T(8,128)}) custom-call(s32[4]{0:T(128)} %broadcast_xor_fusion.1.where_ref, bf16[2560,2048]{1,0:T(8,128)(2,1)} %get-tuple-element.147.x_ref, bf16[2560,2048]{1,0:T(8,128)(2,1)} %get-tuple-element.142.refs_0_.gh_ref), custom_call_target="tpu_custom_call" | custom-call | flops 429496736 | bytes 419430 | tf_op jit(solution)/shard_map/rows_send/pallas_call | solution.py:1047
  368.4 60.5 %attend_back.1 = (bf16[2048,512]{1,0:T(8,128)(2,1)}, bf16[2048,512]{1,0:T(8,128)(2,1)}, bf16[2048,512]{1,0:T(8,128)(2,1)}) custom-call(s32[8]{0:T(128)} %and_select_fusion.2.first_ref, bf16[2560,1536]{1,0:T(8,128)(2,1)} %get-tuple-element.109.q_ref.k_ref.v_ref, bf16[2560,1536]{1,0:T(8,128)(2,1)} %get-tuple-element.109.q_ref.k_ref.v_ref, ...), custom_call_target="tpu_custom_call" | custom-call | flops 2200000000 | bytes 1048576 | tf_op jit(solution)/shard_map/attend_back/pallas_call | solution.py:735
  429.0 39.2 %grad_normed.1 = bf16[2048,2048]{1,0:T(8,128)(2,1)} custom-call(bf16[2048,512]{1,0:T(8,128)(2,1)} %get-tuple-element.138.gq_ref.refs_0_, bf16[2048,512]{1,0:T(8,128)(2,1)} %get-tuple-element.139.gk_ref.refs_1_, bf16[2048,512]{1,0:T(8,128)(2,1)} %get-tuple-element.140.gv_ref.refs_2_, bf16[2560,2048]{1,0:T(8,128)(2,1)} %get-tuple-element.142.refs_0_.gh_ref, ...), custom_call_target="tpu_custom_call" | custom-call | flops 1503238528 | bytes 838860 | tf_op jit(solution)/shard_map/grad_normed/pallas_call | solution.py:903
  468.2 19.8 %columns_keep.1 = (bf16[4,1280,256]{2,1,0:T(8,128)(2,1)}, bf16[4,1280,256]{2,1,0:T(8,128)(2,1)}) custom-call(s32[16]{0:T(128)} %pad_add_fusion.6.where_ref, bf16[2048,512]{1,0:T(8,128)(2,1)} %get-tuple-element.110.att_ref.o_ref, bf16[2560,2048]{1,0:T(8,128)(2,1)} %get-tuple-element.111.act_ref, bf16[2560,2048]{1,0:T(8,128)(2,1)} %get-tuple-element.136.c_ref, ...), custom_call_target="tpu_custom_call" | custom-call | flops 536870912 | bytes 524288 | tf_op jit(solution)/shard_map/columns_keep/pallas_call | solution.py:1023
  488.0 14.8 %rows_send.3 = (bf16[4,256,1536]{2,1,0:T(8,128)(2,1)}, f32[8,1536]{1,0:T(8,128)}) custom-call(s32[4]{0:T(128)} %broadcast_xor_fusion.1.where_ref, bf16[2560,2048]{1,0:T(8,128)(2,1)} %get-tuple-element.147.x_ref, bf16[2048,512]{1,0:T(8,128)(2,1)} %get-tuple-element.138.gq_ref.refs_0_, bf16[2048,512]{1,0:T(8,128)(2,1)} %get-tuple-element.139.gk_ref.refs_1_, ...), custom_call_target="tpu_custom_call" | custom-call | flops 322122560 | bytes 314572 | tf_op jit(solution)/shard_map/rows_send/pallas_call | solution.py:1047
  508.8 17.2 %rows_keep.2 = (bf16[4,256,1024]{2,1,0:T(8,128)(2,1)}, bf16[4,256,1024]{2,1,0:T(8,128)(2,1)}) custom-call(s32[16]{0:T(128)} %pad_add_fusion.6.where_ref, bf16[2560,2048]{1,0:T(8,128)(2,1)} %get-tuple-element.147.x_ref, bf16[2560,2048]{1,0:T(8,128)(2,1)} %get-tuple-element.142.refs_0_.gh_ref, bf16[4,256,2048]{2,1,0:T(8,128)(2,1)} %collective-permute-done.13.refs_1_), custom_call_target="tpu_custom_call" | custom-call | flops 429496736 | bytes 419430 | tf_op jit(solution)/shard_map/rows_keep/pallas_call | solution.py:1067
  532.7 3.4 collective-permute-done.14
  544.4 15.6 %rows_keep.3 = (bf16[4,256,768]{2,1,0:T(8,128)(2,1)}, bf16[4,256,768]{2,1,0:T(8,128)(2,1)}) custom-call(s32[16]{0:T(128)} %pad_add_fusion.6.where_ref, bf16[2560,2048]{1,0:T(8,128)(2,1)} %get-tuple-element.147.x_ref, bf16[2048,512]{1,0:T(8,128)(2,1)} %get-tuple-element.138.gq_ref.refs_0_, bf16[2048,512]{1,0:T(8,128)(2,1)} %get-tuple-element.139.gk_ref.refs_1_, ...), custom_call_target="tpu_custom_call" | custom-call | flops 322122560 | bytes 314572 | tf_op jit(solution)/shard_map/rows_keep/pallas_call | solution.py:1067
  580.4 3.6 mixed_out.1
  584.0 7.1 %collective-permute-done.18 = bf16[2,256,768]{2,1,0:T(8,128)(2,1)} collective-permute-done((bf16[2,256,768]{2,1,0:T(8,128)(2,1)}, bf16[2,256,768]{2,1,0:T(8,128)(2,1)}, u32[]{:S(2)}, u32[]{:S(2)}) %collective-permute-start.18) | collective-permute-done | bytes 786464 | tf_op jit(solution)/shard_map/ppermute | solution.py:1091
  596.5 4.2 collective-permute-done.25
  605.0 3.5 collective-permute-done.20
  613.5 6.9 %norm_back.1 = (bf16[512,2048]{1,0:T(8,128)(2,1)}, f32[8,2048]{1,0:T(8,128)}) custom-call(bf16[512,2048]{1,0:T(8,128)(2,1)} %x_ref.5, bf16[512,2048]{1,0:T(8,128)(2,1)} %cot_ref, bf16[512,2048]{1,0:T(8,128)(2,1)} %reduce-scatter.5.cloned.1.call-done.refs_0_, f32[1,2048]{1,0:T(1,128)} %bitcast.104), custom_call_target="tpu_custom_call" | custom-call | flops 1048576 | bytes 629145 | tf_op jit(solution)/shard_map/norm_back/pallas_call | solution.py:127
  621.9 18.4 %small_sums.1 = f32[80,128]{1,0:T(8,128)} custom-call(f32[80,128]{1,0:T(8,128)} %select_maximum_fusion.x_ref), custom_call_target="tpu_custom_call" | custom-call | tf_op jit(solution)/shard_map/small_sums/pallas_call | solution.py:1143
  (206 shorter events, 104.6 us)
Async XLA Ops:
  7.2 77.3 %all-gather.7.cloned.1.call-start = ((), (), s32[]{:S(2)}) async-start(), calls=%async_computation.2 | async-start | bytes 7077888 | tf_op jit(solution)/shard_map/all_gather | solution.py:1228
  9.8 130.1 %all-gather.9.cloned.1.call-start = ((), (), s32[]{:S(2)}) async-start(), calls=%async_computation.3 | async-start | bytes 9437184 | tf_op jit(solution)/shard_map/all_gather | solution.py:1229
  10.6 235.3 %all-gather.11.cloned.1.call-start = ((), (), s32[]{:S(2)}) async-start(), calls=%async_computation.6 | async-start | bytes 2359296 | tf_op jit(solution)/shard_map/all_gather | solution.py:1230
  11.3 234.6 %all-gather.13.cloned.1.call-start = ((), (), s32[]{:S(2)}) async-start(), calls=%async_computation.7 | async-start | bytes 9437184 | tf_op jit(solution)/shard_map/all_gather | solution.py:1231
  11.9 456.3 %reduce-scatter.3.cloned.1.call-start = ((), (), s32[]{:S(2)}) async-start(), calls=%async_computation.4 | async-start | bytes 10485760 | tf_op jit(solution)/shard_map/reduce_scatter | solution.py:1248
  15.7 50.1 %collective-permute-start = (bf16[512,2048]{1,0:T(8,128)(2,1)}, bf16[512,2048]{1,0:T(8,128)(2,1)S(1)}, u32[]{:S(2)}, u32[]{:S(2)}) collective-permute-start(bf16[512,2048]{1,0:T(8,128)(2,1)} %norm.1.refs_0_), channel_id=1, source_target_pairs={{0,1},{1,2},{2,3},{4,5},{5,6},{6,7},{8,9},{9,10},{10,11},{12,13},{... | collective-permute-start | bytes 6291464 | tf_op jit(solution)/shard_map/ppermute | solution.py:1171
  20.8 49.3 %collective-permute-start.2 = (bf16[512,2048]{1,0:T(8,128)(2,1)}, bf16[512,2048]{1,0:T(8,128)(2,1)}, u32[]{:S(2)}, u32[]{:S(2)}) collective-permute-start(bf16[512,2048]{1,0:T(8,128)(2,1)} %norm.1.refs_0_), channel_id=1, source_target_pairs={{1,0},{2,1},{3,2},{5,4},{6,5},{7,6},{9,8},{10,9},{11,10},{13,12},{... | collective-permute-start | bytes 6291464 | tf_op jit(solution)/shard_map/ppermute | solution.py:1171
  65.8 35.8 %collective-permute-start.1 = (bf16[512,2048]{1,0:T(8,128)(2,1)S(1)}, bf16[512,2048]{1,0:T(8,128)(2,1)}, u32[]{:S(2)}, u32[]{:S(2)}) collective-permute-start(bf16[512,2048]{1,0:T(8,128)(2,1)S(1)} %collective-permute-done.refs_1_), channel_id=1, source_target_pairs={{1,2},{2,3},{5,6},{6,7},{9,10},{10,11},{13,14},{14,15},{17,18},{18... | collective-permute-start | bytes 6291464 | tf_op jit(solution)/shard_map/ppermute | solution.py:1171
  70.1 49.8 %collective-permute-start.3 = (bf16[512,2048]{1,0:T(8,128)(2,1)}, bf16[512,2048]{1,0:T(8,128)(2,1)}, u32[]{:S(2)}, u32[]{:S(2)}) collective-permute-start(bf16[512,2048]{1,0:T(8,128)(2,1)} %collective-permute-done.2.refs_2_), channel_id=1, source_target_pairs={{1,0},{2,1},{5,4},{6,5},{9,8},{10,9},{13,12},{14,13},{17,16},{18,1... | collective-permute-start | bytes 6291464 | tf_op jit(solution)/shard_map/ppermute | solution.py:1171
  119.8 48.8 %collective-permute-start.6 = (bf16[512,2048]{1,0:T(8,128)(2,1)}, bf16[512,2048]{1,0:T(8,128)(2,1)S(1)}, u32[]{:S(2)}, u32[]{:S(2)}) collective-permute-start(bf16[512,2048]{1,0:T(8,128)(2,1)} %cot_ref), channel_id=1, source_target_pairs={{0,1},{3,2},{4,5},{7,6},{8,9},{11,10},{12,13},{15,14},{16,17},{19,... | collective-permute-start | bytes 6291464 | tf_op jit(solution)/shard_map/ppermute | solution.py:1171
  123.6 45.1 %collective-permute-start.7 = (bf16[512,2048]{1,0:T(8,128)(2,1)}, bf16[512,2048]{1,0:T(8,128)(2,1)}, u32[]{:S(2)}, u32[]{:S(2)}) collective-permute-start(bf16[512,2048]{1,0:T(8,128)(2,1)} %cot_ref), channel_id=1, source_target_pairs={{1,2},{2,1},{5,6},{6,5},{9,10},{10,9},{13,14},{14,13},{17,18},{18,... | collective-permute-start | bytes 6291464 | tf_op jit(solution)/shard_map/ppermute | solution.py:1171
  125.6 43.1 %collective-permute-start.4 = (bf16[512,2048]{1,0:T(8,128)(2,1)}, bf16[512,2048]{1,0:T(8,128)(2,1)}, u32[]{:S(2)}, u32[]{:S(2)}) collective-permute-start(bf16[512,2048]{1,0:T(8,128)(2,1)} %collective-permute-done.1.refs_0_.refs_3_), channel_id=1, source_target_pairs={{2,3},{6,7},{10,11},{14,15},{18,19},{22,23},{26,27},{30,31}} | collective-permute-start | bytes 6291464 | tf_op jit(solution)/shard_map/ppermute | solution.py:1171
  127.6 47.3 %collective-permute-start.5 = (bf16[512,2048]{1,0:T(8,128)(2,1)}, bf16[512,2048]{1,0:T(8,128)(2,1)}, u32[]{:S(2)}, u32[]{:S(2)}) collective-permute-start(bf16[512,2048]{1,0:T(8,128)(2,1)} %collective-permute-done.3.refs_1_.refs_4_), channel_id=1, source_target_pairs={{1,0},{5,4},{9,8},{13,12},{17,16},{21,20},{25,24},{29,28}} | collective-permute-start | bytes 6291464 | tf_op jit(solution)/shard_map/ppermute | solution.py:1171
  174.9 69.6 %collective-permute-start.10 = (bf16[512,2048]{1,0:T(8,128)(2,1)S(1)}, bf16[512,2048]{1,0:T(8,128)(2,1)}, u32[]{:S(2)}, u32[]{:S(2)}) collective-permute-start(bf16[512,2048]{1,0:T(8,128)(2,1)S(1)} %collective-permute-done.6.refs_1_), channel_id=1, source_target_pairs={{1,2},{2,1},{5,6},{6,5},{9,10},{10,9},{13,14},{14,13},{17,18},{18,... | collective-permute-start | bytes 6291464 | tf_op jit(solution)/shard_map/ppermute | solution.py:1171
  178.2 96.3 %collective-permute-start.8 = (bf16[512,2048]{1,0:T(8,128)(2,1)}, bf16[512,2048]{1,0:T(8,128)(2,1)}, u32[]{:S(2)}, u32[]{:S(2)}) collective-permute-start(bf16[512,2048]{1,0:T(8,128)(2,1)} %cot_ref), channel_id=1, source_target_pairs={{2,3},{1,0},{6,7},{5,4},{10,11},{9,8},{14,15},{13,12},{18,19},{17,... | collective-permute-start | bytes 6291464 | tf_op jit(solution)/shard_map/ppermute | solution.py:1171
  179.5 96.7 %collective-permute-start.9 = (bf16[512,2048]{1,0:T(8,128)(2,1)}, bf16[512,2048]{1,0:T(8,128)(2,1)}, u32[]{:S(2)}, u32[]{:S(2)}) collective-permute-start(bf16[512,2048]{1,0:T(8,128)(2,1)} %collective-permute-done.7.refs_2_), channel_id=1, source_target_pairs={{2,3},{1,0},{6,7},{5,4},{10,11},{9,8},{14,15},{13,12},{18,19},{17,... | collective-permute-start | bytes 6291464 | tf_op jit(solution)/shard_map/ppermute | solution.py:1171
  244.6 73.2 %collective-permute-start.11 = (bf16[512,2048]{1,0:T(8,128)(2,1)}, bf16[512,2048]{1,0:T(8,128)(2,1)S(1)}, u32[]{:S(2)}, u32[]{:S(2)}) collective-permute-start(bf16[512,2048]{1,0:T(8,128)(2,1)} %collective-permute-done.10.refs_5_), channel_id=1, source_target_pairs={{2,3},{1,0},{6,7},{5,4},{10,11},{9,8},{14,15},{13,12},{18,19},{17,... | collective-permute-start | bytes 6291464 | tf_op jit(solution)/shard_map/ppermute | solution.py:1171
  319.1 294.4 %reduce-scatter.5.cloned.1.call-start = ((), (), s32[]{:S(2)}) async-start(), calls=%async_computation.5 | async-start | bytes 10485760 | tf_op jit(solution)/shard_map/reduce_scatter | solution.py:1248
  351.7 77.2 %collective-permute-start.12 = (bf16[4,2560,256]{2,1,0:T(8,128)(2,1)}, bf16[4,2560,256]{2,1,0:T(8,128)(2,1)}, u32[]{:S(2)}, u32[]{:S(2)}) collective-permute-start(bf16[4,2560,256]{2,1,0:T(8,128)(2,1)} %columns_send.1), channel_id=1, source_target_pairs={{0,4},{4,0},{8,12},{12,8},{16,20},{20,16},{24,28},{28,24},{1,5},{5... | collective-permute-start | bytes 15728648 | tf_op jit(solution)/shard_map/ppermute | solution.py:1091
  367.9 61.0 %collective-permute-start.13 = (bf16[4,256,2048]{2,1,0:T(8,128)(2,1)}, bf16[4,256,2048]{2,1,0:T(8,128)(2,1)}, u32[]{:S(2)}, u32[]{:S(2)}) collective-permute-start(bf16[4,256,2048]{2,1,0:T(8,128)(2,1)} %get-tuple-element.134), channel_id=1, source_target_pairs={{0,4},{4,0},{8,12},{12,8},{16,20},{20,16},{24,28},{28,24},{1,5},{5... | collective-permute-start | bytes 12582920 | tf_op jit(solution)/shard_map/ppermute | solution.py:1091
  502.8 41.6 %collective-permute-start.16 = (bf16[4,256,1536]{2,1,0:T(8,128)(2,1)}, bf16[4,256,1536]{2,1,0:T(8,128)(2,1)}, u32[]{:S(2)}, u32[]{:S(2)}) collective-permute-start(bf16[4,256,1536]{2,1,0:T(8,128)(2,1)} %get-tuple-element.148), channel_id=1, source_target_pairs={{0,4},{4,0},{8,12},{12,8},{16,20},{20,16},{24,28},{28,24},{1,5},{5... | collective-permute-start | bytes 9437192 | tf_op jit(solution)/shard_map/ppermute | solution.py:1091
  504.1 31.9 %collective-permute-start.14 = (bf16[2,1280,256]{2,1,0:T(8,128)(2,1)}, bf16[2,1280,256]{2,1,0:T(8,128)(2,1)}, u32[]{:S(2)}, u32[]{:S(2)}) collective-permute-start(bf16[2,1280,256]{2,1,0:T(8,128)(2,1)} %slice.190), channel_id=1, source_target_pairs={{0,8},{4,12},{8,0},{12,4},{16,24},{20,28},{24,16},{28,20},{1,9},{5... | collective-permute-start | bytes 3932168 | tf_op jit(solution)/shard_map/ppermute | solution.py:1091
  505.9 34.5 %collective-permute-start.15 = (bf16[2,1280,256]{2,1,0:T(8,128)(2,1)S(1)}, bf16[2,1280,256]{2,1,0:T(8,128)(2,1)}, u32[]{:S(2)}, u32[]{:S(2)}) collective-permute-start(bf16[2,1280,256]{2,1,0:T(8,128)(2,1)S(1)} %slice.192), channel_id=1, source_target_pairs={{0,16},{4,20},{8,24},{12,28},{16,0},{20,4},{24,8},{28,12},{1,17},{... | collective-permute-start | bytes 3932168 | tf_op jit(solution)/shard_map/ppermute | solution.py:1091
  530.8 33.4 %collective-permute-start.24 = (bf16[2,256,1024]{2,1,0:T(8,128)(2,1)}, bf16[2,256,1024]{2,1,0:T(8,128)(2,1)}, u32[]{:S(2)}, u32[]{:S(2)}) collective-permute-start(bf16[2,256,1024]{2,1,0:T(8,128)(2,1)} %slice.215), channel_id=1, source_target_pairs={{0,16},{4,20},{8,24},{12,28},{16,0},{20,4},{24,8},{28,12},{1,17},{... | collective-permute-start | bytes 3145736 | tf_op jit(solution)/shard_map/ppermute | solution.py:1091
  531.3 36.0 %collective-permute-start.22 = (bf16[2,256,1024]{2,1,0:T(8,128)(2,1)}, bf16[2,256,1024]{2,1,0:T(8,128)(2,1)}, u32[]{:S(2)}, u32[]{:S(2)}) collective-permute-start(bf16[2,256,1024]{2,1,0:T(8,128)(2,1)} %slice.211), channel_id=1, source_target_pairs={{0,8},{4,12},{8,0},{12,4},{16,24},{20,28},{24,16},{28,20},{1,9},{5... | collective-permute-start | bytes 3145736 | tf_op jit(solution)/shard_map/ppermute | solution.py:1091
  538.7 35.5 %collective-permute-start.21 = (bf16[1,1280,256]{2,1,0:T(8,128)(2,1)}, bf16[1,1280,256]{2,1,0:T(8,128)(2,1)}, u32[]{:S(2)}, u32[]{:S(2)}) collective-permute-start(bf16[1,1280,256]{2,1,0:T(8,128)(2,1)} %slice.230), channel_id=1, source_target_pairs={{0,16},{4,20},{8,24},{12,28},{16,0},{20,4},{24,8},{28,12},{1,17},{... | collective-permute-start | bytes 1966088 | tf_op jit(solution)/shard_map/ppermute | solution.py:1091
  543.0 33.9 %collective-permute-start.26 = (bf16[1,1280,256]{2,1,0:T(8,128)(2,1)}, bf16[1,1280,256]{2,1,0:T(8,128)(2,1)}, u32[]{:S(2)}, u32[]{:S(2)}) collective-permute-start(bf16[1,1280,256]{2,1,0:T(8,128)(2,1)} %slice.234), channel_id=1, source_target_pairs={{0,8},{4,12},{8,0},{12,4},{16,24},{20,28},{24,16},{28,20},{1,9},{5... | collective-permute-start | bytes 1966088 | tf_op jit(solution)/shard_map/ppermute | solution.py:1091
  561.4 31.1 %collective-permute-start.17 = (bf16[2,256,768]{2,1,0:T(8,128)(2,1)S(1)}, bf16[2,256,768]{2,1,0:T(8,128)(2,1)}, u32[]{:S(2)}, u32[]{:S(2)}) collective-permute-start(bf16[2,256,768]{2,1,0:T(8,128)(2,1)S(1)} %slice.194), channel_id=1, source_target_pairs={{0,8},{4,12},{8,0},{12,4},{16,24},{20,28},{24,16},{28,20},{1,9},{5... | collective-permute-start | bytes 2359304 | tf_op jit(solution)/shard_map/ppermute | solution.py:1091
  564.2 26.8 %collective-permute-start.18 = (bf16[2,256,768]{2,1,0:T(8,128)(2,1)}, bf16[2,256,768]{2,1,0:T(8,128)(2,1)}, u32[]{:S(2)}, u32[]{:S(2)}) collective-permute-start(bf16[2,256,768]{2,1,0:T(8,128)(2,1)} %slice.196), channel_id=1, source_target_pairs={{0,16},{4,20},{8,24},{12,28},{16,0},{20,4},{24,8},{28,12},{1,17},{... | collective-permute-start | bytes 2359304 | tf_op jit(solution)/shard_map/ppermute | solution.py:1091
  567.3 33.3 %collective-permute-start.25 = (bf16[1,256,1024]{2,1,0:T(8,128)(2,1)}, bf16[1,256,1024]{2,1,0:T(8,128)(2,1)}, u32[]{:S(2)}, u32[]{:S(2)}) collective-permute-start(bf16[1,256,1024]{2,1,0:T(8,128)(2,1)} %slice.233), channel_id=1, source_target_pairs={{0,8},{4,12},{8,0},{12,4},{16,24},{20,28},{24,16},{28,20},{1,9},{5... | collective-permute-start | bytes 1572872 | tf_op jit(solution)/shard_map/ppermute | solution.py:1091
  574.2 28.1 %collective-permute-start.23 = (bf16[1,256,1024]{2,1,0:T(8,128)(2,1)}, bf16[1,256,1024]{2,1,0:T(8,128)(2,1)}, u32[]{:S(2)}, u32[]{:S(2)}) collective-permute-start(bf16[1,256,1024]{2,1,0:T(8,128)(2,1)} %slice.232), channel_id=1, source_target_pairs={{0,16},{4,20},{8,24},{12,28},{16,0},{20,4},{24,8},{28,12},{1,17},{... | collective-permute-start | bytes 1572872 | tf_op jit(solution)/shard_map/ppermute | solution.py:1091
  594.3 15.2 %collective-permute-start.19 = (bf16[1,256,768]{2,1,0:T(8,128)(2,1)S(1)}, bf16[1,256,768]{2,1,0:T(8,128)(2,1)S(1)}, u32[]{:S(2)}, u32[]{:S(2)}) collective-permute-start(bf16[1,256,768]{2,1,0:T(8,128)(2,1)S(1)} %slice.227), channel_id=1, source_target_pairs={{0,16},{4,20},{8,24},{12,28},{16,0},{20,4},{24,8},{28,12},{1,17},{... | collective-permute-start | bytes 1179656 | tf_op jit(solution)/shard_map/ppermute | solution.py:1091
  (24 other events, 328.7 us)
Sparse Core Ops, SparseCore 0:
  10.5 48.2 all-gather.6
  60.6 54.3 all-gather.8
  116.9 27.9 all-gather.10
  146.6 54.3 all-gather.12
  317.9 144.8 reduce-scatter.2
  468.3 145.1 reduce-scatter.4

commit v6 on v5

--- a/solution.py
+++ b/solution.py
@@ -122,7 +122,7 @@
 
 def norm_back(x, cot, grads, gain):
     rows, width = x.shape
-    step = min(128, rows)
+    step = min(256, rows)
     tile = pl.BlockSpec((step, width), lambda i: (i, 0))
     return pl.pallas_call(
         norm_back_kernel,

time: 662 us -> 663 us (level)
  no operation moved by 1% of the time
where the time goes in v6:
time: 663 us; the launch traced here: 652 us
  Pallas kernels  427 us (64%)
  waiting for transfers between devices  94.1 us (14%)
  starting transfers between devices  42 us (6%)
  other arithmetic  35.9 us (5%)
  local copies, waits for them, and re-layouts  35 us (5%)
  between operations  18.3 us (3%)
    ppermute x12, waiting for transfers between devices, shift(): return lax.ppermute(x, 'tensor', pairs)  69.7 us
    pallas_call x1, Pallas kernels, attend_back(): pl.pallas_call(attend_back_kernel, grid_spec=pltpu.PrefetchScalarGridSpec...  60.5 us
    pallas_call x1, Pallas kernels, attend(): pl.pallas_call(functools.partial(attend_kernel, skipped), grid_spec=pltpu...  42 us
    pallas_call x1, Pallas kernels, grad_normed(): pl.pallas_call(grad_kernel, grid=((stop - start) // tile,), in_specs=[onc...  39.2 us
    pallas_call x2, Pallas kernels, row_grads(): pl.pallas_call(functools.partial(rows_keep_kernel, len(gs)), grid_spec=pl...  32.9 us
    pallas_call x2, Pallas kernels, row_grads(): pl.pallas_call(functools.partial(rows_send_kernel, len(gs)), grid_spec=pl...  31 us
    pallas_call x1, Pallas kernels, backward_early(): pl.pallas_call(functools.partial(backward_early_kernel, len(cots), parts)...  28.9 us
    pallas_call x1, Pallas kernels, units_early(): pl.pallas_call(functools.partial(units_early_kernel, len(xs), parts), gri...  28.7 us
  transfers between devices with their start and end apart: 33, of which 14 were waited for; matrix products, arithmetic and copies ran while one was open for 10% of the time, Pallas kernels for 62%

profile of v6, /device:TPU:0, one launch (start us, length us, event | category | flops | bytes accessed | tf_op | source)
XLA Modules:
  0.0 652.3 jit_solution(15432271372450844536)
XLA Ops:
  12.0 3.7 norm.1.refs_0_
  15.7 5.0 collective-permute-start
  29.2 3.3 stack.199
  37.1 28.8 %collective-permute-done.refs_1_ = bf16[512,2048]{1,0:T(8,128)(2,1)S(1)} collective-permute-done((bf16[512,2048]{1,0:T(8,128)(2,1)}, bf16[512,2048]{1,0:T(8,128)(2,1)S(1)}, u32[]{:S(2)}, u32[]{:S(2)}) %collective-permute-start) | collective-permute-done | bytes 2097184 | tf_op jit(solution)/shard_map/ppermute | solution.py:1171
  78.7 5.8 fusion
  84.5 17.2 %queries_early.1 = (bf16[2560,2048]{1,0:T(8,128)(2,1)}, bf16[2560,1536]{1,0:T(8,128)(2,1)}) custom-call(s32[11]{0:T(128)} %pad_add_fusion.7.where_ref, bf16[512,2048]{1,0:T(8,128)(2,1)} %norm.1.refs_0_, bf16[512,2048]{1,0:T(8,128)(2,1)} %copy-done, bf16[512,2048]{1,0:T(8,128)(2,1)} %collective-permute-done.2.refs_2_, ...), custom_call_target="tpu_custom_call" | custom-call | flops 644245120 | bytes 314572 | tf_op jit(solution)/shard_map/queries_early/pallas_call | solution.py:415
  101.6 18.2 %collective-permute-done.3.refs_1_.refs_4_ = bf16[512,2048]{1,0:T(8,128)(2,1)} collective-permute-done((bf16[512,2048]{1,0:T(8,128)(2,1)}, bf16[512,2048]{1,0:T(8,128)(2,1)}, u32[]{:S(2)}, u32[]{:S(2)}) %collective-permute-start.3) | collective-permute-done | bytes 2097184 | tf_op jit(solution)/shard_map/ppermute | solution.py:1171
  119.8 3.8 collective-permute-start.6
  128.9 11.0 %queries_chunk.1 = (bf16[2560,2048]{1,0:T(8,128)(2,1)}, bf16[2560,1536]{1,0:T(8,128)(2,1)}) custom-call(s32[6]{0:T(128)} %stack.191.where_ref, bf16[512,2048]{1,0:T(8,128)(2,1)} %collective-permute-done.1.refs_0_.refs_3_, bf16[512,2048]{1,0:T(8,128)(2,1)} %collective-permute-done.3.refs_1_.refs_4_, ...), custom_call_target="tpu_custom_call", output_to_operand_aliasing={{0}: (8, {}), {1}: (9, {})} | custom-call | flops 161061280 | bytes 314572 | tf_op jit(solution)/shard_map/queries_chunk/pallas_call | solution.py:265
  139.9 28.7 %units_early.1 = (bf16[2560,2048]{1,0:T(8,128)(2,1)}, bf16[2560,2048]{1,0:T(8,128)(2,1)}) custom-call(s32[15]{0:T(128)} %pad_add_fusion.4.where_ref, bf16[512,2048]{1,0:T(8,128)(2,1)} %norm.1.refs_0_, bf16[512,2048]{1,0:T(8,128)(2,1)} %copy-done, bf16[512,2048]{1,0:T(8,128)(2,1)} %collective-permute-done.2.refs_2_, ...), custom_call_target="tpu_custom_call" | custom-call | flops 858993472 | bytes 419430 | tf_op jit(solution)/shard_map/units_early/pallas_call | solution.py:443
  168.7 6.2 collective-permute-done.5.refs_1_
  181.3 21.3 %forward_chunk.1 = (bf16[2560,2048]{1,0:T(8,128)(2,1)}, bf16[2560,1536]{1,0:T(8,128)(2,1)}, bf16[2560,2048]{1,0:T(8,128)(2,1)}, bf16[2560,2048]{1,0:T(8,128)(2,1)}) custom-call(s32[6]{0:T(128)} %stack.186.where_ref, bf16[512,2048]{1,0:T(8,128)(2,1)} %collective-permute-done.4.refs_0_, ...), custom_call_target="tpu_custom_call", output_to_operand_aliasing={{0}: (10, {}), {1}: (11, {}), {2}: (12, {}), {3}: (13, {})} | custom-call | flops 375809632 | bytes 734003 | tf_op jit(solution)/shard_map/forward_chunk/pallas_call | solution.py:322
  202.6 42.0 %attend.1 = (bf16[2048,512]{1,0:T(8,128)(2,1)}, f32[4,8,2048]{2,1,0:T(8,128)}) custom-call(s32[8]{0:T(128)} %and_select_fusion.2.first_ref, bf16[2560,1536]{1,0:T(8,128)(2,1)} %get-tuple-element.109.q_ref.k_ref.v_ref, bf16[2560,1536]{1,0:T(8,128)(2,1)} %get-tuple-element.109.q_ref.k_ref.v_ref, bf16[2560,1536]{1,0:T(8,128)(2,1)} %get-tuple-element.109.q_ref.k_ref.v_ref, ...), custom_call_target="tpu_custom_call" | custom-call | flops 1500000000 | bytes 419430 | tf_op jit(solution)/shard_map/attend/pallas_call | solution.py:608
  245.9 28.7 %mix.1 = bf16[2048,2048]{1,0:T(8,128)(2,1)} custom-call(bf16[2048,512]{1,0:T(8,128)(2,1)} %get-tuple-element.110.att_ref.o_ref, bf16[2560,2048]{1,0:T(8,128)(2,1)} %get-tuple-element.111.act_ref, bf16[8,512,256]{2,1,0:T(8,128)(2,1)} %bitcast.92, bf16[8,2048,256]{2,1,0:T(8,128)(2,1)} %bitcast.89), custom_call_target="tpu_custom_call" | custom-call | flops 1073741824 | bytes 838860 | tf_op jit(solution)/shard_map/mix/pallas_call | solution.py:784
  276.3 28.9 %backward_early.1 = (bf16[2560,2048]{1,0:T(8,128)(2,1)}, bf16[2560,512]{1,0:T(8,128)(2,1)}, bf16[2560,2048]{1,0:T(8,128)(2,1)}) custom-call(s32[17]{0:T(128)} %pad_add_fusion.5.where_ref, bf16[512,2048]{1,0:T(8,128)(2,1)} %cot_ref, bf16[512,2048]{1,0:T(8,128)(2,1)} %copy-done.10, bf16[512,2048]{1,0:T(8,128)(2,1)} %collective-permute-done.7.refs_2_, ...), custom_call_target="tpu_custom_call" | custom-call | flops 1073741824 | bytes 524288 | tf_op jit(solution)/shard_map/backward_early/pallas_call | solution.py:510
  305.2 12.6 %collective-permute-done.11.refs_0_.refs_1_ = bf16[512,2048]{1,0:T(8,128)(2,1)S(1)} collective-permute-done((bf16[512,2048]{1,0:T(8,128)(2,1)}, bf16[512,2048]{1,0:T(8,128)(2,1)S(1)}, u32[]{:S(2)}, u32[]{:S(2)}) %collective-permute-start.11) | collective-permute-done | bytes 2097184 | tf_op jit(solution)/shard_map/ppermute | solution.py:1171
  319.2 14.5 %backward_chunk.1 = (bf16[2560,2048]{1,0:T(8,128)(2,1)}, bf16[2560,512]{1,0:T(8,128)(2,1)}, bf16[2560,2048]{1,0:T(8,128)(2,1)}) custom-call(s32[6]{0:T(128)} %stack.186.where_ref, bf16[512,2048]{1,0:T(8,128)(2,1)} %copy-done.1, bf16[512,2048]{1,0:T(8,128)(2,1)} %copy-done.1, ...), custom_call_target="tpu_custom_call", output_to_operand_aliasing={{0}: (6, {}), {1}: (7, {}), {2}: (8, {})} | custom-call | flops 268435456 | bytes 524288 | tf_op jit(solution)/shard_map/backward_chunk/pallas_call | solution.py:870
  333.7 18.0 %columns_send.1 = bf16[4,2560,256]{2,1,0:T(8,128)(2,1)} custom-call(s32[4]{0:T(128)} %broadcast_xor_fusion.1.where_ref, bf16[2048,512]{1,0:T(8,128)(2,1)} %get-tuple-element.110.att_ref.o_ref, bf16[2560,2048]{1,0:T(8,128)(2,1)} %get-tuple-element.111.act_ref, bf16[2560,2048]{1,0:T(8,128)(2,1)} %get-tuple-element.136.c_ref), custom_call_target="tpu_custom_call" | custom-call | flops 536870912 | bytes 524288 | tf_op jit(solution)/shard_map/columns_send/pallas_call | solution.py:1009
  351.7 16.2 %rows_send.2 = (bf16[4,256,2048]{2,1,0:T(8,128)(2,1)}, f32[8,2048]{1,0:T(8,128)}) custom-call(s32[4]{0:T(128)} %broadcast_xor_fusion.1.where_ref, bf16[2560,2048]{1,0:T(8,128)(2,1)} %get-tuple-element.147.x_ref, bf16[2560,2048]{1,0:T(8,128)(2,1)} %get-tuple-element.142.refs_0_.gh_ref), custom_call_target="tpu_custom_call" | custom-call | flops 429496736 | bytes 419430 | tf_op jit(solution)/shard_map/rows_send/pallas_call | solution.py:1047
  368.4 60.5 %attend_back.1 = (bf16[2048,512]{1,0:T(8,128)(2,1)}, bf16[2048,512]{1,0:T(8,128)(2,1)}, bf16[2048,512]{1,0:T(8,128)(2,1)}) custom-call(s32[8]{0:T(128)} %and_select_fusion.2.first_ref, bf16[2560,1536]{1,0:T(8,128)(2,1)} %get-tuple-element.109.q_ref.k_ref.v_ref, bf16[2560,1536]{1,0:T(8,128)(2,1)} %get-tuple-element.109.q_ref.k_ref.v_ref, ...), custom_call_target="tpu_custom_call" | custom-call | flops 2200000000 | bytes 1048576 | tf_op jit(solution)/shard_map/attend_back/pallas_call | solution.py:735
  429.0 39.2 %grad_normed.1 = bf16[2048,2048]{1,0:T(8,128)(2,1)} custom-call(bf16[2048,512]{1,0:T(8,128)(2,1)} %get-tuple-element.138.gq_ref.refs_0_, bf16[2048,512]{1,0:T(8,128)(2,1)} %get-tuple-element.139.gk_ref.refs_1_, bf16[2048,512]{1,0:T(8,128)(2,1)} %get-tuple-element.140.gv_ref.refs_2_, bf16[2560,2048]{1,0:T(8,128)(2,1)} %get-tuple-element.142.refs_0_.gh_ref, ...), custom_call_target="tpu_custom_call" | custom-call | flops 1503238528 | bytes 838860 | tf_op jit(solution)/shard_map/grad_normed/pallas_call | solution.py:903
  468.2 20.1 %columns_keep.1 = (bf16[4,1280,256]{2,1,0:T(8,128)(2,1)}, bf16[4,1280,256]{2,1,0:T(8,128)(2,1)}) custom-call(s32[16]{0:T(128)} %pad_add_fusion.6.where_ref, bf16[2048,512]{1,0:T(8,128)(2,1)} %get-tuple-element.110.att_ref.o_ref, bf16[2560,2048]{1,0:T(8,128)(2,1)} %get-tuple-element.111.act_ref, bf16[2560,2048]{1,0:T(8,128)(2,1)} %get-tuple-element.136.c_ref, ...), custom_call_target="tpu_custom_call" | custom-call | flops 536870912 | bytes 524288 | tf_op jit(solution)/shard_map/columns_keep/pallas_call | solution.py:1023
  488.3 14.8 %rows_send.3 = (bf16[4,256,1536]{2,1,0:T(8,128)(2,1)}, f32[8,1536]{1,0:T(8,128)}) custom-call(s32[4]{0:T(128)} %broadcast_xor_fusion.1.where_ref, bf16[2560,2048]{1,0:T(8,128)(2,1)} %get-tuple-element.147.x_ref, bf16[2048,512]{1,0:T(8,128)(2,1)} %get-tuple-element.138.gq_ref.refs_0_, bf16[2048,512]{1,0:T(8,128)(2,1)} %get-tuple-element.139.gk_ref.refs_1_, ...), custom_call_target="tpu_custom_call" | custom-call | flops 322122560 | bytes 314572 | tf_op jit(solution)/shard_map/rows_send/pallas_call | solution.py:1047
  510.2 17.2 %rows_keep.2 = (bf16[4,256,1024]{2,1,0:T(8,128)(2,1)}, bf16[4,256,1024]{2,1,0:T(8,128)(2,1)}) custom-call(s32[16]{0:T(128)} %pad_add_fusion.6.where_ref, bf16[2560,2048]{1,0:T(8,128)(2,1)} %get-tuple-element.147.x_ref, bf16[2560,2048]{1,0:T(8,128)(2,1)} %get-tuple-element.142.refs_0_.gh_ref, bf16[4,256,2048]{2,1,0:T(8,128)(2,1)} %collective-permute-done.13.refs_1_), custom_call_target="tpu_custom_call" | custom-call | flops 429496736 | bytes 419430 | tf_op jit(solution)/shard_map/rows_keep/pallas_call | solution.py:1067
  538.9 3.2 collective-permute-start.21
  545.0 15.7 %rows_keep.3 = (bf16[4,256,768]{2,1,0:T(8,128)(2,1)}, bf16[4,256,768]{2,1,0:T(8,128)(2,1)}) custom-call(s32[16]{0:T(128)} %pad_add_fusion.6.where_ref, bf16[2560,2048]{1,0:T(8,128)(2,1)} %get-tuple-element.147.x_ref, bf16[2048,512]{1,0:T(8,128)(2,1)} %get-tuple-element.138.gq_ref.refs_0_, bf16[2048,512]{1,0:T(8,128)(2,1)} %get-tuple-element.139.gk_ref.refs_1_, ...), custom_call_target="tpu_custom_call" | custom-call | flops 322122560 | bytes 314572 | tf_op jit(solution)/shard_map/rows_keep/pallas_call | solution.py:1067
  571.5 3.4 collective-permute-done.21
  581.9 3.6 mixed_out.1
  585.4 6.4 collective-permute-done.18
  597.8 3.1 collective-permute-done.25
  614.6 7.3 %norm_back.1 = (bf16[512,2048]{1,0:T(8,128)(2,1)}, f32[8,2048]{1,0:T(8,128)}) custom-call(bf16[512,2048]{1,0:T(8,128)(2,1)} %x_ref.5, bf16[512,2048]{1,0:T(8,128)(2,1)} %cot_ref, bf16[512,2048]{1,0:T(8,128)(2,1)} %reduce-scatter.5.cloned.1.call-done.refs_0_, f32[1,2048]{1,0:T(1,128)} %bitcast.104), custom_call_target="tpu_custom_call" | custom-call | flops 1048576 | bytes 629145 | tf_op jit(solution)/shard_map/norm_back/pallas_call | solution.py:127
  623.3 18.4 %small_sums.1 = f32[80,128]{1,0:T(8,128)} custom-call(f32[80,128]{1,0:T(8,128)} %select_maximum_fusion.x_ref), custom_call_target="tpu_custom_call" | custom-call | tf_op jit(solution)/shard_map/small_sums/pallas_call | solution.py:1143
  (206 shorter events, 107.2 us)
Async XLA Ops:
  7.2 77.3 %all-gather.7.cloned.1.call-start = ((), (), s32[]{:S(2)}) async-start(), calls=%async_computation.2 | async-start | bytes 7077888 | tf_op jit(solution)/shard_map/all_gather | solution.py:1228
  9.8 130.1 %all-gather.9.cloned.1.call-start = ((), (), s32[]{:S(2)}) async-start(), calls=%async_computation.3 | async-start | bytes 9437184 | tf_op jit(solution)/shard_map/all_gather | solution.py:1229
  10.6 235.3 %all-gather.11.cloned.1.call-start = ((), (), s32[]{:S(2)}) async-start(), calls=%async_computation.6 | async-start | bytes 2359296 | tf_op jit(solution)/shard_map/all_gather | solution.py:1230
  11.3 234.6 %all-gather.13.cloned.1.call-start = ((), (), s32[]{:S(2)}) async-start(), calls=%async_computation.7 | async-start | bytes 9437184 | tf_op jit(solution)/shard_map/all_gather | solution.py:1231
  11.9 456.3 %reduce-scatter.3.cloned.1.call-start = ((), (), s32[]{:S(2)}) async-start(), calls=%async_computation.4 | async-start | bytes 10485760 | tf_op jit(solution)/shard_map/reduce_scatter | solution.py:1248
  15.7 50.1 %collective-permute-start = (bf16[512,2048]{1,0:T(8,128)(2,1)}, bf16[512,2048]{1,0:T(8,128)(2,1)S(1)}, u32[]{:S(2)}, u32[]{:S(2)}) collective-permute-start(bf16[512,2048]{1,0:T(8,128)(2,1)} %norm.1.refs_0_), channel_id=1, source_target_pairs={{0,1},{1,2},{2,3},{4,5},{5,6},{6,7},{8,9},{9,10},{10,11},{12,13},{... | collective-permute-start | bytes 6291464 | tf_op jit(solution)/shard_map/ppermute | solution.py:1171
  20.8 49.3 %collective-permute-start.2 = (bf16[512,2048]{1,0:T(8,128)(2,1)}, bf16[512,2048]{1,0:T(8,128)(2,1)}, u32[]{:S(2)}, u32[]{:S(2)}) collective-permute-start(bf16[512,2048]{1,0:T(8,128)(2,1)} %norm.1.refs_0_), channel_id=1, source_target_pairs={{1,0},{2,1},{3,2},{5,4},{6,5},{7,6},{9,8},{10,9},{11,10},{13,12},{... | collective-permute-start | bytes 6291464 | tf_op jit(solution)/shard_map/ppermute | solution.py:1171
  65.8 35.8 %collective-permute-start.1 = (bf16[512,2048]{1,0:T(8,128)(2,1)S(1)}, bf16[512,2048]{1,0:T(8,128)(2,1)}, u32[]{:S(2)}, u32[]{:S(2)}) collective-permute-start(bf16[512,2048]{1,0:T(8,128)(2,1)S(1)} %collective-permute-done.refs_1_), channel_id=1, source_target_pairs={{1,2},{2,3},{5,6},{6,7},{9,10},{10,11},{13,14},{14,15},{17,18},{18... | collective-permute-start | bytes 6291464 | tf_op jit(solution)/shard_map/ppermute | solution.py:1171
  70.1 49.8 %collective-permute-start.3 = (bf16[512,2048]{1,0:T(8,128)(2,1)}, bf16[512,2048]{1,0:T(8,128)(2,1)}, u32[]{:S(2)}, u32[]{:S(2)}) collective-permute-start(bf16[512,2048]{1,0:T(8,128)(2,1)} %collective-permute-done.2.refs_2_), channel_id=1, source_target_pairs={{1,0},{2,1},{5,4},{6,5},{9,8},{10,9},{13,12},{14,13},{17,16},{18,1... | collective-permute-start | bytes 6291464 | tf_op jit(solution)/shard_map/ppermute | solution.py:1171
  119.8 48.8 %collective-permute-start.6 = (bf16[512,2048]{1,0:T(8,128)(2,1)}, bf16[512,2048]{1,0:T(8,128)(2,1)S(1)}, u32[]{:S(2)}, u32[]{:S(2)}) collective-permute-start(bf16[512,2048]{1,0:T(8,128)(2,1)} %cot_ref), channel_id=1, source_target_pairs={{0,1},{3,2},{4,5},{7,6},{8,9},{11,10},{12,13},{15,14},{16,17},{19,... | collective-permute-start | bytes 6291464 | tf_op jit(solution)/shard_map/ppermute | solution.py:1171
  123.6 45.1 %collective-permute-start.7 = (bf16[512,2048]{1,0:T(8,128)(2,1)}, bf16[512,2048]{1,0:T(8,128)(2,1)}, u32[]{:S(2)}, u32[]{:S(2)}) collective-permute-start(bf16[512,2048]{1,0:T(8,128)(2,1)} %cot_ref), channel_id=1, source_target_pairs={{1,2},{2,1},{5,6},{6,5},{9,10},{10,9},{13,14},{14,13},{17,18},{18,... | collective-permute-start | bytes 6291464 | tf_op jit(solution)/shard_map/ppermute | solution.py:1171
  125.6 43.1 %collective-permute-start.4 = (bf16[512,2048]{1,0:T(8,128)(2,1)}, bf16[512,2048]{1,0:T(8,128)(2,1)}, u32[]{:S(2)}, u32[]{:S(2)}) collective-permute-start(bf16[512,2048]{1,0:T(8,128)(2,1)} %collective-permute-done.1.refs_0_.refs_3_), channel_id=1, source_target_pairs={{2,3},{6,7},{10,11},{14,15},{18,19},{22,23},{26,27},{30,31}} | collective-permute-start | bytes 6291464 | tf_op jit(solution)/shard_map/ppermute | solution.py:1171
  127.6 47.3 %collective-permute-start.5 = (bf16[512,2048]{1,0:T(8,128)(2,1)}, bf16[512,2048]{1,0:T(8,128)(2,1)}, u32[]{:S(2)}, u32[]{:S(2)}) collective-permute-start(bf16[512,2048]{1,0:T(8,128)(2,1)} %collective-permute-done.3.refs_1_.refs_4_), channel_id=1, source_target_pairs={{1,0},{5,4},{9,8},{13,12},{17,16},{21,20},{25,24},{29,28}} | collective-permute-start | bytes 6291464 | tf_op jit(solution)/shard_map/ppermute | solution.py:1171
  174.9 69.6 %collective-permute-start.10 = (bf16[512,2048]{1,0:T(8,128)(2,1)S(1)}, bf16[512,2048]{1,0:T(8,128)(2,1)}, u32[]{:S(2)}, u32[]{:S(2)}) collective-permute-start(bf16[512,2048]{1,0:T(8,128)(2,1)S(1)} %collective-permute-done.6.refs_1_), channel_id=1, source_target_pairs={{1,2},{2,1},{5,6},{6,5},{9,10},{10,9},{13,14},{14,13},{17,18},{18,... | collective-permute-start | bytes 6291464 | tf_op jit(solution)/shard_map/ppermute | solution.py:1171
  178.2 96.3 %collective-permute-start.8 = (bf16[512,2048]{1,0:T(8,128)(2,1)}, bf16[512,2048]{1,0:T(8,128)(2,1)}, u32[]{:S(2)}, u32[]{:S(2)}) collective-permute-start(bf16[512,2048]{1,0:T(8,128)(2,1)} %cot_ref), channel_id=1, source_target_pairs={{2,3},{1,0},{6,7},{5,4},{10,11},{9,8},{14,15},{13,12},{18,19},{17,... | collective-permute-start | bytes 6291464 | tf_op jit(solution)/shard_map/ppermute | solution.py:1171
  179.5 96.7 %collective-permute-start.9 = (bf16[512,2048]{1,0:T(8,128)(2,1)}, bf16[512,2048]{1,0:T(8,128)(2,1)}, u32[]{:S(2)}, u32[]{:S(2)}) collective-permute-start(bf16[512,2048]{1,0:T(8,128)(2,1)} %collective-permute-done.7.refs_2_), channel_id=1, source_target_pairs={{2,3},{1,0},{6,7},{5,4},{10,11},{9,8},{14,15},{13,12},{18,19},{17,... | collective-permute-start | bytes 6291464 | tf_op jit(solution)/shard_map/ppermute | solution.py:1171
  244.6 73.2 %collective-permute-start.11 = (bf16[512,2048]{1,0:T(8,128)(2,1)}, bf16[512,2048]{1,0:T(8,128)(2,1)S(1)}, u32[]{:S(2)}, u32[]{:S(2)}) collective-permute-start(bf16[512,2048]{1,0:T(8,128)(2,1)} %collective-permute-done.10.refs_5_), channel_id=1, source_target_pairs={{2,3},{1,0},{6,7},{5,4},{10,11},{9,8},{14,15},{13,12},{18,19},{17,... | collective-permute-start | bytes 6291464 | tf_op jit(solution)/shard_map/ppermute | solution.py:1171
  319.1 295.5 %reduce-scatter.5.cloned.1.call-start = ((), (), s32[]{:S(2)}) async-start(), calls=%async_computation.5 | async-start | bytes 10485760 | tf_op jit(solution)/shard_map/reduce_scatter | solution.py:1248
  351.7 77.2 %collective-permute-start.12 = (bf16[4,2560,256]{2,1,0:T(8,128)(2,1)}, bf16[4,2560,256]{2,1,0:T(8,128)(2,1)}, u32[]{:S(2)}, u32[]{:S(2)}) collective-permute-start(bf16[4,2560,256]{2,1,0:T(8,128)(2,1)} %columns_send.1), channel_id=1, source_target_pairs={{0,4},{4,0},{8,12},{12,8},{16,20},{20,16},{24,28},{28,24},{1,5},{5... | collective-permute-start | bytes 15728648 | tf_op jit(solution)/shard_map/ppermute | solution.py:1091
  367.9 61.0 %collective-permute-start.13 = (bf16[4,256,2048]{2,1,0:T(8,128)(2,1)}, bf16[4,256,2048]{2,1,0:T(8,128)(2,1)}, u32[]{:S(2)}, u32[]{:S(2)}) collective-permute-start(bf16[4,256,2048]{2,1,0:T(8,128)(2,1)} %get-tuple-element.134), channel_id=1, source_target_pairs={{0,4},{4,0},{8,12},{12,8},{16,20},{20,16},{24,28},{28,24},{1,5},{5... | collective-permute-start | bytes 12582920 | tf_op jit(solution)/shard_map/ppermute | solution.py:1091
  503.1 41.8 %collective-permute-start.16 = (bf16[4,256,1536]{2,1,0:T(8,128)(2,1)}, bf16[4,256,1536]{2,1,0:T(8,128)(2,1)}, u32[]{:S(2)}, u32[]{:S(2)}) collective-permute-start(bf16[4,256,1536]{2,1,0:T(8,128)(2,1)} %get-tuple-element.148), channel_id=1, source_target_pairs={{0,4},{4,0},{8,12},{12,8},{16,20},{20,16},{24,28},{28,24},{1,5},{5... | collective-permute-start | bytes 9437192 | tf_op jit(solution)/shard_map/ppermute | solution.py:1091
  504.4 31.9 %collective-permute-start.14 = (bf16[2,1280,256]{2,1,0:T(8,128)(2,1)}, bf16[2,1280,256]{2,1,0:T(8,128)(2,1)}, u32[]{:S(2)}, u32[]{:S(2)}) collective-permute-start(bf16[2,1280,256]{2,1,0:T(8,128)(2,1)} %slice.190), channel_id=1, source_target_pairs={{0,8},{4,12},{8,0},{12,4},{16,24},{20,28},{24,16},{28,20},{1,9},{5... | collective-permute-start | bytes 3932168 | tf_op jit(solution)/shard_map/ppermute | solution.py:1091
  506.0 36.1 %collective-permute-start.15 = (bf16[2,1280,256]{2,1,0:T(8,128)(2,1)S(1)}, bf16[2,1280,256]{2,1,0:T(8,128)(2,1)}, u32[]{:S(2)}, u32[]{:S(2)}) collective-permute-start(bf16[2,1280,256]{2,1,0:T(8,128)(2,1)S(1)} %slice.192), channel_id=1, source_target_pairs={{0,16},{4,20},{8,24},{12,28},{16,0},{20,4},{24,8},{28,12},{1,17},{... | collective-permute-start | bytes 3932168 | tf_op jit(solution)/shard_map/ppermute | solution.py:1091
  532.1 33.9 %collective-permute-start.24 = (bf16[2,256,1024]{2,1,0:T(8,128)(2,1)}, bf16[2,256,1024]{2,1,0:T(8,128)(2,1)}, u32[]{:S(2)}, u32[]{:S(2)}) collective-permute-start(bf16[2,256,1024]{2,1,0:T(8,128)(2,1)} %slice.215), channel_id=1, source_target_pairs={{0,16},{4,20},{8,24},{12,28},{16,0},{20,4},{24,8},{28,12},{1,17},{... | collective-permute-start | bytes 3145736 | tf_op jit(solution)/shard_map/ppermute | solution.py:1091
  532.1 36.6 %collective-permute-start.22 = (bf16[2,256,1024]{2,1,0:T(8,128)(2,1)}, bf16[2,256,1024]{2,1,0:T(8,128)(2,1)}, u32[]{:S(2)}, u32[]{:S(2)}) collective-permute-start(bf16[2,256,1024]{2,1,0:T(8,128)(2,1)} %slice.211), channel_id=1, source_target_pairs={{0,8},{4,12},{8,0},{12,4},{16,24},{20,28},{24,16},{28,20},{1,9},{5... | collective-permute-start | bytes 3145736 | tf_op jit(solution)/shard_map/ppermute | solution.py:1091
  538.9 36.1 %collective-permute-start.21 = (bf16[1,1280,256]{2,1,0:T(8,128)(2,1)}, bf16[1,1280,256]{2,1,0:T(8,128)(2,1)}, u32[]{:S(2)}, u32[]{:S(2)}) collective-permute-start(bf16[1,1280,256]{2,1,0:T(8,128)(2,1)} %slice.230), channel_id=1, source_target_pairs={{0,16},{4,20},{8,24},{12,28},{16,0},{20,4},{24,8},{28,12},{1,17},{... | collective-permute-start | bytes 1966088 | tf_op jit(solution)/shard_map/ppermute | solution.py:1091
  544.7 33.6 %collective-permute-start.26 = (bf16[1,1280,256]{2,1,0:T(8,128)(2,1)}, bf16[1,1280,256]{2,1,0:T(8,128)(2,1)}, u32[]{:S(2)}, u32[]{:S(2)}) collective-permute-start(bf16[1,1280,256]{2,1,0:T(8,128)(2,1)} %slice.234), channel_id=1, source_target_pairs={{0,8},{4,12},{8,0},{12,4},{16,24},{20,28},{24,16},{28,20},{1,9},{5... | collective-permute-start | bytes 1966088 | tf_op jit(solution)/shard_map/ppermute | solution.py:1091
  562.0 31.2 %collective-permute-start.17 = (bf16[2,256,768]{2,1,0:T(8,128)(2,1)S(1)}, bf16[2,256,768]{2,1,0:T(8,128)(2,1)}, u32[]{:S(2)}, u32[]{:S(2)}) collective-permute-start(bf16[2,256,768]{2,1,0:T(8,128)(2,1)S(1)} %slice.194), channel_id=1, source_target_pairs={{0,8},{4,12},{8,0},{12,4},{16,24},{20,28},{24,16},{28,20},{1,9},{5... | collective-permute-start | bytes 2359304 | tf_op jit(solution)/shard_map/ppermute | solution.py:1091
  566.0 25.9 %collective-permute-start.18 = (bf16[2,256,768]{2,1,0:T(8,128)(2,1)}, bf16[2,256,768]{2,1,0:T(8,128)(2,1)}, u32[]{:S(2)}, u32[]{:S(2)}) collective-permute-start(bf16[2,256,768]{2,1,0:T(8,128)(2,1)} %slice.196), channel_id=1, source_target_pairs={{0,16},{4,20},{8,24},{12,28},{16,0},{20,4},{24,8},{28,12},{1,17},{... | collective-permute-start | bytes 2359304 | tf_op jit(solution)/shard_map/ppermute | solution.py:1091
  568.8 32.1 %collective-permute-start.25 = (bf16[1,256,1024]{2,1,0:T(8,128)(2,1)}, bf16[1,256,1024]{2,1,0:T(8,128)(2,1)}, u32[]{:S(2)}, u32[]{:S(2)}) collective-permute-start(bf16[1,256,1024]{2,1,0:T(8,128)(2,1)} %slice.233), channel_id=1, source_target_pairs={{0,8},{4,12},{8,0},{12,4},{16,24},{20,28},{24,16},{28,20},{1,9},{5... | collective-permute-start | bytes 1572872 | tf_op jit(solution)/shard_map/ppermute | solution.py:1091
  575.0 28.1 %collective-permute-start.23 = (bf16[1,256,1024]{2,1,0:T(8,128)(2,1)}, bf16[1,256,1024]{2,1,0:T(8,128)(2,1)}, u32[]{:S(2)}, u32[]{:S(2)}) collective-permute-start(bf16[1,256,1024]{2,1,0:T(8,128)(2,1)} %slice.232), channel_id=1, source_target_pairs={{0,16},{4,20},{8,24},{12,28},{16,0},{20,4},{24,8},{28,12},{1,17},{... | collective-permute-start | bytes 1572872 | tf_op jit(solution)/shard_map/ppermute | solution.py:1091
  595.7 14.5 %collective-permute-start.19 = (bf16[1,256,768]{2,1,0:T(8,128)(2,1)S(1)}, bf16[1,256,768]{2,1,0:T(8,128)(2,1)S(1)}, u32[]{:S(2)}, u32[]{:S(2)}) collective-permute-start(bf16[1,256,768]{2,1,0:T(8,128)(2,1)S(1)} %slice.227), channel_id=1, source_target_pairs={{0,16},{4,20},{8,24},{12,28},{16,0},{20,4},{24,8},{28,12},{1,17},{... | collective-permute-start | bytes 1179656 | tf_op jit(solution)/shard_map/ppermute | solution.py:1091
  (24 other events, 325.9 us)
Sparse Core Ops, SparseCore 0:
  10.5 48.2 all-gather.6
  60.6 54.3 all-gather.8
  116.9 27.9 all-gather.10
  146.6 54.3 all-gather.12
  317.9 144.8 reduce-scatter.2
  468.3 146.1 reduce-scatter.4
